TPU v7x, 128 devices: a whole 4x4x4 slice. The times are simulated.
128 devices in a mesh: row: 8 (over z, core), col: 16 (over y, x).
Axes of the slice: x: 4, y: 4, z: 4, core: 2. Of those that a mesh axis runs over, the one named last changes fastest.
Arguments:
- tile_values: bfloat16 [8, 16, 512, 128, 128], P('row', 'col'), may hold values from -0.046875 to 0.046875
- tile_rows: int32 [8, 16, 512], P('row', 'col'), may hold values from 0 to 63, as said below
- tile_cols: int32 [8, 16, 512], P('row', 'col'), may hold values from 0 to 31
- tile_count: int32 [8, 16], P('row', 'col'), may hold values from 64 to 512, as said below
- features: bfloat16 [65536, 256], P(('row', 'col')), may hold values from -6 to 6
- weight: bfloat16 [256, 256], replicated, may hold values from -0.375 to 0.375
- cotangent: bfloat16 [65536, 256], P(('row', 'col')), may hold values from -6 to 6
Outputs:
- output: bfloat16 [65536, 256], P(('row', 'col'))
- weight_grad: float32 [256, 256], replicated
- input_grad: float32 [65536, 256], P(('row', 'col'))
Inputs may be any that keep to these rules, and one draw needn't show every extreme that they name: Within a cell, all slots hold distinct positions (tile_rows, tile_cols). `tile_count`: some cell holds exactly 512 tiles in every draw.
All inputs are finite; a program needn't handle non-finite values.
Results may differ from a plain program's by a relative error of at most 0.025.
Values may be sent and summed in bfloat16 or wider, within the bound.
A program may use at most 192 MiB of HBM per device.

v0:
```python
import math

import jax
import jax.numpy as jnp
from jax import lax
from jax.sharding import PartitionSpec as P


def sparse_product(
    tile_block,
    take_index,
    add_index,
    live_count,
    source,
    segments,
    einsum_form,
    loop_count,
    block_size,
):
    tile_edge = tile_block.shape[1]
    feat_width = source.shape[2]
    source_count = source.shape[0]
    source_flat = source.reshape(source_count, tile_edge * feat_width)
    source_ids = lax.iota(jnp.int32, source_count)
    target_ids = lax.iota(jnp.int32, segments)

    def add_block(block_index, running):
        first_slot = block_index * block_size
        tile_part = lax.dynamic_slice_in_dim(tile_block, first_slot, block_size, 0)
        take_part = lax.dynamic_slice_in_dim(take_index, first_slot, block_size, 0)
        add_part = lax.dynamic_slice_in_dim(add_index, first_slot, block_size, 0)
        is_live = first_slot + lax.iota(jnp.int32, block_size) < live_count
        take_table = (take_part[:, None] == source_ids[None, :]).astype(jnp.bfloat16)
        picked = jnp.dot(take_table, source_flat, preferred_element_type=jnp.float32).astype(
            jnp.bfloat16
        )
        picked = picked.reshape(block_size, tile_edge, feat_width)
        products = jnp.einsum(einsum_form, tile_part, picked, preferred_element_type=jnp.float32)
        products = products.reshape(block_size, tile_edge * feat_width)
        upper_part = products.astype(jnp.bfloat16)
        lower_part = (products - upper_part.astype(jnp.float32)).astype(jnp.bfloat16)
        add_table = ((add_part[:, None] == target_ids[None, :]) & is_live[:, None]).astype(
            jnp.bfloat16
        )
        contract = (((0,), (0,)), ((), ()))
        added = lax.dot_general(add_table, upper_part, contract, preferred_element_type=jnp.float32)
        added = added + lax.dot_general(
            add_table, lower_part, contract, preferred_element_type=jnp.float32
        )
        return running + added

    initial = jnp.zeros((segments, tile_edge * feat_width), jnp.float32)
    summed = lax.fori_loop(0, loop_count, add_block, initial)
    return summed.reshape(segments, tile_edge, feat_width)


def activation(aggregated, weight, cot_rows):
    hidden = jnp.dot(aggregated, weight, preferred_element_type=jnp.float32)
    sigmoid_value = jax.nn.sigmoid(hidden)
    output = (hidden * sigmoid_value).astype(jnp.bfloat16)
    silu_slope = sigmoid_value * (1.0 + hidden * (1.0 - sigmoid_value))
    hidden_grad = (cot_rows.astype(jnp.float32) * silu_slope).astype(jnp.bfloat16)
    return (output, hidden_grad)


def per_device(tile_values, tile_rows, tile_cols, tile_count, features, weight, cotangent):
    slot_total = tile_values.shape[2]
    tile_edge = tile_values.shape[3]
    tile_block = tile_values.reshape(slot_total, tile_edge, tile_edge)
    row_index = tile_rows.reshape(slot_total)
    col_index = tile_cols.reshape(slot_total)
    live_count = tile_count.reshape(())
    own_rows = features.shape[0]
    feat_width = features.shape[1]
    row_count = lax.axis_size("row")
    col_count = lax.axis_size("col")
    row_tiles = col_count * own_rows // tile_edge
    col_tiles = row_count * own_rows // tile_edge
    block_size = min(slot_total, 64)
    loop_count = slot_total // block_size
    column_block = lax.all_gather(features, "row", axis=0, tiled=True)
    source = column_block.reshape(col_tiles, tile_edge, feat_width)
    partial_rows = sparse_product(
        tile_block,
        col_index,
        row_index,
        live_count,
        source,
        row_tiles,
        "kab,kbf->kaf",
        loop_count,
        block_size,
    )
    partial_flat = partial_rows.reshape(row_tiles * tile_edge, feat_width)
    node_total = row_count * col_count * own_rows
    aggregated = lax.psum_scatter(
        partial_flat.astype(jnp.bfloat16), "col", scatter_dimension=0, tiled=True
    )
    output, hidden_grad = activation(aggregated, weight, cotangent)
    own_grad = lax.dot_general(
        hidden_grad, weight, (((1,), (1,)), ((), ())), preferred_element_type=jnp.float32
    ).astype(jnp.bfloat16)
    row_block = lax.all_gather(own_grad, "col", axis=0, tiled=True)
    local_grad = lax.dot_general(
        aggregated, hidden_grad, (((0,), (0,)), ((), ())), preferred_element_type=jnp.float32
    )
    weight_grad = lax.psum(local_grad, ("row", "col")) * (1.0 / math.sqrt(node_total))
    source_back = row_block.reshape(row_tiles, tile_edge, feat_width)
    partial_cols = sparse_product(
        tile_block,
        row_index,
        col_index,
        live_count,
        source_back,
        col_tiles,
        "kab,kaf->kbf",
        loop_count,
        block_size,
    )
    input_grad = lax.psum_scatter(
        partial_cols.reshape(col_tiles * tile_edge, feat_width).astype(jnp.bfloat16),
        "row",
        scatter_dimension=0,
        tiled=True,
    ).astype(jnp.float32)
    return (output, weight_grad, input_grad)


def solution(mesh):
    placed = (
        P("row", "col", None, None, None),
        P("row", "col", None),
        P("row", "col", None),
        P("row", "col"),
        P(("row", "col"), None),
        P(),
        P(("row", "col"), None),
    )
    return jax.shard_map(
        per_device,
        mesh=mesh,
        in_specs=placed,
        out_specs=(P(("row", "col"), None), P(), P(("row", "col"), None)),
        check_vma=False,
    )
```

profile of v0, /device:TPU:0, one launch (start us, length us, event | category | flops | bytes accessed | tf_op | source)
XLA Modules:
  0.0 546.3 jit_solution(16715004213160616526)
XLA Ops:
  8.0 29.6 %all-gather.3.cloned.1.call-done = bf16[4096,256]{1,0:T(8,128)(2,1)} async-done(((bf16[512,256]{1,0:T(8,128)(2,1)}), bf16[4096,256]{1,0:T(8,128)(2,1)}) %all-gather.3.cloned.1.call-update) | async-done | bytes 2097168 | tf_op jit(solution)/shard_map/all_gather | solution.py:81
  37.6 2.9 reshape_reshape.8
  40.5 148.5 %while.28 = (s32[]{:T(128)}, f32[64,32768]{1,0:T(8,128)}, s32[512]{0:T(512)S(1)}, s32[]{:T(128)}, bf16[512,128,128]{2,1,0:T(8,128)(2,1)}, /*index=5*/s32[512]{0:...) while((s32[]{:T(128)}, f32[64,32768]{1,0:T(8,128)}, ...), condition=%wide.region_1.0_spmd.clone, body=%wide.region_0.0_spmd.clone.sunk | while | flops 1226852480 | bytes 96471168 | solution.py:53
  43.8 2.9 fusion.73
  46.6 4.7 copy.22
  52.7 4.5 fusion.75
  60.4 2.9 fusion.73
  63.3 4.7 copy.22
  69.4 6.7 %fusion.75 = f32[64,32768]{1,0:T(8,128)} fusion(f32[64,32768]{1,0:T(8,128)S(1)} %fusion.74, f32[64,32768]{1,0:T(8,128)} %get-tuple-element.504, f32[64,32768]{1,0:T(8,128)S(1)} %bitcast.50, pred[]{:T(512)S(6)} %compare.6, s32[64]{0:T(128)S(1)} %dynamic_slice.60, pred[64]{0:T(512)(128)(4,1)S(1)} %add_compare_fusion.4), kind=kOutput, calls=%fused_computation.5.clone.1 | convolution fusion | flops 283123712 | bytes 33554752 | tf_op jit(solution)/shard_map/while/body/eval_jaxpr/dot_general | solution.py:47
  82.1 4.7 copy.22
  88.2 6.7 %fusion.75 = f32[64,32768]{1,0:T(8,128)} fusion(f32[64,32768]{1,0:T(8,128)S(1)} %fusion.74, f32[64,32768]{1,0:T(8,128)} %get-tuple-element.504, f32[64,32768]{1,0:T(8,128)S(1)} %bitcast.50, pred[]{:T(512)S(6)} %compare.6, s32[64]{0:T(128)S(1)} %dynamic_slice.60, pred[64]{0:T(512)(128)(4,1)S(1)} %add_compare_fusion.4), kind=kOutput, calls=%fused_computation.5.clone.1 | convolution fusion | flops 283123712 | bytes 33554752 | tf_op jit(solution)/shard_map/while/body/eval_jaxpr/dot_general | solution.py:47
  100.9 4.7 copy.22
  107.1 6.7 %fusion.75 = f32[64,32768]{1,0:T(8,128)} fusion(f32[64,32768]{1,0:T(8,128)S(1)} %fusion.74, f32[64,32768]{1,0:T(8,128)} %get-tuple-element.504, f32[64,32768]{1,0:T(8,128)S(1)} %bitcast.50, pred[]{:T(512)S(6)} %compare.6, s32[64]{0:T(128)S(1)} %dynamic_slice.60, pred[64]{0:T(512)(128)(4,1)S(1)} %add_compare_fusion.4), kind=kOutput, calls=%fused_computation.5.clone.1 | convolution fusion | flops 283123712 | bytes 33554752 | tf_op jit(solution)/shard_map/while/body/eval_jaxpr/dot_general | solution.py:47
  119.8 4.7 copy.22
  125.9 6.7 %fusion.75 = f32[64,32768]{1,0:T(8,128)} fusion(f32[64,32768]{1,0:T(8,128)S(1)} %fusion.74, f32[64,32768]{1,0:T(8,128)} %get-tuple-element.504, f32[64,32768]{1,0:T(8,128)S(1)} %bitcast.50, pred[]{:T(512)S(6)} %compare.6, s32[64]{0:T(128)S(1)} %dynamic_slice.60, pred[64]{0:T(512)(128)(4,1)S(1)} %add_compare_fusion.4), kind=kOutput, calls=%fused_computation.5.clone.1 | convolution fusion | flops 283123712 | bytes 33554752 | tf_op jit(solution)/shard_map/while/body/eval_jaxpr/dot_general | solution.py:47
  138.6 4.7 copy.22
  144.7 6.7 %fusion.75 = f32[64,32768]{1,0:T(8,128)} fusion(f32[64,32768]{1,0:T(8,128)S(1)} %fusion.74, f32[64,32768]{1,0:T(8,128)} %get-tuple-element.504, f32[64,32768]{1,0:T(8,128)S(1)} %bitcast.50, pred[]{:T(512)S(6)} %compare.6, s32[64]{0:T(128)S(1)} %dynamic_slice.60, pred[64]{0:T(512)(128)(4,1)S(1)} %add_compare_fusion.4), kind=kOutput, calls=%fused_computation.5.clone.1 | convolution fusion | flops 283123712 | bytes 33554752 | tf_op jit(solution)/shard_map/while/body/eval_jaxpr/dot_general | solution.py:47
  157.4 4.7 copy.22
  163.5 6.7 %fusion.75 = f32[64,32768]{1,0:T(8,128)} fusion(f32[64,32768]{1,0:T(8,128)S(1)} %fusion.74, f32[64,32768]{1,0:T(8,128)} %get-tuple-element.504, f32[64,32768]{1,0:T(8,128)S(1)} %bitcast.50, pred[]{:T(512)S(6)} %compare.6, s32[64]{0:T(128)S(1)} %dynamic_slice.60, pred[64]{0:T(512)(128)(4,1)S(1)} %add_compare_fusion.4), kind=kOutput, calls=%fused_computation.5.clone.1 | convolution fusion | flops 283123712 | bytes 33554752 | tf_op jit(solution)/shard_map/while/body/eval_jaxpr/dot_general | solution.py:47
  176.3 4.7 copy.22
  182.4 6.7 %fusion.75 = f32[64,32768]{1,0:T(8,128)} fusion(f32[64,32768]{1,0:T(8,128)S(1)} %fusion.74, f32[64,32768]{1,0:T(8,128)} %get-tuple-element.504, f32[64,32768]{1,0:T(8,128)S(1)} %bitcast.50, pred[]{:T(512)S(6)} %compare.6, s32[64]{0:T(128)S(1)} %dynamic_slice.60, pred[64]{0:T(512)(128)(4,1)S(1)} %add_compare_fusion.4), kind=kOutput, calls=%fused_computation.5.clone.1 | convolution fusion | flops 283123712 | bytes 33554752 | tf_op jit(solution)/shard_map/while/body/eval_jaxpr/dot_general | solution.py:47
  189.0 5.8 %convert_element_type.95 = bf16[64,32768]{1,0:T(8,128)(2,1)} convert(f32[64,32768]{1,0:T(8,128)} %get-tuple-element.311) | non-fusion elementwise | flops 2097152 | bytes 12582912 | tf_op jit(solution)/shard_map/convert_element_type | solution.py:97
  194.8 7.4 %convert_element_type.96 = bf16[8192,256]{1,0:T(8,128)(2,1)} reshape(bf16[64,32768]{1,0:T(8,128)(2,1)} %convert_element_type.95) | data formatting | bytes 8388608 | tf_op jit(solution)/shard_map/convert_element_type | solution.py:97
  202.3 77.9 %reduce-scatter.3.cloned.1.call-done = bf16[512,256]{1,0:T(8,128)(2,1)} async-done(((bf16[8192,256]{1,0:T(8,128)(2,1)}), bf16[512,256]{1,0:T(8,128)(2,1)}) %reduce-scatter.3.cloned.1.call-update) | async-done | bytes 262160 | tf_op jit(solution)/shard_map/reduce_scatter | solution.py:96
  283.3 22.5 %copy.10 = bf16[1,1,512,128,128]{3,4,2,1,0:T(8,128)(2,1)} copy(bf16[1,1,512,128,128]{4,3,2,1,0:T(8,128)(2,1)} %bitcast.58) | data formatting | bytes 33554432 | tf_op args[0]
  307.0 27.2 %all-gather.5.cloned.1.call-done = bf16[8192,256]{1,0:T(8,128)(2,1)} async-done(((bf16[512,256]{1,0:T(8,128)(2,1)}), bf16[8192,256]{1,0:T(8,128)(2,1)}) %all-gather.5.cloned.1.call-update) | async-done | bytes 4194320 | tf_op jit(solution)/shard_map/all_gather | solution.py:103
  334.2 7.4 %reshape_reshape.9 = bf16[64,32768]{1,0:T(8,128)(2,1)} reshape(bf16[8192,256]{1,0:T(8,128)(2,1)} %all-gather.5.cloned.1.call-done) | data formatting | bytes 8388608 | tf_op jit(solution)/shard_map/reshape;reshape | solution.py:23
  341.6 157.8 %while.29 = (s32[]{:T(128)}, f32[32,32768]{1,0:T(8,128)}, s32[512]{0:T(512)S(1)}, s32[]{:T(128)}, bf16[512,128,128]{1,2,0:T(8,128)(2,1)}, /*index=5*/s32[512]{0:...) while((s32[]{:T(128)}, f32[32,32768]{1,0:T(8,128)}, ...), condition=%wide.region_5.0_spmd.clone, body=%wide.region_4.0_spmd.clone.sunk | while | flops 1089482880 | bytes 115345592 | solution.py:53
  342.4 3.5 convolution_convert_fusion.6
  347.0 2.9 fusion.82
  349.9 4.7 copy.24
  362.2 3.5 convolution_convert_fusion.6
  366.8 2.9 fusion.82
  369.6 4.7 copy.24
  381.9 3.5 convolution_convert_fusion.6
  389.3 4.7 copy.24
  401.6 3.5 convolution_convert_fusion.6
  409.0 4.7 copy.24
  421.3 3.5 convolution_convert_fusion.6
  428.8 4.7 copy.24
  441.0 3.5 convolution_convert_fusion.6
  445.6 2.9 fusion.82
  448.5 4.7 copy.24
  460.8 3.5 convolution_convert_fusion.6
  468.2 4.7 copy.24
  480.5 3.5 convolution_convert_fusion.6
  487.9 4.7 copy.24
  505.9 32.0 %reduce-scatter.5.cloned.1.call-done = bf16[512,256]{1,0:T(8,128)(2,1)} async-done(((bf16[4096,256]{1,0:T(8,128)(2,1)}), bf16[512,256]{1,0:T(8,128)(2,1)}) %reduce-scatter.5.cloned.1.call-update) | async-done | bytes 262160 | tf_op jit(solution)/shard_map/reduce_scatter | solution.py:120
  (171 shorter events, 150.1 us)
Async XLA Ops:
  7.2 273.0 %copy-start = (bf16[256,256]{1,0:T(8,128)(2,1)S(1)}, bf16[256,256]{1,0:T(8,128)(2,1)}, u32[]{:S(2)}) copy-start(bf16[256,256]{1,0:T(8,128)(2,1)} %param.16) | copy-start | bytes 393220
  7.2 33.3 %copy-start.7 = (s32[1,1,512]{2,1,0:T(1,128)S(1)}, s32[1,1,512]{2,1,0:T(1,128)}, u32[]{:S(2)}) copy-start(s32[1,1,512]{2,1,0:T(1,128)} %param.13) | copy-start | bytes 6148
  7.2 33.3 %copy-start.6 = (s32[1,1,512]{2,1,0:T(1,128)S(1)}, s32[1,1,512]{2,1,0:T(1,128)}, u32[]{:S(2)}) copy-start(s32[1,1,512]{2,1,0:T(1,128)} %param.12) | copy-start | bytes 6148
  7.2 30.4 %all-gather.3.cloned.1.call-start = ((), (), s32[]{:S(2)}) async-start(), calls=%async_computation.2 | async-start | bytes 2359296 | tf_op jit(solution)/shard_map/all_gather | solution.py:81
  7.9 272.3 %reduce-scatter.3.cloned.1.call-start = ((), (), s32[]{:S(2)}) async-start(), calls=%async_computation.3 | async-start | bytes 4456448 | tf_op jit(solution)/shard_map/reduce_scatter | solution.py:96
  202.2 78.0 %copy-start.5 = (bf16[512,256]{1,0:T(8,128)(2,1)S(1)}, bf16[512,256]{1,0:T(8,128)(2,1)}, u32[]{:S(2)}) copy-start(bf16[512,256]{1,0:T(8,128)(2,1)} %param.17) | copy-start | bytes 786436
  202.2 132.0 %all-gather.5.cloned.1.call-start = ((), (), s32[]{:S(2)}) async-start(), calls=%async_computation.5 | async-start | bytes 4456448 | tf_op jit(solution)/shard_map/all_gather | solution.py:103
  283.2 221.0 %all-reduce.2.cloned.1.call-start = ((), (), s32[]{:S(2)}) async-start(), calls=%async_computation.4 | async-start | bytes 524288 | tf_op jit(solution)/shard_map/psum | solution.py:107
  283.3 22.5 %copy-start.4 = (bf16[512,256]{1,0:T(8,128)(2,1)S(1)}, bf16[512,256]{1,0:T(8,128)(2,1)}, u32[]{:S(2)}) copy-start(bf16[512,256]{1,0:T(8,128)(2,1)} %reduce-scatter.3.cloned.1.call-done) | copy-start | bytes 786436
  306.8 231.2 %reduce-scatter.5.cloned.1.call-start = ((), (), s32[]{:S(2)}) async-start(), calls=%async_computation.6 | async-start | bytes 2359296 | tf_op jit(solution)/shard_map/reduce_scatter | solution.py:120
  354.6 2.2 copy-start.2
  359.4 2.0 copy-start.3
  374.4 2.2 copy-start.2
  379.1 2.0 copy-start.3
  394.1 2.2 copy-start.2
  398.8 2.0 copy-start.3
  413.8 2.2 copy-start.2
  418.5 2.0 copy-start.3
  433.5 2.2 copy-start.2
  438.2 2.0 copy-start.3
  453.2 2.2 copy-start.2
  458.0 2.0 copy-start.3
  473.0 2.2 copy-start.2
  477.7 2.0 copy-start.3
  492.7 2.2 copy-start.2
  497.4 2.0 copy-start.3
  499.4 40.4 %copy-start.1 = (bf16[256,256]{1,0:T(8,128)(2,1)S(1)}, bf16[256,256]{1,0:T(8,128)(2,1)}, u32[]{:S(2)}) copy-start(bf16[256,256]{1,0:T(8,128)(2,1)} %param.16) | copy-start | bytes 393220
Sparse Core Ops, SparseCore 0:
  9.8 27.8 all-gather.2
  202.3 77.8 reduce-scatter.2
  283.4 50.7 all-gather.4
  340.1 141.5 all-reduce.1
  504.4 33.5 reduce-scatter.4
where the time goes:
time: 549 us; the launch traced here: 546 us
  matrix products  177 us (32%)
  waiting for transfers between devices  168 us (31%)
  local copies, waits for them, and re-layouts  165 us (30%)
  other arithmetic  22 us (4%)
  between operations  13.9 us (3%)
    while x64, local copies, waits for them, and re-layouts  120 us
    reduce_scatter x1, waiting for transfers between devices, per_device(): lax.psum_scatter(partial_flat.astype(jnp.bfloat16), 'col', scatter_dimens...  77.9 us
    dot_general x16, matrix products, add_block(): lax.dot_general(add_table, lower_part, contract, preferred_element_type=j...  71.5 us
    dot_general x16, matrix products, add_block(): jnp.einsum(einsum_form, tile_part, picked, preferred_element_type=jnp.flo...  45.7 us
    dot_general x16, matrix products, add_block(): jnp.dot(take_table, source_flat, preferred_element_type=jnp.float32)  38.1 us
    reduce_scatter x1, waiting for transfers between devices, per_device(): lax.psum_scatter(partial_cols.reshape(col_tiles * tile_edge, feat_width)....  32 us
    all_gather x1, waiting for transfers between devices, per_device(): column_block = lax.all_gather(features, 'row', axis=0, tiled=True)  29.6 us
    all_gather x1, waiting for transfers between devices, per_device(): row_block = lax.all_gather(own_grad, 'col', axis=0, tiled=True)  27.2 us
  transfers between devices with their start and end apart: 5, of which 4 were waited for; matrix products, arithmetic and copies ran while one was open for 31% of the time, Pallas kernels for 0%

commit v1 on v0

v1 whole, which is shorter than its diff:
```python
import functools
import math

import jax
import jax.numpy as jnp
from jax import lax
from jax.experimental import pallas as pl
from jax.experimental.pallas import tpu as pltpu
from jax.sharding import PartitionSpec as P

SLOTS_PER_STEP = 32


def spmm_kernel(transpose, acc_index, src_index, count_ref, tiles_ref, src_ref, out_ref, acc_ref):
    step = pl.program_id(0)
    per_step = tiles_ref.shape[0]
    live = count_ref[0]
    acc_last = acc_ref.shape[0] - 1
    src_last = src_ref.shape[0] - 1

    @pl.when(step == 0)
    def _():
        acc_ref[...] = jnp.zeros_like(acc_ref)

    def one_slot(k, carry):
        slot = step * per_step + k

        @pl.when(slot < live)
        def _():
            target = jnp.clip(acc_index[slot], 0, acc_last)
            picked = jnp.clip(src_index[slot], 0, src_last)
            tile = tiles_ref[k]
            block = src_ref[picked]
            if transpose:
                product = lax.dot_general(
                    tile, block, (((0,), (0,)), ((), ())), preferred_element_type=jnp.float32
                )
            else:
                product = jnp.dot(tile, block, preferred_element_type=jnp.float32)
            acc_ref[target] += product

        return carry

    lax.fori_loop(0, per_step, one_slot, 0)

    @pl.when(step == pl.num_programs(0) - 1)
    def _():
        out_ref[...] = acc_ref[...].astype(out_ref.dtype)


def sparse_product(tile_block, acc_index, src_index, live_count, source, segments, transpose):
    slot_total, tile_edge, _ = tile_block.shape
    feat_width = source.shape[2]
    per_step = min(SLOTS_PER_STEP, slot_total)
    steps = slot_total // per_step

    def tile_map(step, acc_ref, src_ref, count_ref):
        last_live = jnp.maximum(count_ref[0] - 1, 0) // per_step
        return (jnp.minimum(step, last_live), 0, 0)

    grid_spec = pltpu.PrefetchScalarGridSpec(
        num_scalar_prefetch=3,
        grid=(steps,),
        in_specs=[
            pl.BlockSpec((per_step, tile_edge, tile_edge), tile_map),
            pl.BlockSpec(source.shape, lambda step, *_: (0, 0, 0)),
        ],
        out_specs=pl.BlockSpec((segments, tile_edge, feat_width), lambda step, *_: (0, 0, 0)),
        scratch_shapes=[pltpu.VMEM((segments, tile_edge, feat_width), jnp.float32)],
    )
    flops = 2 * slot_total * tile_edge * tile_edge * feat_width
    bytes_accessed = (
        tile_block.size * 2 + source.size * 2 + segments * tile_edge * feat_width * 2
    )
    return pl.pallas_call(
        functools.partial(spmm_kernel, transpose),
        out_shape=jax.ShapeDtypeStruct((segments, tile_edge, feat_width), jnp.bfloat16),
        grid_spec=grid_spec,
        compiler_params=pltpu.CompilerParams(
            dimension_semantics=("arbitrary",), vmem_limit_bytes=56 * 1024 * 1024
        ),
        cost_estimate=pl.CostEstimate(
            flops=flops, transcendentals=0, bytes_accessed=bytes_accessed
        ),
    )(acc_index, src_index, live_count, tile_block, source)


def activation(aggregated, weight, cot_rows):
    hidden = jnp.dot(aggregated, weight, preferred_element_type=jnp.float32)
    sigmoid_value = jax.nn.sigmoid(hidden)
    output = (hidden * sigmoid_value).astype(jnp.bfloat16)
    silu_slope = sigmoid_value * (1.0 + hidden * (1.0 - sigmoid_value))
    hidden_grad = (cot_rows.astype(jnp.float32) * silu_slope).astype(jnp.bfloat16)
    return (output, hidden_grad)


def per_device(tile_values, tile_rows, tile_cols, tile_count, features, weight, cotangent):
    slot_total = tile_values.shape[2]
    tile_edge = tile_values.shape[3]
    tile_block = tile_values.reshape(slot_total, tile_edge, tile_edge)
    row_index = tile_rows.reshape(slot_total)
    col_index = tile_cols.reshape(slot_total)
    live_count = tile_count.reshape(1)
    own_rows = features.shape[0]
    feat_width = features.shape[1]
    row_count = lax.axis_size("row")
    col_count = lax.axis_size("col")
    row_tiles = col_count * own_rows // tile_edge
    col_tiles = row_count * own_rows // tile_edge
    column_block = lax.all_gather(features, "row", axis=0, tiled=True)
    source = column_block.reshape(col_tiles, tile_edge, feat_width)
    partial_rows = sparse_product(
        tile_block, row_index, col_index, live_count, source, row_tiles, False
    )
    partial_flat = partial_rows.reshape(row_tiles * tile_edge, feat_width)
    node_total = row_count * col_count * own_rows
    aggregated = lax.psum_scatter(partial_flat, "col", scatter_dimension=0, tiled=True)
    output, hidden_grad = activation(aggregated, weight, cotangent)
    own_grad = lax.dot_general(
        hidden_grad, weight, (((1,), (1,)), ((), ())), preferred_element_type=jnp.float32
    ).astype(jnp.bfloat16)
    row_block = lax.all_gather(own_grad, "col", axis=0, tiled=True)
    local_grad = lax.dot_general(
        aggregated, hidden_grad, (((0,), (0,)), ((), ())), preferred_element_type=jnp.float32
    )
    weight_grad = lax.psum(local_grad, ("row", "col")) * (1.0 / math.sqrt(node_total))
    source_back = row_block.reshape(row_tiles, tile_edge, feat_width)
    partial_cols = sparse_product(
        tile_block, col_index, row_index, live_count, source_back, col_tiles, True
    )
    input_grad = lax.psum_scatter(
        partial_cols.reshape(col_tiles * tile_edge, feat_width),
        "row",
        scatter_dimension=0,
        tiled=True,
    ).astype(jnp.float32)
    return (output, weight_grad, input_grad)


def solution(mesh):
    placed = (
        P("row", "col", None, None, None),
        P("row", "col", None),
        P("row", "col", None),
        P("row", "col"),
        P(("row", "col"), None),
        P(),
        P(("row", "col"), None),
    )
    return jax.shard_map(
        per_device,
        mesh=mesh,
        in_specs=placed,
        out_specs=(P(("row", "col"), None), P(), P(("row", "col"), None)),
        check_vma=False,
    )
```

time: 549 us -> 445 us (0.81)
  Pallas kernels: 0 us -> 194 us
  matrix products: 177 us -> 4.05 us
  local copies, waits for them, and re-layouts: 165 us -> 0.02 us
  waiting for transfers between devices: 168 us -> 229 us
  other arithmetic: 22 us -> 3.45 us
    pallas_call x0 -> x2, Pallas kernels: none -> 194 us  [sparse_product(): pl.pallas_call(functools.partial(spmm_kernel, transpose), out_shape=jax.S...]
    dot_general x64 -> x0, matrix products: 173 us -> none  [the longest x16 71.5 us: add_block(): lax.dot_general(add_table, lower_part, contract, preferred_element_type=j...]
    while x64 -> x0, local copies, waits for them, and re-layouts: 120 us -> none
    psum x1, waiting for transfers between devices: 0.02 us -> 40.3 us  [per_device(): lax.psum(local_grad, ('row', 'col')) * (1.0 / math.sqrt(node_total))]
    all_gather x1, waiting for transfers between devices: 27.2 us -> 49.8 us  [per_device(): row_block = lax.all_gather(own_grad, 'col', axis=0, tiled=True)]
    unnamed x13 -> x6, local copies, waits for them, and re-layouts: 22.5 us -> 0.02 us
    lt x16 -> x0, other arithmetic: 10.4 us -> none  [add_block(): is_live = first_slot + lax.iota(jnp.int32, block_size) < live_count]
    another operation x2 -> x0, local copies, waits for them, and re-layouts: 10.3 us -> none  [sparse_product(): source_flat = source.reshape(source_count, tile_edge * feat_width)]
  transfers between devices with their start and end apart: 5 -> 5, of which waited for: 4 -> 5; matrix products, arithmetic and copies ran while one was open for 31% -> 1% of each run, Pallas kernels for 0% -> 24%
where the time goes in v1:
time: 445 us; the launch traced here: 444 us
  waiting for transfers between devices  229 us (51%)
  Pallas kernels  194 us (44%)
  between operations  14.4 us (3%)
    pallas_call x2, Pallas kernels, sparse_product(): pl.pallas_call(functools.partial(spmm_kernel, transpose), out_shape=jax.S...  194 us
    reduce_scatter x1, waiting for transfers between devices, per_device(): lax.psum_scatter(partial_flat, 'col', scatter_dimension=0, tiled=True)  77 us
    all_gather x1, waiting for transfers between devices, per_device(): row_block = lax.all_gather(own_grad, 'col', axis=0, tiled=True)  49.8 us
    psum x1, waiting for transfers between devices, per_device(): lax.psum(local_grad, ('row', 'col')) * (1.0 / math.sqrt(node_total))  40.3 us
    reduce_scatter x1, waiting for transfers between devices, per_device(): lax.psum_scatter(partial_cols.reshape(col_tiles * tile_edge, feat_width),...  31.6 us
    all_gather x1, waiting for transfers between devices, per_device(): column_block = lax.all_gather(features, 'row', axis=0, tiled=True)  29 us
  transfers between devices with their start and end apart: 5, of which 5 were waited for; matrix products, arithmetic and copies ran while one was open for 1% of the time, Pallas kernels for 24%

profile of v1, /device:TPU:0, one launch (start us, length us, event | category | flops | bytes accessed | tf_op | source)
XLA Modules:
  0.0 444.3 jit_solution(9432629551905720428)
XLA Ops:
  7.2 0.0 copy-start
  7.2 0.0 all-gather.3.cloned.1.call-start
  7.2 0.7 all-gather.3.cloned.1.call-update
  7.9 0.0 reduce-scatter.3.cloned.1.call-start
  8.6 29.0 %all-gather.3.cloned.1.call-done = bf16[4096,256]{1,0:T(8,128)(2,1)} async-done(((bf16[512,256]{1,0:T(8,128)(2,1)}), bf16[4096,256]{1,0:T(8,128)(2,1)}) %all-gather.3.cloned.1.call-update) | async-done | bytes 2097168 | tf_op jit(solution)/shard_map/all_gather | solution.py:110
  37.6 85.8 %shard_map.94 = bf16[64,128,256]{2,1,0:T(8,128)(2,1)} custom-call(s32[512]{0:T(512)} %bitcast.22, s32[512]{0:T(512)} %bitcast.24, s32[1]{0:T(128)} %bitcast.14.count_ref, bf16[512,128,128]{2,1,0:T(8,128)(2,1)} %bitcast.16, bf16[32,128,256]{2,1,0:T(8,128)(2,1)} %bitcast.21), custom_call_target="tpu_custom_call" | custom-call | flops 4294967296 | bytes 23068672 | tf_op jit(solution)/shard_map/pallas_call | solution.py:75
  123.4 0.0 copy-start.2
  123.4 0.0 reduce-scatter.3.cloned.1.call-update
  123.4 0.0 all-gather.5.cloned.1.call-start
  123.4 77.0 %reduce-scatter.3.cloned.1.call-done = bf16[512,256]{1,0:T(8,128)(2,1)} async-done(((bf16[8192,256]{1,0:T(8,128)(2,1)}), bf16[512,256]{1,0:T(8,128)(2,1)}) %reduce-scatter.3.cloned.1.call-update) | async-done | bytes 262160 | tf_op jit(solution)/shard_map/reduce_scatter | solution.py:117
  200.4 0.0 copy-done
  200.5 0.0 copy-done.2
  200.5 0.0 copy-start.1
  200.5 2.1 multiply_convert_fusion
  202.6 1.0 convolution_convert_fusion
  203.5 0.0 all-gather.5.cloned.1.call-update
  203.6 0.0 all-reduce.2.cloned.1.call-start
  203.6 0.0 copy-done.1
  203.6 1.0 fusion
  204.6 0.0 all-reduce.2.cloned.1.call-update
  204.6 0.0 reduce-scatter.5.cloned.1.call-start
  204.7 49.8 %all-gather.5.cloned.1.call-done = bf16[8192,256]{1,0:T(8,128)(2,1)} async-done(((bf16[512,256]{1,0:T(8,128)(2,1)}), bf16[8192,256]{1,0:T(8,128)(2,1)}) %all-gather.5.cloned.1.call-update) | async-done | bytes 4194320 | tf_op jit(solution)/shard_map/all_gather | solution.py:122
  254.5 107.8 %shard_map.95 = bf16[32,128,256]{2,1,0:T(8,128)(2,1)} custom-call(s32[512]{0:T(512)} %bitcast.25, s32[512]{0:T(512)} %bitcast.23, s32[1]{0:T(128)} %bitcast.15.count_ref, bf16[512,128,128]{2,1,0:T(8,128)(2,1)} %bitcast.17, bf16[64,128,256]{2,1,0:T(8,128)(2,1)} %bitcast.20), custom_call_target="tpu_custom_call" | custom-call | flops 4294967296 | bytes 23068672 | tf_op jit(solution)/shard_map/pallas_call | solution.py:75
  362.3 0.0 reduce-scatter.5.cloned.1.call-update
  362.3 40.3 %all-reduce.2.cloned.1.call-done = f32[256,256]{1,0:T(8,128)} async-done(((f32[256,256]{1,0:T(8,128)}), f32[256,256]{1,0:T(8,128)}) %all-reduce.2.cloned.1.call-update) | async-done | bytes 262160 | tf_op jit(solution)/shard_map/psum | solution.py:126
  402.6 1.7 broadcast_multiply_fusion
  404.3 31.6 %reduce-scatter.5.cloned.1.call-done = bf16[512,256]{1,0:T(8,128)(2,1)} async-done(((bf16[4096,256]{1,0:T(8,128)(2,1)}), bf16[512,256]{1,0:T(8,128)(2,1)}) %reduce-scatter.5.cloned.1.call-update) | async-done | bytes 262160 | tf_op jit(solution)/shard_map/reduce_scatter | solution.py:131
  435.9 1.8 convert_element_type.19
Async XLA Ops:
  7.2 193.3 %copy-start = (bf16[256,256]{1,0:T(8,128)(2,1)S(1)}, bf16[256,256]{1,0:T(8,128)(2,1)}, u32[]{:S(2)}) copy-start(bf16[256,256]{1,0:T(8,128)(2,1)} %param.12) | copy-start | bytes 393220
  7.2 30.4 %all-gather.3.cloned.1.call-start = ((), (), s32[]{:S(2)}) async-start(), calls=%async_computation.2 | async-start | bytes 2359296 | tf_op jit(solution)/shard_map/all_gather | solution.py:110
  7.9 192.5 %reduce-scatter.3.cloned.1.call-start = ((), (), s32[]{:S(2)}) async-start(), calls=%async_computation.3 | async-start | bytes 4456448 | tf_op jit(solution)/shard_map/reduce_scatter | solution.py:117
  123.4 77.1 %copy-start.2 = (bf16[512,256]{1,0:T(8,128)(2,1)S(1)}, bf16[512,256]{1,0:T(8,128)(2,1)}, u32[]{:S(2)}) copy-start(bf16[512,256]{1,0:T(8,128)(2,1)} %param.13) | copy-start | bytes 786436
  123.4 131.1 %all-gather.5.cloned.1.call-start = ((), (), s32[]{:S(2)}) async-start(), calls=%async_computation.5 | async-start | bytes 4456448 | tf_op jit(solution)/shard_map/all_gather | solution.py:122
  200.5 3.2 copy-start.1
  203.6 199.1 %all-reduce.2.cloned.1.call-start = ((), (), s32[]{:S(2)}) async-start(), calls=%async_computation.4 | async-start | bytes 524288 | tf_op jit(solution)/shard_map/psum | solution.py:126
  204.6 231.3 %reduce-scatter.5.cloned.1.call-start = ((), (), s32[]{:S(2)}) async-start(), calls=%async_computation.6 | async-start | bytes 2359296 | tf_op jit(solution)/shard_map/reduce_scatter | solution.py:131
Sparse Core Ops, SparseCore 0:
  9.7 27.8 all-gather.2
  123.5 76.8 reduce-scatter.2
  203.7 50.7 all-gather.4
  260.4 142.2 all-reduce.1
  405.0 30.8 reduce-scatter.4

commit v2 on v1

--- a/solution.py
+++ b/solution.py
@@ -83,6 +83,149 @@
             flops=flops, transcendentals=0, bytes_accessed=bytes_accessed
         ),
     )(acc_index, src_index, live_count, tile_block, source)
+
+
+def peer_id(axis, other_axis, peer):
+    if axis == "row":
+        return (peer, lax.axis_index(other_axis))
+    return (lax.axis_index(other_axis), peer)
+
+
+def greet_all(axis, other_axis, n, me):
+    barrier = pltpu.get_barrier_semaphore()
+    for offset in range(1, n):
+        peer = lax.rem(me + offset, n)
+        pl.semaphore_signal(
+            barrier, 1, device_id=peer_id(axis, other_axis, peer),
+            device_id_type=pl.DeviceIdType.MESH,
+        )
+    pl.semaphore_wait(barrier, n - 1)
+
+
+def scatter_sum_kernel(axis, other_axis, n, x_hbm, out_ref, recv, send_sems, recv_sems, own_sem):
+    me = lax.axis_index(axis)
+    greet_all(axis, other_axis, n, me)
+    own = pltpu.make_async_copy(x_hbm.at[me], recv.at[me], own_sem)
+    own.start()
+    sends = []
+    for offset in range(1, n):
+        peer = lax.rem(me + offset, n)
+        copy = pltpu.make_async_remote_copy(
+            src_ref=x_hbm.at[peer],
+            dst_ref=recv.at[me],
+            send_sem=send_sems.at[offset],
+            recv_sem=recv_sems.at[me],
+            device_id=peer_id(axis, other_axis, peer),
+            device_id_type=pl.DeviceIdType.MESH,
+        )
+        copy.start()
+        sends.append(copy)
+    own.wait()
+    for offset in range(1, n):
+        source = lax.rem(me + n - offset, n)
+        pltpu.make_async_remote_copy(
+            src_ref=x_hbm.at[source],
+            dst_ref=recv.at[source],
+            send_sem=send_sems.at[offset],
+            recv_sem=recv_sems.at[source],
+            device_id=peer_id(axis, other_axis, source),
+            device_id_type=pl.DeviceIdType.MESH,
+        ).wait_recv()
+    total = recv[0].astype(jnp.float32)
+    for j in range(1, n):
+        total = total + recv[j].astype(jnp.float32)
+    out_ref[...] = total.astype(out_ref.dtype)
+    for copy in sends:
+        copy.wait_send()
+
+
+def scatter_sum(x, axis, other_axis, out_dtype, collective_id):
+    n, rows, lanes = x.shape
+    return pl.pallas_call(
+        functools.partial(scatter_sum_kernel, axis, other_axis, n),
+        out_shape=jax.ShapeDtypeStruct((rows, lanes), out_dtype),
+        in_specs=[pl.BlockSpec(memory_space=pl.ANY)],
+        out_specs=pl.BlockSpec(memory_space=pltpu.VMEM),
+        scratch_shapes=[
+            pltpu.VMEM((n, rows, lanes), x.dtype),
+            pltpu.SemaphoreType.DMA((n,)),
+            pltpu.SemaphoreType.DMA((n,)),
+            pltpu.SemaphoreType.DMA(()),
+        ],
+        compiler_params=pltpu.CompilerParams(
+            collective_id=collective_id, has_side_effects=True,
+            vmem_limit_bytes=48 * 1024 * 1024,
+        ),
+    )(x)
+
+
+def gather_all_kernel(axis, other_axis, n, x_ref, out_ref, recv, send_sems, recv_sems):
+    me = lax.axis_index(axis)
+    recv[me] = x_ref[...]
+    greet_all(axis, other_axis, n, me)
+    sends = []
+    for offset in range(1, n):
+        peer = lax.rem(me + offset, n)
+        copy = pltpu.make_async_remote_copy(
+            src_ref=x_ref,
+            dst_ref=recv.at[me],
+            send_sem=send_sems.at[offset],
+            recv_sem=recv_sems.at[me],
+            device_id=peer_id(axis, other_axis, peer),
+            device_id_type=pl.DeviceIdType.MESH,
+        )
+        copy.start()
+        sends.append(copy)
+    for offset in range(1, n):
+        source = lax.rem(me + n - offset, n)
+        pltpu.make_async_remote_copy(
+            src_ref=x_ref,
+            dst_ref=recv.at[source],
+            send_sem=send_sems.at[offset],
+            recv_sem=recv_sems.at[source],
+            device_id=peer_id(axis, other_axis, source),
+            device_id_type=pl.DeviceIdType.MESH,
+        ).wait_recv()
+    out_ref[...] = recv[...]
+    for copy in sends:
+        copy.wait_send()
+
+
+def gather_all(x, axis, other_axis, n, collective_id):
+    rows, lanes = x.shape
+    return pl.pallas_call(
+        functools.partial(gather_all_kernel, axis, other_axis, n),
+        out_shape=jax.ShapeDtypeStruct((n, rows, lanes), x.dtype),
+        in_specs=[pl.BlockSpec(memory_space=pltpu.VMEM)],
+        out_specs=pl.BlockSpec(memory_space=pltpu.VMEM),
+        scratch_shapes=[
+            pltpu.VMEM((n, rows, lanes), x.dtype),
+            pltpu.SemaphoreType.DMA((n,)),
+            pltpu.SemaphoreType.DMA((n,)),
+        ],
+        compiler_params=pltpu.CompilerParams(
+            collective_id=collective_id, has_side_effects=True,
+            vmem_limit_bytes=48 * 1024 * 1024,
+        ),
+    )(x)
+
+
+def all_sum(local, collective_base):
+    row_count = lax.axis_size("row")
+    col_count = lax.axis_size("col")
+    height, width = local.shape
+    by_col = scatter_sum(
+        local.reshape(col_count, height // col_count, width), "col", "row", jnp.float32,
+        collective_base,
+    )
+    part = height // col_count
+    by_row = scatter_sum(
+        by_col.reshape(row_count, part // row_count, width), "row", "col", jnp.float32,
+        collective_base + 1,
+    )
+    back_row = gather_all(by_row, "row", "col", row_count, collective_base + 2)
+    back_col = gather_all(back_row.reshape(part, width), "col", "row", col_count, collective_base + 3)
+    return back_col.reshape(height, width)
 
 
 def activation(aggregated, weight, cot_rows):
@@ -114,7 +257,9 @@
     )
     partial_flat = partial_rows.reshape(row_tiles * tile_edge, feat_width)
     node_total = row_count * col_count * own_rows
-    aggregated = lax.psum_scatter(partial_flat, "col", scatter_dimension=0, tiled=True)
+    aggregated = scatter_sum(
+        partial_rows.reshape(col_count, own_rows, feat_width), "col", "row", jnp.bfloat16, 0
+    )
     output, hidden_grad = activation(aggregated, weight, cotangent)
     own_grad = lax.dot_general(
         hidden_grad, weight, (((1,), (1,)), ((), ())), preferred_element_type=jnp.float32
@@ -123,7 +268,7 @@
     local_grad = lax.dot_general(
         aggregated, hidden_grad, (((0,), (0,)), ((), ())), preferred_element_type=jnp.float32
     )
-    weight_grad = lax.psum(local_grad, ("row", "col")) * (1.0 / math.sqrt(node_total))
+    weight_grad = all_sum(local_grad, 1) * (1.0 / math.sqrt(node_total))
     source_back = row_block.reshape(row_tiles, tile_edge, feat_width)
     partial_cols = sparse_product(
         tile_block, col_index, row_index, live_count, source_back, col_tiles, True

time: 445 us -> 405 us (0.910)
  waiting for transfers between devices: 229 us -> 119 us
  Pallas kernels: 194 us -> 264 us
    pallas_call x0 -> x5, Pallas kernels: none -> 200 us  [the longest x3 184 us: scatter_sum(): pl.pallas_call(functools.partial(scatter_sum_kernel, axis, other_axis, n)...]
    pallas_call x2, Pallas kernels: 194 us -> 64.4 us  [sparse_product(): pl.pallas_call(functools.partial(spmm_kernel, transpose), out_shape=jax.S...]
    reduce_scatter x1 -> x0, waiting for transfers between devices: 77 us -> none  [per_device(): lax.psum_scatter(partial_flat, 'col', scatter_dimension=0, tiled=True)]
    psum x1 -> x0, waiting for transfers between devices: 40.3 us -> none  [per_device(): lax.psum(local_grad, ('row', 'col')) * (1.0 / math.sqrt(node_total))]
    all_gather x1, waiting for transfers between devices: 49.8 us -> 87.5 us  [per_device(): row_block = lax.all_gather(own_grad, 'col', axis=0, tiled=True)]
    reduce_scatter x1, waiting for transfers between devices: 31.6 us -> 1.73 us  [per_device(): lax.psum_scatter(partial_cols.reshape(col_tiles * tile_edge, feat_width),...]
  transfers between devices with their start and end apart: 5 -> 3, of which waited for: 5 -> 3; matrix products, arithmetic and copies ran while one was open for 1% -> 0% of each run, Pallas kernels for 24% -> 26%
where the time goes in v2:
time: 405 us; the launch traced here: 404 us
  Pallas kernels  264 us (65%)
  waiting for transfers between devices  119 us (29%)
  between operations  14.5 us (4%)
    pallas_call x3, Pallas kernels, scatter_sum(): pl.pallas_call(functools.partial(scatter_sum_kernel, axis, other_axis, n)...  184 us
    all_gather x1, waiting for transfers between devices, per_device(): row_block = lax.all_gather(own_grad, 'col', axis=0, tiled=True)  87.5 us
    pallas_call x2, Pallas kernels, sparse_product(): pl.pallas_call(functools.partial(spmm_kernel, transpose), out_shape=jax.S...  64.4 us
    all_gather x1, waiting for transfers between devices, per_device(): column_block = lax.all_gather(features, 'row', axis=0, tiled=True)  29 us
    pallas_call x2, Pallas kernels, gather_all(): pl.pallas_call(functools.partial(gather_all_kernel, axis, other_axis, n),...  15.1 us
  transfers between devices with their start and end apart: 3, of which 3 were waited for; matrix products, arithmetic and copies ran while one was open for 0% of the time, Pallas kernels for 26%

profile of v2, /device:TPU:0, one launch (start us, length us, event | category | flops | bytes accessed | tf_op | source)
XLA Modules:
  0.0 404.5 jit_solution(16033069307563296353)
XLA Ops:
  7.2 0.0 copy-start
  7.2 0.0 all-gather.3.cloned.1.call-start
  7.2 0.7 all-gather.3.cloned.1.call-update
  7.9 0.0 all-gather.5.cloned.1.call-start
  8.6 29.0 %all-gather.3.cloned.1.call-done = bf16[4096,256]{1,0:T(8,128)(2,1)} async-done(((bf16[512,256]{1,0:T(8,128)(2,1)}), bf16[4096,256]{1,0:T(8,128)(2,1)}) %all-gather.3.cloned.1.call-update) | async-done | bytes 2097168 | tf_op jit(solution)/shard_map/all_gather | solution.py:253
  37.6 29.7 %shard_map.94 = bf16[64,128,256]{2,1,0:T(8,128)(2,1)} custom-call(s32[512]{0:T(512)} %bitcast.26, s32[512]{0:T(512)} %bitcast.28, s32[1]{0:T(128)} %bitcast.16.count_ref, bf16[512,128,128]{2,1,0:T(8,128)(2,1)} %bitcast.20, bf16[32,128,256]{2,1,0:T(8,128)(2,1)} %bitcast.24), custom_call_target="tpu_custom_call" | custom-call | flops 4294967296 | bytes 23068672 | tf_op jit(solution)/shard_map/pallas_call | solution.py:75
  67.3 0.0 copy-start.1
  67.3 2.2 copy-done.1
  69.5 0.0 copy-start.2
  69.5 95.5 %shard_map.95 = bf16[512,256]{1,0:T(8,128)(2,1)S(1)} custom-call(bf16[16,512,256]{2,1,0:T(8,128)(2,1)S(1)} %bitcast.18), custom_call_target="tpu_custom_call" | custom-call | tf_op jit(solution)/shard_map/pallas_call | solution.py:144
  165.0 0.0 copy-done
  165.0 0.0 copy-done.2
  165.1 1.1 multiply_convert_fusion
  166.2 1.0 convolution_convert_fusion
  167.1 0.0 all-gather.5.cloned.1.call-update
  167.1 0.0 reduce-scatter.2.cloned.1.call-start
  167.2 87.5 %all-gather.5.cloned.1.call-done = bf16[8192,256]{1,0:T(8,128)(2,1)} async-done(((bf16[512,256]{1,0:T(8,128)(2,1)}), bf16[8192,256]{1,0:T(8,128)(2,1)}) %all-gather.5.cloned.1.call-update) | async-done | bytes 4194320 | tf_op jit(solution)/shard_map/all_gather | solution.py:267
  254.7 34.6 %shard_map.100 = bf16[32,128,256]{2,1,0:T(8,128)(2,1)} custom-call(s32[512]{0:T(512)} %bitcast.29, s32[512]{0:T(512)} %bitcast.27, s32[1]{0:T(128)} %bitcast.17.count_ref, bf16[512,128,128]{2,1,0:T(8,128)(2,1)} %bitcast.21, bf16[64,128,256]{2,1,0:T(8,128)(2,1)} %bitcast.23), custom_call_target="tpu_custom_call" | custom-call | flops 4294967296 | bytes 23068672 | tf_op jit(solution)/shard_map/pallas_call | solution.py:75
  289.3 0.0 reduce-scatter.2.cloned.1.call-update
  289.4 0.3 fusion
  289.6 82.6 %shard_map.96 = f32[16,256]{1,0:T(8,128)S(1)} custom-call(f32[16,16,256]{2,1,0:T(8,128)S(1)} %bitcast.19), custom_call_target="tpu_custom_call" | custom-call | tf_op jit(solution)/shard_map/pallas_call | solution.py:144
  372.3 6.4 %shard_map.97.x_ref = f32[2,256]{1,0:T(2,128)S(1)} custom-call(f32[8,2,256]{2,1,0:T(2,128)S(1)} %reshape.49.x_hbm), custom_call_target="tpu_custom_call" | custom-call | tf_op jit(solution)/shard_map/pallas_call | solution.py:144
  378.6 5.5 %shard_map.98 = f32[8,2,256]{2,1,0:T(2,128)S(1)} custom-call(f32[2,256]{1,0:T(2,128)S(1)} %shard_map.97.x_ref), custom_call_target="tpu_custom_call" | custom-call | tf_op jit(solution)/shard_map/pallas_call | solution.py:196
  384.1 9.6 %shard_map.99 = f32[16,16,256]{2,1,0:T(8,128)S(1)} custom-call(f32[16,256]{1,0:T(8,128)S(1)} %reshape.50.x_ref), custom_call_target="tpu_custom_call" | custom-call | tf_op jit(solution)/shard_map/pallas_call | solution.py:196
  393.7 0.7 broadcast_multiply_fusion
  394.4 1.7 reduce-scatter.2.cloned.1.call-done
  396.2 1.8 convert_element_type.19
  (2 shorter events, 0.0 us)
Async XLA Ops:
  7.2 157.9 %copy-start = (bf16[256,256]{1,0:T(8,128)(2,1)S(1)}, bf16[256,256]{1,0:T(8,128)(2,1)}, u32[]{:S(2)}) copy-start(bf16[256,256]{1,0:T(8,128)(2,1)} %param.12) | copy-start | bytes 393220
  7.2 30.4 %all-gather.3.cloned.1.call-start = ((), (), s32[]{:S(2)}) async-start(), calls=%async_computation.1 | async-start | bytes 2359296 | tf_op jit(solution)/shard_map/all_gather | solution.py:253
  7.9 246.8 %all-gather.5.cloned.1.call-start = ((), (), s32[]{:S(2)}) async-start(), calls=%async_computation.2 | async-start | bytes 4456448 | tf_op jit(solution)/shard_map/all_gather | solution.py:267
  67.3 2.2 copy-start.1
  69.5 95.5 %copy-start.2 = (bf16[512,256]{1,0:T(8,128)(2,1)S(1)}, bf16[512,256]{1,0:T(8,128)(2,1)}, u32[]{:S(2)}) copy-start(bf16[512,256]{1,0:T(8,128)(2,1)} %param.13) | copy-start | bytes 786436
  167.1 229.0 %reduce-scatter.2.cloned.1.call-start = ((), (), s32[]{:S(2)}) async-start(), calls=%async_computation.3 | async-start | bytes 2359296 | tf_op jit(solution)/shard_map/reduce_scatter | solution.py:276
Sparse Core Ops, SparseCore 0:
  9.7 27.8 all-gather.2
  167.3 87.4 all-gather.4
  289.5 106.6 reduce-scatter.1

commit v3 on v2

--- a/solution.py
+++ b/solution.py
@@ -9,6 +9,7 @@
 from jax.sharding import PartitionSpec as P
 
 SLOTS_PER_STEP = 32
+UNROLL = 32
 
 
 def spmm_kernel(transpose, acc_index, src_index, count_ref, tiles_ref, src_ref, out_ref, acc_ref):
@@ -24,24 +25,21 @@
 
     def one_slot(k, carry):
         slot = step * per_step + k
-
-        @pl.when(slot < live)
-        def _():
-            target = jnp.clip(acc_index[slot], 0, acc_last)
-            picked = jnp.clip(src_index[slot], 0, src_last)
-            tile = tiles_ref[k]
-            block = src_ref[picked]
-            if transpose:
-                product = lax.dot_general(
-                    tile, block, (((0,), (0,)), ((), ())), preferred_element_type=jnp.float32
-                )
-            else:
-                product = jnp.dot(tile, block, preferred_element_type=jnp.float32)
-            acc_ref[target] += product
-
+        target = jnp.clip(acc_index[slot], 0, acc_last)
+        picked = jnp.clip(src_index[slot], 0, src_last)
+        tile = tiles_ref[k]
+        tile = jnp.where(slot < live, tile, jnp.zeros_like(tile))
+        block = src_ref[picked]
+        if transpose:
+            product = lax.dot_general(
+                tile, block, (((0,), (0,)), ((), ())), preferred_element_type=jnp.float32
+            )
+        else:
+            product = jnp.dot(tile, block, preferred_element_type=jnp.float32)
+        acc_ref[target] += product
         return carry
 
-    lax.fori_loop(0, per_step, one_slot, 0)
+    lax.fori_loop(0, per_step, one_slot, 0, unroll=UNROLL)
 
     @pl.when(step == pl.num_programs(0) - 1)
     def _():

time: 405 us -> 253 us (0.62)
  Pallas kernels: 264 us -> 148 us
  waiting for transfers between devices: 119 us -> 83 us
    pallas_call x3, Pallas kernels: 184 us -> 95.3 us  [scatter_sum(): pl.pallas_call(functools.partial(scatter_sum_kernel, axis, other_axis, n)...]
    all_gather x1, waiting for transfers between devices: 87.5 us -> 51.4 us  [per_device(): row_block = lax.all_gather(own_grad, 'col', axis=0, tiled=True)]
    pallas_call x2, Pallas kernels: 64.4 us -> 37.4 us  [sparse_product(): pl.pallas_call(functools.partial(spmm_kernel, transpose), out_shape=jax.S...]
  transfers between devices with their start and end apart: 3 -> 3, of which waited for: 3 -> 3; matrix products, arithmetic and copies ran while one was open for 0% -> 0% of each run, Pallas kernels for 26% -> 13%
where the time goes in v3:
time: 253 us; the launch traced here: 252 us
  Pallas kernels  148 us (58%)
  waiting for transfers between devices  83 us (33%)
  between operations  14.5 us (6%)
    pallas_call x3, Pallas kernels, scatter_sum(): pl.pallas_call(functools.partial(scatter_sum_kernel, axis, other_axis, n)...  95.3 us
    all_gather x1, waiting for transfers between devices, per_device(): row_block = lax.all_gather(own_grad, 'col', axis=0, tiled=True)  51.4 us
    pallas_call x2, Pallas kernels, sparse_product(): pl.pallas_call(functools.partial(spmm_kernel, transpose), out_shape=jax.S...  37.4 us
    all_gather x1, waiting for transfers between devices, per_device(): column_block = lax.all_gather(features, 'row', axis=0, tiled=True)  29 us
    pallas_call x2, Pallas kernels, gather_all(): pl.pallas_call(functools.partial(gather_all_kernel, axis, other_axis, n),...  14.9 us
  transfers between devices with their start and end apart: 3, of which 3 were waited for; matrix products, arithmetic and copies ran while one was open for 0% of the time, Pallas kernels for 13%

profile of v3, /device:TPU:0, one launch (start us, length us, event | category | flops | bytes accessed | tf_op | source)
XLA Modules:
  0.0 252.3 jit_solution(16858036094255988191)
XLA Ops:
  7.2 0.0 copy-start
  7.2 0.0 all-gather.3.cloned.1.call-start
  7.2 0.7 all-gather.3.cloned.1.call-update
  7.9 0.0 all-gather.5.cloned.1.call-start
  8.6 29.0 %all-gather.3.cloned.1.call-done = bf16[4096,256]{1,0:T(8,128)(2,1)} async-done(((bf16[512,256]{1,0:T(8,128)(2,1)}), bf16[4096,256]{1,0:T(8,128)(2,1)}) %all-gather.3.cloned.1.call-update) | async-done | bytes 2097168 | tf_op jit(solution)/shard_map/all_gather | solution.py:251
  37.6 18.5 %shard_map.94 = bf16[64,128,256]{2,1,0:T(8,128)(2,1)} custom-call(s32[512]{0:T(512)} %bitcast.26, s32[512]{0:T(512)} %bitcast.28, s32[1]{0:T(128)} %bitcast.16.count_ref, bf16[512,128,128]{2,1,0:T(8,128)(2,1)} %bitcast.20, bf16[32,128,256]{2,1,0:T(8,128)(2,1)} %bitcast.24), custom_call_target="tpu_custom_call" | custom-call | flops 4294967296 | bytes 23068672 | tf_op jit(solution)/shard_map/pallas_call | solution.py:73
  56.2 0.0 copy-start.1
  56.2 2.2 copy-done.1
  58.3 0.0 copy-start.2
  58.3 77.1 %shard_map.95 = bf16[512,256]{1,0:T(8,128)(2,1)S(1)} custom-call(bf16[16,512,256]{2,1,0:T(8,128)(2,1)S(1)} %bitcast.18), custom_call_target="tpu_custom_call" | custom-call | tf_op jit(solution)/shard_map/pallas_call | solution.py:142
  135.5 0.0 copy-done
  135.5 0.0 copy-done.2
  135.5 1.1 multiply_convert_fusion
  136.6 1.0 convolution_convert_fusion
  137.6 0.0 all-gather.5.cloned.1.call-update
  137.6 0.0 reduce-scatter.2.cloned.1.call-start
  137.6 51.4 %all-gather.5.cloned.1.call-done = bf16[8192,256]{1,0:T(8,128)(2,1)} async-done(((bf16[512,256]{1,0:T(8,128)(2,1)}), bf16[8192,256]{1,0:T(8,128)(2,1)}) %all-gather.5.cloned.1.call-update) | async-done | bytes 4194320 | tf_op jit(solution)/shard_map/all_gather | solution.py:265
  189.0 18.8 %shard_map.100 = bf16[32,128,256]{2,1,0:T(8,128)(2,1)} custom-call(s32[512]{0:T(512)} %bitcast.29, s32[512]{0:T(512)} %bitcast.27, s32[1]{0:T(128)} %bitcast.17.count_ref, bf16[512,128,128]{2,1,0:T(8,128)(2,1)} %bitcast.21, bf16[64,128,256]{2,1,0:T(8,128)(2,1)} %bitcast.23), custom_call_target="tpu_custom_call" | custom-call | flops 4294967296 | bytes 23068672 | tf_op jit(solution)/shard_map/pallas_call | solution.py:73
  207.8 0.0 reduce-scatter.2.cloned.1.call-update
  207.8 0.3 fusion
  208.1 11.3 %shard_map.96 = f32[16,256]{1,0:T(8,128)S(1)} custom-call(f32[16,16,256]{2,1,0:T(8,128)S(1)} %bitcast.19), custom_call_target="tpu_custom_call" | custom-call | tf_op jit(solution)/shard_map/pallas_call | solution.py:142
  219.4 6.9 %shard_map.97.x_ref = f32[2,256]{1,0:T(2,128)S(1)} custom-call(f32[8,2,256]{2,1,0:T(2,128)S(1)} %reshape.49.x_hbm), custom_call_target="tpu_custom_call" | custom-call | tf_op jit(solution)/shard_map/pallas_call | solution.py:142
  226.4 5.5 %shard_map.98 = f32[8,2,256]{2,1,0:T(2,128)S(1)} custom-call(f32[2,256]{1,0:T(2,128)S(1)} %shard_map.97.x_ref), custom_call_target="tpu_custom_call" | custom-call | tf_op jit(solution)/shard_map/pallas_call | solution.py:194
  231.9 9.4 %shard_map.99 = f32[16,16,256]{2,1,0:T(8,128)S(1)} custom-call(f32[16,256]{1,0:T(8,128)S(1)} %reshape.50.x_ref), custom_call_target="tpu_custom_call" | custom-call | tf_op jit(solution)/shard_map/pallas_call | solution.py:194
  241.4 0.7 broadcast_multiply_fusion
  242.1 1.9 reduce-scatter.2.cloned.1.call-done
  243.9 1.8 convert_element_type.19
  (2 shorter events, 0.0 us)
Async XLA Ops:
  7.2 128.3 %copy-start = (bf16[256,256]{1,0:T(8,128)(2,1)S(1)}, bf16[256,256]{1,0:T(8,128)(2,1)}, u32[]{:S(2)}) copy-start(bf16[256,256]{1,0:T(8,128)(2,1)} %param.12) | copy-start | bytes 393220
  7.2 30.4 %all-gather.3.cloned.1.call-start = ((), (), s32[]{:S(2)}) async-start(), calls=%async_computation.1 | async-start | bytes 2359296 | tf_op jit(solution)/shard_map/all_gather | solution.py:251
  7.9 181.1 %all-gather.5.cloned.1.call-start = ((), (), s32[]{:S(2)}) async-start(), calls=%async_computation.2 | async-start | bytes 4456448 | tf_op jit(solution)/shard_map/all_gather | solution.py:265
  56.2 2.2 copy-start.1
  58.3 77.1 %copy-start.2 = (bf16[512,256]{1,0:T(8,128)(2,1)S(1)}, bf16[512,256]{1,0:T(8,128)(2,1)}, u32[]{:S(2)}) copy-start(bf16[512,256]{1,0:T(8,128)(2,1)} %param.13) | copy-start | bytes 786436
  137.6 106.4 %reduce-scatter.2.cloned.1.call-start = ((), (), s32[]{:S(2)}) async-start(), calls=%async_computation.3 | async-start | bytes 2359296 | tf_op jit(solution)/shard_map/reduce_scatter | solution.py:274
Sparse Core Ops, SparseCore 0:
  9.7 27.8 all-gather.2
  137.7 51.2 all-gather.4
  208.0 35.9 reduce-scatter.1

commit v4 on v3

--- a/solution.py
+++ b/solution.py
@@ -154,6 +154,9 @@
             collective_id=collective_id, has_side_effects=True,
             vmem_limit_bytes=48 * 1024 * 1024,
         ),
+        cost_estimate=pl.CostEstimate(
+            flops=x.size, transcendentals=0, bytes_accessed=3 * x.size * x.dtype.itemsize
+        ),
     )(x)
 
 
@@ -204,6 +207,9 @@
         compiler_params=pltpu.CompilerParams(
             collective_id=collective_id, has_side_effects=True,
             vmem_limit_bytes=48 * 1024 * 1024,
+        ),
+        cost_estimate=pl.CostEstimate(
+            flops=0, transcendentals=0, bytes_accessed=3 * n * x.size * x.dtype.itemsize
         ),
     )(x)
 
@@ -267,6 +273,7 @@
         aggregated, hidden_grad, (((0,), (0,)), ((), ())), preferred_element_type=jnp.float32
     )
     weight_grad = all_sum(local_grad, 1) * (1.0 / math.sqrt(node_total))
+    row_block, weight_grad = lax.optimization_barrier((row_block, weight_grad))
     source_back = row_block.reshape(row_tiles, tile_edge, feat_width)
     partial_cols = sparse_product(
         tile_block, col_index, row_index, live_count, source_back, col_tiles, True

time: 253 us -> 249 us (0.984)
  Pallas kernels: 148 us -> 144 us
    all_gather x1, waiting for transfers between devices: 51.4 us -> 17.1 us  [per_device(): row_block = lax.all_gather(own_grad, 'col', axis=0, tiled=True)]
    reduce_scatter x1, waiting for transfers between devices: 1.87 us -> 35.8 us  [per_device(): lax.psum_scatter(partial_cols.reshape(col_tiles * tile_edge, feat_width),...]
    pallas_call x3, Pallas kernels: 95.3 us -> 91.3 us  [scatter_sum(): pl.pallas_call(functools.partial(scatter_sum_kernel, axis, other_axis, n)...]
where the time goes in v4:
time: 249 us; the launch traced here: 248 us
  Pallas kernels  144 us (58%)
  waiting for transfers between devices  82.5 us (33%)
  between operations  14.5 us (6%)
  other arithmetic  2.5 us (1%)
    pallas_call x3, Pallas kernels, scatter_sum(): pl.pallas_call(functools.partial(scatter_sum_kernel, axis, other_axis, n)...  91.3 us
    pallas_call x2, Pallas kernels, sparse_product(): pl.pallas_call(functools.partial(spmm_kernel, transpose), out_shape=jax.S...  38 us
    reduce_scatter x1, waiting for transfers between devices, per_device(): lax.psum_scatter(partial_cols.reshape(col_tiles * tile_edge, feat_width),...  35.8 us
    all_gather x1, waiting for transfers between devices, per_device(): column_block = lax.all_gather(features, 'row', axis=0, tiled=True)  29 us
    all_gather x1, waiting for transfers between devices, per_device(): row_block = lax.all_gather(own_grad, 'col', axis=0, tiled=True)  17.1 us
    pallas_call x2, Pallas kernels, gather_all(): pl.pallas_call(functools.partial(gather_all_kernel, axis, other_axis, n),...  14.7 us
  transfers between devices with their start and end apart: 3, of which 3 were waited for; matrix products, arithmetic and copies ran while one was open for 0% of the time, Pallas kernels for 13%

profile of v4, /device:TPU:0, one launch (start us, length us, event | category | flops | bytes accessed | tf_op | source)
XLA Modules:
  0.0 248.2 jit_solution(2454441938015469571)
XLA Ops:
  7.2 0.0 copy-start
  7.2 0.0 all-gather.3.cloned.1.call-start
  7.2 0.7 all-gather.3.cloned.1.call-update
  7.9 0.0 all-gather.5.cloned.1.call-start
  8.6 29.0 %all-gather.3.cloned.1.call-done = bf16[4096,256]{1,0:T(8,128)(2,1)} async-done(((bf16[512,256]{1,0:T(8,128)(2,1)}), bf16[4096,256]{1,0:T(8,128)(2,1)}) %all-gather.3.cloned.1.call-update) | async-done | bytes 2097168 | tf_op jit(solution)/shard_map/all_gather | solution.py:257
  37.6 18.9 %shard_map.94 = bf16[64,128,256]{2,1,0:T(8,128)(2,1)} custom-call(s32[512]{0:T(512)} %bitcast.26, s32[512]{0:T(512)} %bitcast.28, s32[1]{0:T(128)} %bitcast.16.count_ref, bf16[512,128,128]{2,1,0:T(8,128)(2,1)} %bitcast.20, bf16[32,128,256]{2,1,0:T(8,128)(2,1)} %bitcast.24), custom_call_target="tpu_custom_call" | custom-call | flops 4294967296 | bytes 23068672 | tf_op jit(solution)/shard_map/pallas_call | solution.py:73
  56.5 0.0 copy-start.1
  56.5 2.2 copy-done.1
  58.7 0.0 copy-start.2
  58.7 74.5 %shard_map.95 = bf16[512,256]{1,0:T(8,128)(2,1)S(1)} custom-call(bf16[16,512,256]{2,1,0:T(8,128)(2,1)S(1)} %bitcast.18), custom_call_target="tpu_custom_call" | custom-call | flops 2097152 | bytes 12582912 | tf_op jit(solution)/shard_map/pallas_call | solution.py:142
  133.2 0.0 copy-done
  133.3 0.0 copy-done.2
  133.3 1.1 multiply_convert_fusion
  134.4 1.0 convolution_convert_fusion
  135.3 0.0 all-gather.5.cloned.1.call-update
  135.4 0.0 reduce-scatter.2.cloned.1.call-start
  135.4 0.3 fusion
  135.7 11.3 %shard_map.96 = f32[16,256]{1,0:T(8,128)S(1)} custom-call(f32[16,16,256]{2,1,0:T(8,128)S(1)} %bitcast.19), custom_call_target="tpu_custom_call" | custom-call | flops 65536 | bytes 786432 | tf_op jit(solution)/shard_map/pallas_call | solution.py:142
  147.0 5.5 %shard_map.97.x_ref = f32[2,256]{1,0:T(2,128)S(1)} custom-call(f32[8,2,256]{2,1,0:T(2,128)S(1)} %reshape.49.x_hbm), custom_call_target="tpu_custom_call" | custom-call | flops 4096 | bytes 49152 | tf_op jit(solution)/shard_map/pallas_call | solution.py:142
  152.5 5.4 %shard_map.98 = f32[8,2,256]{2,1,0:T(2,128)S(1)} custom-call(f32[2,256]{1,0:T(2,128)S(1)} %shard_map.97.x_ref), custom_call_target="tpu_custom_call" | custom-call | bytes 49152 | tf_op jit(solution)/shard_map/pallas_call | solution.py:197
  157.9 9.3 %shard_map.99 = f32[16,16,256]{2,1,0:T(8,128)S(1)} custom-call(f32[16,256]{1,0:T(8,128)S(1)} %reshape.50.x_ref), custom_call_target="tpu_custom_call" | custom-call | bytes 786432 | tf_op jit(solution)/shard_map/pallas_call | solution.py:197
  167.2 0.7 broadcast_multiply_fusion
  167.9 17.1 %all-gather.5.cloned.1.call-done = bf16[8192,256]{1,0:T(8,128)(2,1)} async-done(((bf16[512,256]{1,0:T(8,128)(2,1)}), bf16[8192,256]{1,0:T(8,128)(2,1)}) %all-gather.5.cloned.1.call-update) | async-done | bytes 4194320 | tf_op jit(solution)/shard_map/all_gather | solution.py:271
  185.0 19.1 %shard_map.100 = bf16[32,128,256]{2,1,0:T(8,128)(2,1)} custom-call(s32[512]{0:T(512)} %bitcast.29, s32[512]{0:T(512)} %bitcast.27, s32[1]{0:T(128)} %bitcast.17.count_ref, bf16[512,128,128]{2,1,0:T(8,128)(2,1)} %bitcast.21, bf16[64,128,256]{2,1,0:T(8,128)(2,1)} %bitcast.23), custom_call_target="tpu_custom_call" | custom-call | flops 4294967296 | bytes 23068672 | tf_op jit(solution)/shard_map/pallas_call | solution.py:73
  204.1 0.0 reduce-scatter.2.cloned.1.call-update
  204.1 35.8 %reduce-scatter.2.cloned.1.call-done = bf16[512,256]{1,0:T(8,128)(2,1)} async-done(((bf16[4096,256]{1,0:T(8,128)(2,1)}), bf16[512,256]{1,0:T(8,128)(2,1)}) %reduce-scatter.2.cloned.1.call-update) | async-done | bytes 262160 | tf_op jit(solution)/shard_map/reduce_scatter | solution.py:281
  239.9 1.8 convert_element_type.19
  (2 shorter events, 0.0 us)
Async XLA Ops:
  7.2 126.1 %copy-start = (bf16[256,256]{1,0:T(8,128)(2,1)S(1)}, bf16[256,256]{1,0:T(8,128)(2,1)}, u32[]{:S(2)}) copy-start(bf16[256,256]{1,0:T(8,128)(2,1)} %param.12) | copy-start | bytes 393220
  7.2 30.4 %all-gather.3.cloned.1.call-start = ((), (), s32[]{:S(2)}) async-start(), calls=%async_computation.1 | async-start | bytes 2359296 | tf_op jit(solution)/shard_map/all_gather | solution.py:257
  7.9 177.1 %all-gather.5.cloned.1.call-start = ((), (), s32[]{:S(2)}) async-start(), calls=%async_computation.2 | async-start | bytes 4456448 | tf_op jit(solution)/shard_map/all_gather | solution.py:271
  56.5 2.2 copy-start.1
  58.7 74.5 %copy-start.2 = (bf16[512,256]{1,0:T(8,128)(2,1)S(1)}, bf16[512,256]{1,0:T(8,128)(2,1)}, u32[]{:S(2)}) copy-start(bf16[512,256]{1,0:T(8,128)(2,1)} %param.13) | copy-start | bytes 786436
  135.4 104.5 %reduce-scatter.2.cloned.1.call-start = ((), (), s32[]{:S(2)}) async-start(), calls=%async_computation.3 | async-start | bytes 2359296 | tf_op jit(solution)/shard_map/reduce_scatter | solution.py:281
Sparse Core Ops, SparseCore 0:
  9.7 27.8 all-gather.2
  135.5 49.4 all-gather.4
  204.3 35.5 reduce-scatter.1

commit v5 on v4

--- a/solution.py
+++ b/solution.py
@@ -10,6 +10,7 @@
 
 SLOTS_PER_STEP = 32
 UNROLL = 32
+TORUS_X = 4
 
 
 def spmm_kernel(transpose, acc_index, src_index, count_ref, tiles_ref, src_ref, out_ref, acc_ref):
@@ -212,6 +213,152 @@
             flops=0, transcendentals=0, bytes_accessed=3 * n * x.size * x.dtype.itemsize
         ),
     )(x)
+
+
+def torus_peer(y, x, nx):
+    return (lax.axis_index("row"), y * nx + x)
+
+
+def scatter_sum_2d_kernel(nx, ny, x_hbm, out_ref, recv1, mid, recv2, sems):
+    send1, got1, send2, got2, own_sems = sems
+    me = lax.axis_index("col")
+    my_y = me // nx
+    my_x = lax.rem(me, nx)
+    half = x_hbm.shape[2] // 2
+    lower = pl.ds(0, half)
+    upper = pl.ds(half, half)
+    mesh_kind = pl.DeviceIdType.MESH
+
+    barrier = pltpu.get_barrier_semaphore()
+    for offset in range(1, nx):
+        pl.semaphore_signal(barrier, 1, device_id=torus_peer(my_y, lax.rem(my_x + offset, nx), nx),
+                            device_id_type=mesh_kind)
+    for offset in range(1, ny):
+        pl.semaphore_signal(barrier, 1, device_id=torus_peer(lax.rem(my_y + offset, ny), my_x, nx),
+                            device_id_type=mesh_kind)
+    pl.semaphore_wait(barrier, nx + ny - 2)
+
+    own_a = pltpu.make_async_copy(x_hbm.at[:, my_x, lower], recv1.at[0, my_x], own_sems.at[0])
+    own_b = pltpu.make_async_copy(x_hbm.at[my_y, :, upper], recv1.at[1, my_y], own_sems.at[1])
+    own_a.start()
+    own_b.start()
+    sends = []
+    for offset in range(1, nx):
+        peer_x = lax.rem(my_x + offset, nx)
+        copy = pltpu.make_async_remote_copy(
+            src_ref=x_hbm.at[:, peer_x, lower], dst_ref=recv1.at[0, my_x],
+            send_sem=send1.at[0, offset], recv_sem=got1.at[0, my_x],
+            device_id=torus_peer(my_y, peer_x, nx), device_id_type=mesh_kind,
+        )
+        copy.start()
+        sends.append(copy)
+    for offset in range(1, ny):
+        peer_y = lax.rem(my_y + offset, ny)
+        copy = pltpu.make_async_remote_copy(
+            src_ref=x_hbm.at[peer_y, :, upper], dst_ref=recv1.at[1, my_y],
+            send_sem=send1.at[1, offset], recv_sem=got1.at[1, my_y],
+            device_id=torus_peer(peer_y, my_x, nx), device_id_type=mesh_kind,
+        )
+        copy.start()
+        sends.append(copy)
+    own_a.wait()
+    own_b.wait()
+    for offset in range(1, nx):
+        source_x = lax.rem(my_x + nx - offset, nx)
+        pltpu.make_async_remote_copy(
+            src_ref=x_hbm.at[:, source_x, lower], dst_ref=recv1.at[0, source_x],
+            send_sem=send1.at[0, offset], recv_sem=got1.at[0, source_x],
+            device_id=torus_peer(my_y, source_x, nx), device_id_type=mesh_kind,
+        ).wait_recv()
+    for offset in range(1, ny):
+        source_y = lax.rem(my_y + ny - offset, ny)
+        pltpu.make_async_remote_copy(
+            src_ref=x_hbm.at[source_y, :, upper], dst_ref=recv1.at[1, source_y],
+            send_sem=send1.at[1, offset], recv_sem=got1.at[1, source_y],
+            device_id=torus_peer(source_y, my_x, nx), device_id_type=mesh_kind,
+        ).wait_recv()
+
+    def add_up(stack):
+        total = stack[0].astype(jnp.float32)
+        for j in range(1, stack.shape[0]):
+            total = total + stack[j].astype(jnp.float32)
+        return total
+
+    for target in range(ny):
+        mid[0, target] = add_up(recv1[0, :, target]).astype(mid.dtype)
+    for target in range(nx):
+        mid[1, target] = add_up(recv1[1, :, target]).astype(mid.dtype)
+    recv2[0, my_y] = mid[0, my_y]
+    recv2[1, my_x] = mid[1, my_x]
+
+    for offset in range(1, ny):
+        peer_y = lax.rem(my_y + offset, ny)
+        copy = pltpu.make_async_remote_copy(
+            src_ref=mid.at[0, peer_y], dst_ref=recv2.at[0, my_y],
+            send_sem=send2.at[0, offset], recv_sem=got2.at[0, my_y],
+            device_id=torus_peer(peer_y, my_x, nx), device_id_type=mesh_kind,
+        )
+        copy.start()
+        sends.append(copy)
+    for offset in range(1, nx):
+        peer_x = lax.rem(my_x + offset, nx)
+        copy = pltpu.make_async_remote_copy(
+            src_ref=mid.at[1, peer_x], dst_ref=recv2.at[1, my_x],
+            send_sem=send2.at[1, offset], recv_sem=got2.at[1, my_x],
+            device_id=torus_peer(my_y, peer_x, nx), device_id_type=mesh_kind,
+        )
+        copy.start()
+        sends.append(copy)
+    for offset in range(1, ny):
+        source_y = lax.rem(my_y + ny - offset, ny)
+        pltpu.make_async_remote_copy(
+            src_ref=mid.at[0, source_y], dst_ref=recv2.at[0, source_y],
+            send_sem=send2.at[0, offset], recv_sem=got2.at[0, source_y],
+            device_id=torus_peer(source_y, my_x, nx), device_id_type=mesh_kind,
+        ).wait_recv()
+    for offset in range(1, nx):
+        source_x = lax.rem(my_x + nx - offset, nx)
+        pltpu.make_async_remote_copy(
+            src_ref=mid.at[1, source_x], dst_ref=recv2.at[1, source_x],
+            send_sem=send2.at[1, offset], recv_sem=got2.at[1, source_x],
+            device_id=torus_peer(my_y, source_x, nx), device_id_type=mesh_kind,
+        ).wait_recv()
+    out_ref[lower] = add_up(recv2[0]).astype(out_ref.dtype)
+    out_ref[upper] = add_up(recv2[1]).astype(out_ref.dtype)
+    for copy in sends:
+        copy.wait_send()
+
+
+def scatter_sum_2d(x, nx, out_dtype, collective_id):
+    n, rows, lanes = x.shape
+    ny = n // nx
+    half = rows // 2
+    side = max(nx, ny)
+    return pl.pallas_call(
+        functools.partial(scatter_sum_2d_kernel, nx, ny),
+        out_shape=jax.ShapeDtypeStruct((rows, lanes), out_dtype),
+        in_specs=[pl.BlockSpec(memory_space=pl.ANY)],
+        out_specs=pl.BlockSpec(memory_space=pltpu.VMEM),
+        scratch_shapes=[
+            pltpu.VMEM((2, side, side, half, lanes), x.dtype),
+            pltpu.VMEM((2, side, half, lanes), x.dtype),
+            pltpu.VMEM((2, side, half, lanes), x.dtype),
+            (
+                pltpu.SemaphoreType.DMA((2, side)),
+                pltpu.SemaphoreType.DMA((2, side)),
+                pltpu.SemaphoreType.DMA((2, side)),
+                pltpu.SemaphoreType.DMA((2, side)),
+                pltpu.SemaphoreType.DMA((2,)),
+            ),
+        ],
+        compiler_params=pltpu.CompilerParams(
+            collective_id=collective_id, has_side_effects=True,
+            vmem_limit_bytes=48 * 1024 * 1024,
+        ),
+        cost_estimate=pl.CostEstimate(
+            flops=x.size, transcendentals=0, bytes_accessed=3 * x.size * x.dtype.itemsize
+        ),
+    )(x.reshape(ny, nx, rows, lanes))
 
 
 def all_sum(local, collective_base):
@@ -261,8 +408,8 @@
     )
     partial_flat = partial_rows.reshape(row_tiles * tile_edge, feat_width)
     node_total = row_count * col_count * own_rows
-    aggregated = scatter_sum(
-        partial_rows.reshape(col_count, own_rows, feat_width), "col", "row", jnp.bfloat16, 0
+    aggregated = scatter_sum_2d(
+        partial_rows.reshape(col_count, own_rows, feat_width), TORUS_X, jnp.bfloat16, 0
     )
     output, hidden_grad = activation(aggregated, weight, cotangent)
     own_grad = lax.dot_general(

time: 249 us -> 215 us (0.86)
  Pallas kernels: 144 us -> 107 us
  waiting for transfers between devices: 82.5 us -> 85.7 us
    pallas_call x3 -> x2, Pallas kernels: 91.3 us -> 15.8 us  [scatter_sum(): pl.pallas_call(functools.partial(scatter_sum_kernel, axis, other_axis, n)...]
    pallas_call x0 -> x1, Pallas kernels: none -> 39.2 us  [scatter_sum_2d(): pl.pallas_call(functools.partial(scatter_sum_2d_kernel, nx, ny), out_shap...]
  transfers between devices with their start and end apart: 3 -> 3, of which waited for: 3 -> 3; matrix products, arithmetic and copies ran while one was open for 0% -> 0% of each run, Pallas kernels for 13% -> 15%
where the time goes in v5:
time: 215 us; the launch traced here: 214 us
  Pallas kernels  107 us (50%)
  waiting for transfers between devices  85.7 us (40%)
  between operations  14.5 us (7%)
  other arithmetic  2.5 us (1%)
  matrix products  2.34 us (1%)
  local copies, waits for them, and re-layouts  2.23 us (1%)
    pallas_call x1, Pallas kernels, scatter_sum_2d(): pl.pallas_call(functools.partial(scatter_sum_2d_kernel, nx, ny), out_shap...  39.2 us
    reduce_scatter x1, waiting for transfers between devices, per_device(): lax.psum_scatter(partial_cols.reshape(col_tiles * tile_edge, feat_width),...  36.5 us
    pallas_call x2, Pallas kernels, sparse_product(): pl.pallas_call(functools.partial(spmm_kernel, transpose), out_shape=jax.S...  36.2 us
    all_gather x1, waiting for transfers between devices, per_device(): column_block = lax.all_gather(features, 'row', axis=0, tiled=True)  29 us
    all_gather x1, waiting for transfers between devices, per_device(): row_block = lax.all_gather(own_grad, 'col', axis=0, tiled=True)  19.5 us
    pallas_call x2, Pallas kernels, scatter_sum(): pl.pallas_call(functools.partial(scatter_sum_kernel, axis, other_axis, n)...  15.8 us
    pallas_call x2, Pallas kernels, gather_all(): pl.pallas_call(functools.partial(gather_all_kernel, axis, other_axis, n),...  15.5 us
  transfers between devices with their start and end apart: 3, of which 3 were waited for; matrix products, arithmetic and copies ran while one was open for 0% of the time, Pallas kernels for 15%

profile of v5, /device:TPU:0, one launch (start us, length us, event | category | flops | bytes accessed | tf_op | source)
XLA Modules:
  0.0 214.0 jit_solution(544249191648569242)
XLA Ops:
  7.2 0.0 copy-start
  7.2 0.0 all-gather.3.cloned.1.call-start
  7.2 0.7 all-gather.3.cloned.1.call-update
  7.9 0.0 all-gather.5.cloned.1.call-start
  8.6 29.0 %all-gather.3.cloned.1.call-done = bf16[4096,256]{1,0:T(8,128)(2,1)} async-done(((bf16[512,256]{1,0:T(8,128)(2,1)}), bf16[4096,256]{1,0:T(8,128)(2,1)}) %all-gather.3.cloned.1.call-update) | async-done | bytes 2097168 | tf_op jit(solution)/shard_map/all_gather | solution.py:404
  37.6 18.0 %shard_map.94 = bf16[64,128,256]{2,1,0:T(8,128)(2,1)} custom-call(s32[512]{0:T(512)} %bitcast.26, s32[512]{0:T(512)} %bitcast.28, s32[1]{0:T(128)} %bitcast.16.count_ref, bf16[512,128,128]{2,1,0:T(8,128)(2,1)} %bitcast.20, bf16[32,128,256]{2,1,0:T(8,128)(2,1)} %bitcast.24), custom_call_target="tpu_custom_call" | custom-call | flops 4294967296 | bytes 23068672 | tf_op jit(solution)/shard_map/pallas_call | solution.py:74
  55.6 0.0 copy-start.1
  55.6 2.2 %copy-done.1 = bf16[64,128,256]{2,1,0:T(8,128)(2,1)S(1)} copy-done((bf16[64,128,256]{2,1,0:T(8,128)(2,1)S(1)}, bf16[64,128,256]{2,1,0:T(8,128)(2,1)}, u32[]{:S(2)}) %copy-start.1) | copy-done | bytes 4194328
  57.8 0.0 copy-start.2
  57.8 39.2 %shard_map.95 = bf16[512,256]{1,0:T(8,128)(2,1)S(1)} custom-call(bf16[4,4,512,256]{3,2,1,0:T(8,128)(2,1)S(1)} %bitcast.18), custom_call_target="tpu_custom_call" | custom-call | flops 2097152 | bytes 12582912 | tf_op jit(solution)/shard_map/pallas_call | solution.py:337
  97.0 0.0 copy-done
  97.0 0.0 copy-done.2
  97.0 1.1 multiply_convert_fusion
  98.1 1.0 convolution_convert_fusion
  99.1 0.0 all-gather.5.cloned.1.call-update
  99.1 0.0 reduce-scatter.2.cloned.1.call-start
  99.1 0.3 fusion
  99.4 8.7 %shard_map.96 = f32[16,256]{1,0:T(8,128)S(1)} custom-call(f32[16,16,256]{2,1,0:T(8,128)S(1)} %bitcast.19), custom_call_target="tpu_custom_call" | custom-call | flops 65536 | bytes 786432 | tf_op jit(solution)/shard_map/pallas_call | solution.py:143
  108.2 7.0 %shard_map.97.x_ref = f32[2,256]{1,0:T(2,128)S(1)} custom-call(f32[8,2,256]{2,1,0:T(2,128)S(1)} %reshape.45.x_hbm), custom_call_target="tpu_custom_call" | custom-call | flops 4096 | bytes 49152 | tf_op jit(solution)/shard_map/pallas_call | solution.py:143
  115.2 6.1 %shard_map.98 = f32[8,2,256]{2,1,0:T(2,128)S(1)} custom-call(f32[2,256]{1,0:T(2,128)S(1)} %shard_map.97.x_ref), custom_call_target="tpu_custom_call" | custom-call | bytes 49152 | tf_op jit(solution)/shard_map/pallas_call | solution.py:198
  121.3 9.4 %shard_map.99 = f32[16,16,256]{2,1,0:T(8,128)S(1)} custom-call(f32[16,256]{1,0:T(8,128)S(1)} %reshape.46.x_ref), custom_call_target="tpu_custom_call" | custom-call | bytes 786432 | tf_op jit(solution)/shard_map/pallas_call | solution.py:198
  130.7 0.7 broadcast_multiply_fusion
  131.4 19.5 %all-gather.5.cloned.1.call-done = bf16[8192,256]{1,0:T(8,128)(2,1)} async-done(((bf16[512,256]{1,0:T(8,128)(2,1)}), bf16[8192,256]{1,0:T(8,128)(2,1)}) %all-gather.5.cloned.1.call-update) | async-done | bytes 4194320 | tf_op jit(solution)/shard_map/all_gather | solution.py:418
  150.9 18.2 %shard_map.100 = bf16[32,128,256]{2,1,0:T(8,128)(2,1)} custom-call(s32[512]{0:T(512)} %bitcast.29, s32[512]{0:T(512)} %bitcast.27, s32[1]{0:T(128)} %bitcast.17.count_ref, bf16[512,128,128]{2,1,0:T(8,128)(2,1)} %bitcast.21, bf16[64,128,256]{2,1,0:T(8,128)(2,1)} %bitcast.23), custom_call_target="tpu_custom_call" | custom-call | flops 4294967296 | bytes 23068672 | tf_op jit(solution)/shard_map/pallas_call | solution.py:74
  169.2 0.0 reduce-scatter.2.cloned.1.call-update
  169.2 36.5 %reduce-scatter.2.cloned.1.call-done = bf16[512,256]{1,0:T(8,128)(2,1)} async-done(((bf16[4096,256]{1,0:T(8,128)(2,1)}), bf16[512,256]{1,0:T(8,128)(2,1)}) %reduce-scatter.2.cloned.1.call-update) | async-done | bytes 262160 | tf_op jit(solution)/shard_map/reduce_scatter | solution.py:428
  205.7 1.8 convert_element_type.19
  (2 shorter events, 0.0 us)
Async XLA Ops:
  7.2 89.8 %copy-start = (bf16[256,256]{1,0:T(8,128)(2,1)S(1)}, bf16[256,256]{1,0:T(8,128)(2,1)}, u32[]{:S(2)}) copy-start(bf16[256,256]{1,0:T(8,128)(2,1)} %param.12) | copy-start | bytes 393220
  7.2 30.4 %all-gather.3.cloned.1.call-start = ((), (), s32[]{:S(2)}) async-start(), calls=%async_computation.1 | async-start | bytes 2359296 | tf_op jit(solution)/shard_map/all_gather | solution.py:404
  7.9 143.0 %all-gather.5.cloned.1.call-start = ((), (), s32[]{:S(2)}) async-start(), calls=%async_computation.2 | async-start | bytes 4456448 | tf_op jit(solution)/shard_map/all_gather | solution.py:418
  55.6 2.2 %copy-start.1 = (bf16[64,128,256]{2,1,0:T(8,128)(2,1)S(1)}, bf16[64,128,256]{2,1,0:T(8,128)(2,1)}, u32[]{:S(2)}) copy-start(bf16[64,128,256]{2,1,0:T(8,128)(2,1)} %shard_map.94) | copy-start | bytes 12582916
  57.8 39.2 %copy-start.2 = (bf16[512,256]{1,0:T(8,128)(2,1)S(1)}, bf16[512,256]{1,0:T(8,128)(2,1)}, u32[]{:S(2)}) copy-start(bf16[512,256]{1,0:T(8,128)(2,1)} %param.13) | copy-start | bytes 786436
  99.1 106.6 %reduce-scatter.2.cloned.1.call-start = ((), (), s32[]{:S(2)}) async-start(), calls=%async_computation.3 | async-start | bytes 2359296 | tf_op jit(solution)/shard_map/reduce_scatter | solution.py:428
Sparse Core Ops, SparseCore 0:
  9.7 27.8 all-gather.2
  99.2 51.6 all-gather.4
  169.3 36.2 reduce-scatter.1

commit v6 on v5

--- a/solution.py
+++ b/solution.py
@@ -361,6 +361,170 @@
     )(x.reshape(ny, nx, rows, lanes))
 
 
+def row_peer(index):
+    return (index, lax.axis_index("col"))
+
+
+def greet_row(my_z, my_core, nz):
+    barrier = pltpu.get_barrier_semaphore()
+    mesh_kind = pl.DeviceIdType.MESH
+    pl.semaphore_signal(barrier, 1, device_id=row_peer(my_z * 2 + 1 - my_core), device_id_type=mesh_kind)
+    for offset in range(1, nz):
+        peer_z = lax.rem(my_z + offset, nz)
+        pl.semaphore_signal(barrier, 1, device_id=row_peer(peer_z * 2 + my_core), device_id_type=mesh_kind)
+    pl.semaphore_wait(barrier, nz)
+
+
+def scatter_sum_row_kernel(nz, x_hbm, out_ref, own1, recv1, mid, recv2, sems):
+    send1, got1, send2, got2, own_sem = sems
+    mesh_kind = pl.DeviceIdType.MESH
+    me = lax.axis_index("row")
+    my_z = me // 2
+    my_core = lax.rem(me, 2)
+    other_core = 1 - my_core
+    greet_row(my_z, my_core, nz)
+    own = pltpu.make_async_copy(x_hbm.at[:, my_core], own1, own_sem.at[0])
+    own.start()
+    first = pltpu.make_async_remote_copy(
+        src_ref=x_hbm.at[:, other_core], dst_ref=recv1,
+        send_sem=send1.at[0], recv_sem=got1.at[0],
+        device_id=row_peer(my_z * 2 + other_core), device_id_type=mesh_kind,
+    )
+    first.start()
+    own.wait()
+    first.wait_recv()
+    for target in range(nz):
+        mid[target] = (own1[target].astype(jnp.float32) + recv1[target].astype(jnp.float32)).astype(mid.dtype)
+    sends = []
+    for offset in range(1, nz):
+        peer_z = lax.rem(my_z + offset, nz)
+        copy = pltpu.make_async_remote_copy(
+            src_ref=mid.at[peer_z], dst_ref=recv2.at[my_z],
+            send_sem=send2.at[offset], recv_sem=got2.at[my_z],
+            device_id=row_peer(peer_z * 2 + my_core), device_id_type=mesh_kind,
+        )
+        copy.start()
+        sends.append(copy)
+    total = mid[my_z].astype(jnp.float32)
+    for offset in range(1, nz):
+        source_z = lax.rem(my_z + nz - offset, nz)
+        pltpu.make_async_remote_copy(
+            src_ref=mid.at[source_z], dst_ref=recv2.at[source_z],
+            send_sem=send2.at[offset], recv_sem=got2.at[source_z],
+            device_id=row_peer(source_z * 2 + my_core), device_id_type=mesh_kind,
+        ).wait_recv()
+        total = total + recv2[source_z].astype(jnp.float32)
+    out_ref[...] = total.astype(out_ref.dtype)
+    first.wait_send()
+    for copy in sends:
+        copy.wait_send()
+
+
+def scatter_sum_row(x, out_dtype, collective_id):
+    n, rows, lanes = x.shape
+    nz = n // 2
+    return pl.pallas_call(
+        functools.partial(scatter_sum_row_kernel, nz),
+        out_shape=jax.ShapeDtypeStruct((rows, lanes), out_dtype),
+        in_specs=[pl.BlockSpec(memory_space=pl.ANY)],
+        out_specs=pl.BlockSpec(memory_space=pltpu.VMEM),
+        scratch_shapes=[
+            pltpu.VMEM((nz, rows, lanes), x.dtype),
+            pltpu.VMEM((nz, rows, lanes), x.dtype),
+            pltpu.VMEM((nz, rows, lanes), x.dtype),
+            pltpu.VMEM((nz, rows, lanes), x.dtype),
+            (
+                pltpu.SemaphoreType.DMA((1,)),
+                pltpu.SemaphoreType.DMA((1,)),
+                pltpu.SemaphoreType.DMA((nz,)),
+                pltpu.SemaphoreType.DMA((nz,)),
+                pltpu.SemaphoreType.DMA((1,)),
+            ),
+        ],
+        compiler_params=pltpu.CompilerParams(
+            collective_id=collective_id, has_side_effects=True,
+            vmem_limit_bytes=48 * 1024 * 1024,
+        ),
+        cost_estimate=pl.CostEstimate(
+            flops=x.size, transcendentals=0, bytes_accessed=3 * x.size * x.dtype.itemsize
+        ),
+    )(x.reshape(nz, 2, rows, lanes))
+
+
+def gather_row_kernel(nz, x_ref, out_ref, full, sems):
+    send1, got1, send2, got2, own_sem = sems
+    mesh_kind = pl.DeviceIdType.MESH
+    me = lax.axis_index("row")
+    my_z = me // 2
+    my_core = lax.rem(me, 2)
+    other_core = 1 - my_core
+    greet_row(my_z, my_core, nz)
+    own = pltpu.make_async_copy(x_ref, full.at[my_z, my_core], own_sem.at[0])
+    own.start()
+    sends = []
+    for offset in range(1, nz):
+        peer_z = lax.rem(my_z + offset, nz)
+        copy = pltpu.make_async_remote_copy(
+            src_ref=x_ref, dst_ref=full.at[my_z, my_core],
+            send_sem=send1.at[offset], recv_sem=got1.at[my_z],
+            device_id=row_peer(peer_z * 2 + my_core), device_id_type=mesh_kind,
+        )
+        copy.start()
+        sends.append(copy)
+    own.wait()
+    for offset in range(1, nz):
+        source_z = lax.rem(my_z + nz - offset, nz)
+        pltpu.make_async_remote_copy(
+            src_ref=x_ref, dst_ref=full.at[source_z, my_core],
+            send_sem=send1.at[offset], recv_sem=got1.at[source_z],
+            device_id=row_peer(source_z * 2 + my_core), device_id_type=mesh_kind,
+        ).wait_recv()
+    second = pltpu.make_async_remote_copy(
+        src_ref=full.at[:, my_core], dst_ref=full.at[:, my_core],
+        send_sem=send2.at[0], recv_sem=got2.at[0],
+        device_id=row_peer(my_z * 2 + other_core), device_id_type=mesh_kind,
+    )
+    second.start()
+    pltpu.make_async_remote_copy(
+        src_ref=full.at[:, other_core], dst_ref=full.at[:, other_core],
+        send_sem=send2.at[0], recv_sem=got2.at[0],
+        device_id=row_peer(my_z * 2 + other_core), device_id_type=mesh_kind,
+    ).wait_recv()
+    for copy in sends:
+        copy.wait_send()
+    second.wait_send()
+    out_ref[...] = full[...]
+
+
+def gather_row(x, collective_id):
+    rows, lanes = x.shape
+    nz = lax.axis_size("row") // 2
+    out = pl.pallas_call(
+        functools.partial(gather_row_kernel, nz),
+        out_shape=jax.ShapeDtypeStruct((nz, 2, rows, lanes), x.dtype),
+        in_specs=[pl.BlockSpec(memory_space=pltpu.VMEM)],
+        out_specs=pl.BlockSpec(memory_space=pltpu.VMEM),
+        scratch_shapes=[
+            pltpu.VMEM((nz, 2, rows, lanes), x.dtype),
+            (
+                pltpu.SemaphoreType.DMA((nz,)),
+                pltpu.SemaphoreType.DMA((nz,)),
+                pltpu.SemaphoreType.DMA((1,)),
+                pltpu.SemaphoreType.DMA((1,)),
+                pltpu.SemaphoreType.DMA((1,)),
+            ),
+        ],
+        compiler_params=pltpu.CompilerParams(
+            collective_id=collective_id, has_side_effects=True,
+            vmem_limit_bytes=48 * 1024 * 1024,
+        ),
+        cost_estimate=pl.CostEstimate(
+            flops=0, transcendentals=0, bytes_accessed=3 * 2 * nz * x.size * x.dtype.itemsize
+        ),
+    )(x)
+    return out.reshape(2 * nz * rows, lanes)
+
+
 def all_sum(local, collective_base):
     row_count = lax.axis_size("row")
     col_count = lax.axis_size("col")
@@ -401,7 +565,7 @@
     col_count = lax.axis_size("col")
     row_tiles = col_count * own_rows // tile_edge
     col_tiles = row_count * own_rows // tile_edge
-    column_block = lax.all_gather(features, "row", axis=0, tiled=True)
+    column_block = gather_row(features, 8)
     source = column_block.reshape(col_tiles, tile_edge, feat_width)
     partial_rows = sparse_product(
         tile_block, row_index, col_index, live_count, source, row_tiles, False
@@ -425,12 +589,9 @@
     partial_cols = sparse_product(
         tile_block, col_index, row_index, live_count, source_back, col_tiles, True
     )
-    input_grad = lax.psum_scatter(
-        partial_cols.reshape(col_tiles * tile_edge, feat_width),
-        "row",
-        scatter_dimension=0,
-        tiled=True,
-    ).astype(jnp.float32)
+    input_grad = scatter_sum_row(
+        partial_cols.reshape(row_count, own_rows, feat_width), jnp.float32, 9
+    )
     return (output, weight_grad, input_grad)
 
 

time: 215 us -> 193 us (0.90)
  waiting for transfers between devices: 85.7 us -> 19.7 us
  Pallas kernels: 107 us -> 148 us
  local copies, waits for them, and re-layouts: 2.23 us -> 6.87 us
    pallas_call x0 -> x2, Pallas kernels: none -> 41.1 us  [the longest x1 21.3 us: scatter_sum_row(): pl.pallas_call(functools.partial(scatter_sum_row_kernel, nz), out_shape=j...]
    reduce_scatter x1 -> x0, waiting for transfers between devices: 36.5 us -> none  [per_device(): lax.psum_scatter(partial_cols.reshape(col_tiles * tile_edge, feat_width),...]
    all_gather x1 -> x0, waiting for transfers between devices: 29 us -> none  [per_device(): column_block = lax.all_gather(features, 'row', axis=0, tiled=True)]
    unnamed x6 -> x13, local copies, waits for them, and re-layouts: 2.2 us -> 6.84 us
    pallas_call x1, Pallas kernels: 39.2 us -> 41.4 us  [scatter_sum_2d(): pl.pallas_call(functools.partial(scatter_sum_2d_kernel, nx, ny), out_shap...]
  transfers between devices with their start and end apart: 3 -> 1, of which waited for: 3 -> 1; matrix products, arithmetic and copies ran while one was open for 0% -> 1% of each run, Pallas kernels for 15% -> 15%
where the time goes in v6:
time: 193 us; the launch traced here: 192 us
  Pallas kernels  148 us (77%)
  waiting for transfers between devices  19.7 us (10%)
  between operations  14.8 us (8%)
  local copies, waits for them, and re-layouts  6.87 us (4%)
  matrix products  2.34 us (1%)
    pallas_call x1, Pallas kernels, scatter_sum_2d(): pl.pallas_call(functools.partial(scatter_sum_2d_kernel, nx, ny), out_shap...  41.4 us
    pallas_call x2, Pallas kernels, sparse_product(): pl.pallas_call(functools.partial(spmm_kernel, transpose), out_shape=jax.S...  36.3 us
    pallas_call x1, Pallas kernels, scatter_sum_row(): pl.pallas_call(functools.partial(scatter_sum_row_kernel, nz), out_shape=j...  21.3 us
    pallas_call x1, Pallas kernels, gather_row(): pl.pallas_call(functools.partial(gather_row_kernel, nz), out_shape=jax.Sh...  19.8 us
    all_gather x1, waiting for transfers between devices, per_device(): row_block = lax.all_gather(own_grad, 'col', axis=0, tiled=True)  19.6 us
    pallas_call x2, Pallas kernels, gather_all(): pl.pallas_call(functools.partial(gather_all_kernel, axis, other_axis, n),...  14.7 us
    pallas_call x2, Pallas kernels, scatter_sum(): pl.pallas_call(functools.partial(scatter_sum_kernel, axis, other_axis, n)...  14.1 us
    unnamed x13, local copies, waits for them, and re-layouts  6.84 us
  transfers between devices with their start and end apart: 1, of which 1 were waited for; matrix products, arithmetic and copies ran while one was open for 1% of the time, Pallas kernels for 15%

profile of v6, /device:TPU:0, one launch (start us, length us, event | category | flops | bytes accessed | tf_op | source)
XLA Modules:
  0.0 192.1 jit_solution(4295043507445825589)
XLA Ops:
  7.2 0.0 copy-start
  7.2 0.0 all-gather.2.cloned.1.call-start
  7.9 0.0 copy-start.4
  7.9 0.9 copy-done.4
  8.9 19.8 %shard_map.94 = bf16[4,2,512,256]{3,2,1,0:T(8,128)(2,1)S(1)} custom-call(bf16[512,256]{1,0:T(8,128)(2,1)S(1)} %copy-done.4), custom_call_target="tpu_custom_call" | custom-call | bytes 6291456 | tf_op jit(solution)/shard_map/pallas_call | solution.py:502
  28.6 0.0 copy-start.3
  28.6 1.3 copy-done.3
  29.9 18.0 %shard_map.95 = bf16[64,128,256]{2,1,0:T(8,128)(2,1)} custom-call(s32[512]{0:T(512)} %bitcast.26, s32[512]{0:T(512)} %bitcast.28, s32[1]{0:T(128)} %bitcast.16.count_ref, bf16[512,128,128]{2,1,0:T(8,128)(2,1)} %bitcast.22, bf16[32,128,256]{2,1,0:T(8,128)(2,1)} %bitcast.20), custom_call_target="tpu_custom_call" | custom-call | flops 4294967296 | bytes 23068672 | tf_op jit(solution)/shard_map/pallas_call | solution.py:74
  47.9 0.0 copy-start.1
  47.9 2.2 %copy-done.1 = bf16[64,128,256]{2,1,0:T(8,128)(2,1)S(1)} copy-done((bf16[64,128,256]{2,1,0:T(8,128)(2,1)S(1)}, bf16[64,128,256]{2,1,0:T(8,128)(2,1)}, u32[]{:S(2)}) %copy-start.1) | copy-done | bytes 4194328
  50.1 0.0 copy-start.5
  50.1 41.4 %shard_map.96 = bf16[512,256]{1,0:T(8,128)(2,1)S(1)} custom-call(bf16[4,4,512,256]{3,2,1,0:T(8,128)(2,1)S(1)} %bitcast.18), custom_call_target="tpu_custom_call" | custom-call | flops 2097152 | bytes 12582912 | tf_op jit(solution)/shard_map/pallas_call | solution.py:337
  91.6 0.0 copy-done
  91.6 0.0 copy-done.5
  91.6 1.1 multiply_convert_fusion
  92.7 1.0 convolution_convert_fusion
  93.7 0.0 all-gather.2.cloned.1.call-update
  93.7 0.3 fusion
  94.0 8.7 %shard_map.97 = f32[16,256]{1,0:T(8,128)S(1)} custom-call(f32[16,16,256]{2,1,0:T(8,128)S(1)} %bitcast.21), custom_call_target="tpu_custom_call" | custom-call | flops 65536 | bytes 786432 | tf_op jit(solution)/shard_map/pallas_call | solution.py:143
  102.7 5.4 %shard_map.98.x_ref = f32[2,256]{1,0:T(2,128)S(1)} custom-call(f32[8,2,256]{2,1,0:T(2,128)S(1)} %reshape.38.x_hbm), custom_call_target="tpu_custom_call" | custom-call | flops 4096 | bytes 49152 | tf_op jit(solution)/shard_map/pallas_call | solution.py:143
  108.1 5.4 %shard_map.99 = f32[8,2,256]{2,1,0:T(2,128)S(1)} custom-call(f32[2,256]{1,0:T(2,128)S(1)} %shard_map.98.x_ref), custom_call_target="tpu_custom_call" | custom-call | bytes 49152 | tf_op jit(solution)/shard_map/pallas_call | solution.py:198
  113.6 9.3 %shard_map.100 = f32[16,16,256]{2,1,0:T(8,128)S(1)} custom-call(f32[16,256]{1,0:T(8,128)S(1)} %reshape.39.x_ref), custom_call_target="tpu_custom_call" | custom-call | bytes 786432 | tf_op jit(solution)/shard_map/pallas_call | solution.py:198
  122.9 0.7 broadcast_multiply_fusion
  123.6 19.6 %all-gather.2.cloned.1.call-done = bf16[8192,256]{1,0:T(8,128)(2,1)} async-done(((bf16[512,256]{1,0:T(8,128)(2,1)}), bf16[8192,256]{1,0:T(8,128)(2,1)}) %all-gather.2.cloned.1.call-update) | async-done | bytes 4194320 | tf_op jit(solution)/shard_map/all_gather | solution.py:582
  143.2 18.3 %shard_map.101 = bf16[32,128,256]{2,1,0:T(8,128)(2,1)} custom-call(s32[512]{0:T(512)} %bitcast.29, s32[512]{0:T(512)} %bitcast.27, s32[1]{0:T(128)} %bitcast.17.count_ref, bf16[512,128,128]{2,1,0:T(8,128)(2,1)} %bitcast.23, bf16[64,128,256]{2,1,0:T(8,128)(2,1)} %bitcast.24), custom_call_target="tpu_custom_call" | custom-call | flops 4294967296 | bytes 23068672 | tf_op jit(solution)/shard_map/pallas_call | solution.py:74
  161.5 0.0 copy-start.2
  161.5 1.6 copy-done.2
  163.1 21.3 %shard_map.102 = f32[512,256]{1,0:T(8,128)S(1)} custom-call(bf16[4,2,512,256]{3,2,1,0:T(8,128)(2,1)S(1)} %bitcast.19), custom_call_target="tpu_custom_call" | custom-call | flops 1048576 | bytes 6291456 | tf_op jit(solution)/shard_map/pallas_call | solution.py:426
  184.4 0.8 copy.12
  (2 shorter events, 0.0 us)
Async XLA Ops:
  7.2 84.4 %copy-start = (bf16[256,256]{1,0:T(8,128)(2,1)S(1)}, bf16[256,256]{1,0:T(8,128)(2,1)}, u32[]{:S(2)}) copy-start(bf16[256,256]{1,0:T(8,128)(2,1)} %param.12) | copy-start | bytes 393220
  7.2 136.0 %all-gather.2.cloned.1.call-start = ((), (), s32[]{:S(2)}) async-start(), calls=%async_computation | async-start | bytes 4456448 | tf_op jit(solution)/shard_map/all_gather | solution.py:582
  7.9 1.0 copy-start.4
  28.6 1.3 copy-start.3
  47.9 2.2 %copy-start.1 = (bf16[64,128,256]{2,1,0:T(8,128)(2,1)S(1)}, bf16[64,128,256]{2,1,0:T(8,128)(2,1)}, u32[]{:S(2)}) copy-start(bf16[64,128,256]{2,1,0:T(8,128)(2,1)} %shard_map.95) | copy-start | bytes 12582916
  50.1 41.5 %copy-start.5 = (bf16[512,256]{1,0:T(8,128)(2,1)S(1)}, bf16[512,256]{1,0:T(8,128)(2,1)}, u32[]{:S(2)}) copy-start(bf16[512,256]{1,0:T(8,128)(2,1)} %param.13) | copy-start | bytes 786436
  161.5 1.6 copy-start.2
Sparse Core Ops, SparseCore 0:
  93.8 49.3 all-gather.1

commit v7 on v6

--- a/solution.py
+++ b/solution.py
@@ -525,6 +525,127 @@
     return out.reshape(2 * nz * rows, lanes)
 
 
+def gather_all_2d_kernel(nx, ny, x_ref, out_ref, full, sems):
+    send, got, own_sem = sems
+    mesh_kind = pl.DeviceIdType.MESH
+    me = lax.axis_index("col")
+    my_y = me // nx
+    my_x = lax.rem(me, nx)
+    half = x_ref.shape[0] // 2
+    lower = pl.ds(0, half)
+    upper = pl.ds(half, half)
+
+    barrier = pltpu.get_barrier_semaphore()
+    for offset in range(1, nx):
+        pl.semaphore_signal(barrier, 1, device_id=torus_peer(my_y, lax.rem(my_x + offset, nx), nx),
+                            device_id_type=mesh_kind)
+    for offset in range(1, ny):
+        pl.semaphore_signal(barrier, 1, device_id=torus_peer(lax.rem(my_y + offset, ny), my_x, nx),
+                            device_id_type=mesh_kind)
+    pl.semaphore_wait(barrier, nx + ny - 2)
+
+    own = pltpu.make_async_copy(x_ref, full.at[my_y, my_x], own_sem.at[0])
+    own.start()
+    sends = []
+    for offset in range(1, nx):
+        peer_x = lax.rem(my_x + offset, nx)
+        copy = pltpu.make_async_remote_copy(
+            src_ref=x_ref.at[lower], dst_ref=full.at[my_y, my_x, lower],
+            send_sem=send.at[0, offset], recv_sem=got.at[0, my_x],
+            device_id=torus_peer(my_y, peer_x, nx), device_id_type=mesh_kind,
+        )
+        copy.start()
+        sends.append(copy)
+    for offset in range(1, ny):
+        peer_y = lax.rem(my_y + offset, ny)
+        copy = pltpu.make_async_remote_copy(
+            src_ref=x_ref.at[upper], dst_ref=full.at[my_y, my_x, upper],
+            send_sem=send.at[1, offset], recv_sem=got.at[1, my_y],
+            device_id=torus_peer(peer_y, my_x, nx), device_id_type=mesh_kind,
+        )
+        copy.start()
+        sends.append(copy)
+    own.wait()
+    for offset in range(1, nx):
+        source_x = lax.rem(my_x + nx - offset, nx)
+        pltpu.make_async_remote_copy(
+            src_ref=x_ref.at[lower], dst_ref=full.at[my_y, source_x, lower],
+            send_sem=send.at[0, offset], recv_sem=got.at[0, source_x],
+            device_id=torus_peer(my_y, source_x, nx), device_id_type=mesh_kind,
+        ).wait_recv()
+    for offset in range(1, ny):
+        peer_y = lax.rem(my_y + offset, ny)
+        copy = pltpu.make_async_remote_copy(
+            src_ref=full.at[my_y, :, lower], dst_ref=full.at[my_y, :, lower],
+            send_sem=send.at[2, offset], recv_sem=got.at[2, my_y],
+            device_id=torus_peer(peer_y, my_x, nx), device_id_type=mesh_kind,
+        )
+        copy.start()
+        sends.append(copy)
+    for offset in range(1, ny):
+        source_y = lax.rem(my_y + ny - offset, ny)
+        pltpu.make_async_remote_copy(
+            src_ref=x_ref.at[upper], dst_ref=full.at[source_y, my_x, upper],
+            send_sem=send.at[1, offset], recv_sem=got.at[1, source_y],
+            device_id=torus_peer(source_y, my_x, nx), device_id_type=mesh_kind,
+        ).wait_recv()
+    for offset in range(1, nx):
+        peer_x = lax.rem(my_x + offset, nx)
+        copy = pltpu.make_async_remote_copy(
+            src_ref=full.at[:, my_x, upper], dst_ref=full.at[:, my_x, upper],
+            send_sem=send.at[3, offset], recv_sem=got.at[3, my_x],
+            device_id=torus_peer(my_y, peer_x, nx), device_id_type=mesh_kind,
+        )
+        copy.start()
+        sends.append(copy)
+    for offset in range(1, ny):
+        source_y = lax.rem(my_y + ny - offset, ny)
+        pltpu.make_async_remote_copy(
+            src_ref=full.at[source_y, :, lower], dst_ref=full.at[source_y, :, lower],
+            send_sem=send.at[2, offset], recv_sem=got.at[2, source_y],
+            device_id=torus_peer(source_y, my_x, nx), device_id_type=mesh_kind,
+        ).wait_recv()
+    for offset in range(1, nx):
+        source_x = lax.rem(my_x + nx - offset, nx)
+        pltpu.make_async_remote_copy(
+            src_ref=full.at[:, source_x, upper], dst_ref=full.at[:, source_x, upper],
+            send_sem=send.at[3, offset], recv_sem=got.at[3, source_x],
+            device_id=torus_peer(my_y, source_x, nx), device_id_type=mesh_kind,
+        ).wait_recv()
+    for copy in sends:
+        copy.wait_send()
+    out_ref[...] = full[...]
+
+
+def gather_all_2d(x, nx, collective_id):
+    rows, lanes = x.shape
+    n = lax.axis_size("col")
+    ny = n // nx
+    side = max(nx, ny)
+    out = pl.pallas_call(
+        functools.partial(gather_all_2d_kernel, nx, ny),
+        out_shape=jax.ShapeDtypeStruct((ny, nx, rows, lanes), x.dtype),
+        in_specs=[pl.BlockSpec(memory_space=pltpu.VMEM)],
+        out_specs=pl.BlockSpec(memory_space=pltpu.VMEM),
+        scratch_shapes=[
+            pltpu.VMEM((ny, nx, rows, lanes), x.dtype),
+            (
+                pltpu.SemaphoreType.DMA((4, side)),
+                pltpu.SemaphoreType.DMA((4, side)),
+                pltpu.SemaphoreType.DMA((1,)),
+            ),
+        ],
+        compiler_params=pltpu.CompilerParams(
+            collective_id=collective_id, has_side_effects=True,
+            vmem_limit_bytes=48 * 1024 * 1024,
+        ),
+        cost_estimate=pl.CostEstimate(
+            flops=0, transcendentals=0, bytes_accessed=3 * n * x.size * x.dtype.itemsize
+        ),
+    )(x)
+    return out.reshape(n, rows, lanes)
+
+
 def all_sum(local, collective_base):
     row_count = lax.axis_size("row")
     col_count = lax.axis_size("col")
@@ -579,12 +700,11 @@
     own_grad = lax.dot_general(
         hidden_grad, weight, (((1,), (1,)), ((), ())), preferred_element_type=jnp.float32
     ).astype(jnp.bfloat16)
-    row_block = lax.all_gather(own_grad, "col", axis=0, tiled=True)
+    row_block = gather_all_2d(own_grad, TORUS_X, 7)
     local_grad = lax.dot_general(
         aggregated, hidden_grad, (((0,), (0,)), ((), ())), preferred_element_type=jnp.float32
     )
-    weight_grad = all_sum(local_grad, 1) * (1.0 / math.sqrt(node_total))
-    row_block, weight_grad = lax.optimization_barrier((row_block, weight_grad))
+    weight_grad = lax.psum(local_grad, ("row", "col")) * (1.0 / math.sqrt(node_total))
     source_back = row_block.reshape(row_tiles, tile_edge, feat_width)
     partial_cols = sparse_product(
         tile_block, col_index, row_index, live_count, source_back, col_tiles, True

time: 193 us -> 259 us (1.34)
  waiting for transfers between devices: 19.7 us -> 77.3 us
  Pallas kernels: 148 us -> 153 us
    psum x0 -> x1, waiting for transfers between devices: none -> 77.3 us  [per_device(): lax.psum(local_grad, ('row', 'col')) * (1.0 / math.sqrt(node_total))]
    all_gather x1 -> x0, waiting for transfers between devices: 19.6 us -> none  [per_device(): row_block = lax.all_gather(own_grad, 'col', axis=0, tiled=True)]
    pallas_call x4 -> x1, Pallas kernels: 28.8 us -> 34.9 us  [gather_all_2d(): pl.pallas_call(functools.partial(gather_all_2d_kernel, nx, ny), out_shape...]
    unnamed x13 -> x15, local copies, waits for them, and re-layouts: 6.84 us -> 8.77 us
  transfers between devices with their start and end apart: 1 -> 1, of which waited for: 1 -> 1; matrix products, arithmetic and copies ran while one was open for 1% -> 0% of each run, Pallas kernels for 15% -> 29%
where the time goes in v7:
time: 259 us; the launch traced here: 258 us
  Pallas kernels  153 us (59%)
  waiting for transfers between devices  77.3 us (30%)
  between operations  14.8 us (6%)
  local copies, waits for them, and re-layouts  8.77 us (3%)
    psum x1, waiting for transfers between devices, per_device(): lax.psum(local_grad, ('row', 'col')) * (1.0 / math.sqrt(node_total))  77.3 us
    pallas_call x1, Pallas kernels, scatter_sum_2d(): pl.pallas_call(functools.partial(scatter_sum_2d_kernel, nx, ny), out_shap...  40.9 us
    pallas_call x2, Pallas kernels, sparse_product(): pl.pallas_call(functools.partial(spmm_kernel, transpose), out_shape=jax.S...  37.4 us
    pallas_call x1, Pallas kernels, gather_all_2d(): pl.pallas_call(functools.partial(gather_all_2d_kernel, nx, ny), out_shape...  34.9 us
    pallas_call x1, Pallas kernels, gather_row(): pl.pallas_call(functools.partial(gather_row_kernel, nz), out_shape=jax.Sh...  19.8 us
    pallas_call x1, Pallas kernels, scatter_sum_row(): pl.pallas_call(functools.partial(scatter_sum_row_kernel, nz), out_shape=j...  19.7 us
    unnamed x15, local copies, waits for them, and re-layouts  8.77 us
  transfers between devices with their start and end apart: 1, of which 1 were waited for; matrix products, arithmetic and copies ran while one was open for 0% of the time, Pallas kernels for 29%

profile of v7, /device:TPU:0, one launch (start us, length us, event | category | flops | bytes accessed | tf_op | source)
XLA Modules:
  0.0 257.5 jit_solution(1568059534502355041)
XLA Ops:
  7.2 0.0 copy-start
  7.2 0.0 all-reduce.2.cloned.1.call-start
  7.9 0.0 copy-start.5
  7.9 0.9 copy-done.5
  8.9 19.8 %shard_map.94 = bf16[4,2,512,256]{3,2,1,0:T(8,128)(2,1)S(1)} custom-call(bf16[512,256]{1,0:T(8,128)(2,1)S(1)} %copy-done.5), custom_call_target="tpu_custom_call" | custom-call | bytes 6291456 | tf_op jit(solution)/shard_map/pallas_call | solution.py:502
  28.6 0.0 copy-start.4
  28.6 1.3 copy-done.4
  29.9 18.5 %shard_map.95 = bf16[64,128,256]{2,1,0:T(8,128)(2,1)} custom-call(s32[512]{0:T(512)} %bitcast.22, s32[512]{0:T(512)} %bitcast.24, s32[1]{0:T(128)} %bitcast.14.count_ref, bf16[512,128,128]{2,1,0:T(8,128)(2,1)} %bitcast.20, bf16[32,128,256]{2,1,0:T(8,128)(2,1)} %bitcast.19), custom_call_target="tpu_custom_call" | custom-call | flops 4294967296 | bytes 23068672 | tf_op jit(solution)/shard_map/pallas_call | solution.py:74
  48.5 0.0 copy-start.2
  48.5 2.2 copy-done.2
  50.7 0.0 copy-start.6
  50.7 40.9 %shard_map.96 = bf16[512,256]{1,0:T(8,128)(2,1)S(1)} custom-call(bf16[4,4,512,256]{3,2,1,0:T(8,128)(2,1)S(1)} %bitcast.17), custom_call_target="tpu_custom_call" | custom-call | flops 2097152 | bytes 12582912 | tf_op jit(solution)/shard_map/pallas_call | solution.py:337
  91.5 0.0 copy-done
  91.6 0.0 copy-done.6
  91.6 1.1 multiply_convert_fusion
  92.7 1.0 fusion
  93.6 0.0 all-reduce.2.cloned.1.call-update
  93.7 0.3 convolution_convert_fusion.x_ref
  93.9 34.9 %shard_map.97 = bf16[4,4,512,256]{3,2,1,0:T(8,128)(2,1)S(1)} custom-call(bf16[512,256]{1,0:T(8,128)(2,1)S(1)} %convolution_convert_fusion.x_ref), custom_call_target="tpu_custom_call" | custom-call | bytes 12582912 | tf_op jit(solution)/shard_map/pallas_call | solution.py:625
  128.9 0.0 copy-start.1
  128.9 1.9 copy-done.1
  130.8 18.8 %shard_map.98 = bf16[32,128,256]{2,1,0:T(8,128)(2,1)} custom-call(s32[512]{0:T(512)} %bitcast.25, s32[512]{0:T(512)} %bitcast.23, s32[1]{0:T(128)} %bitcast.15.count_ref, bf16[512,128,128]{2,1,0:T(8,128)(2,1)} %bitcast.21, bf16[64,128,256]{2,1,0:T(8,128)(2,1)} %bitcast.16), custom_call_target="tpu_custom_call" | custom-call | flops 4294967296 | bytes 23068672 | tf_op jit(solution)/shard_map/pallas_call | solution.py:74
  149.7 0.0 copy-start.3
  149.7 1.6 copy-done.3
  151.2 19.7 %shard_map.99 = f32[512,256]{1,0:T(8,128)S(1)} custom-call(bf16[4,2,512,256]{3,2,1,0:T(8,128)(2,1)S(1)} %bitcast.18), custom_call_target="tpu_custom_call" | custom-call | flops 1048576 | bytes 6291456 | tf_op jit(solution)/shard_map/pallas_call | solution.py:426
  171.0 77.3 %all-reduce.2.cloned.1.call-done = f32[256,256]{1,0:T(8,128)} async-done(((f32[256,256]{1,0:T(8,128)}), f32[256,256]{1,0:T(8,128)}) %all-reduce.2.cloned.1.call-update) | async-done | bytes 262160 | tf_op jit(solution)/shard_map/psum | solution.py:707
  248.2 1.7 broadcast_multiply_fusion
  249.9 0.8 copy.13
Async XLA Ops:
  7.2 84.4 %copy-start = (bf16[256,256]{1,0:T(8,128)(2,1)S(1)}, bf16[256,256]{1,0:T(8,128)(2,1)}, u32[]{:S(2)}) copy-start(bf16[256,256]{1,0:T(8,128)(2,1)} %param.12) | copy-start | bytes 393220
  7.2 241.1 %all-reduce.2.cloned.1.call-start = ((), (), s32[]{:S(2)}) async-start(), calls=%async_computation | async-start | bytes 524288 | tf_op jit(solution)/shard_map/psum | solution.py:707
  7.9 1.0 copy-start.5
  28.6 1.3 copy-start.4
  48.5 2.2 copy-start.2
  50.7 40.9 %copy-start.6 = (bf16[512,256]{1,0:T(8,128)(2,1)S(1)}, bf16[512,256]{1,0:T(8,128)(2,1)}, u32[]{:S(2)}) copy-start(bf16[512,256]{1,0:T(8,128)(2,1)} %param.13) | copy-start | bytes 786436
  128.9 1.9 copy-start.1
  149.7 1.6 copy-start.3
Sparse Core Ops, SparseCore 0:
  93.8 154.4 all-reduce.1

commit v8 on v7

--- a/solution.py
+++ b/solution.py
@@ -704,7 +704,7 @@
     local_grad = lax.dot_general(
         aggregated, hidden_grad, (((0,), (0,)), ((), ())), preferred_element_type=jnp.float32
     )
-    weight_grad = lax.psum(local_grad, ("row", "col")) * (1.0 / math.sqrt(node_total))
+    weight_grad = lax.psum(lax.psum(local_grad, "row"), "col") * (1.0 / math.sqrt(node_total))
     source_back = row_block.reshape(row_tiles, tile_edge, feat_width)
     partial_cols = sparse_product(
         tile_block, col_index, row_index, live_count, source_back, col_tiles, True

time: 259 us -> 248 us (0.958)
  waiting for transfers between devices: 77.3 us -> 70.1 us
  Pallas kernels: 153 us -> 150 us
    psum x1 -> x2, waiting for transfers between devices: 77.3 us -> 70 us  [the longest x1 49.5 us: per_device(): lax.psum(lax.psum(local_grad, 'row'), 'col') * (1.0 / math.sqrt(node_total))]
    pallas_call x1, Pallas kernels: 19.7 us -> 17 us  [scatter_sum_row(): pl.pallas_call(functools.partial(scatter_sum_row_kernel, nz), out_shape=j...]
  transfers between devices with their start and end apart: 1 -> 2, of which waited for: 1 -> 2; matrix products, arithmetic and copies ran while one was open for 0% -> 0% of each run, Pallas kernels for 29% -> 29%
where the time goes in v8:
time: 248 us; the launch traced here: 247 us
  Pallas kernels  150 us (60%)
  waiting for transfers between devices  70.1 us (28%)
  between operations  14.8 us (6%)
  local copies, waits for them, and re-layouts  8.77 us (4%)
    psum x1, waiting for transfers between devices, per_device(): lax.psum(lax.psum(local_grad, 'row'), 'col') * (1.0 / math.sqrt(node_total))  49.5 us
    pallas_call x1, Pallas kernels, scatter_sum_2d(): pl.pallas_call(functools.partial(scatter_sum_2d_kernel, nx, ny), out_shap...  41.2 us
    pallas_call x2, Pallas kernels, sparse_product(): pl.pallas_call(functools.partial(spmm_kernel, transpose), out_shape=jax.S...  36.3 us
    pallas_call x1, Pallas kernels, gather_all_2d(): pl.pallas_call(functools.partial(gather_all_2d_kernel, nx, ny), out_shape...  35.4 us
    psum x1, waiting for transfers between devices, per_device(): lax.psum(local_grad, 'row')  20.5 us
    pallas_call x1, Pallas kernels, gather_row(): pl.pallas_call(functools.partial(gather_row_kernel, nz), out_shape=jax.Sh...  19.8 us
    pallas_call x1, Pallas kernels, scatter_sum_row(): pl.pallas_call(functools.partial(scatter_sum_row_kernel, nz), out_shape=j...  17 us
    unnamed x15, local copies, waits for them, and re-layouts  8.77 us
  transfers between devices with their start and end apart: 2, of which 2 were waited for; matrix products, arithmetic and copies ran while one was open for 0% of the time, Pallas kernels for 29%

profile of v8, /device:TPU:0, one launch (start us, length us, event | category | flops | bytes accessed | tf_op | source)
XLA Modules:
  0.0 247.4 jit_solution(13071219266420246122)
XLA Ops:
  7.2 0.0 copy-start
  7.2 0.0 all-reduce.3.cloned.1.call-start
  7.9 0.0 copy-start.5
  7.9 0.9 copy-done.5
  8.9 19.8 %shard_map.94 = bf16[4,2,512,256]{3,2,1,0:T(8,128)(2,1)S(1)} custom-call(bf16[512,256]{1,0:T(8,128)(2,1)S(1)} %copy-done.5), custom_call_target="tpu_custom_call" | custom-call | bytes 6291456 | tf_op jit(solution)/shard_map/pallas_call | solution.py:502
  28.6 0.0 copy-start.4
  28.6 1.3 copy-done.4
  29.9 18.0 %shard_map.95 = bf16[64,128,256]{2,1,0:T(8,128)(2,1)} custom-call(s32[512]{0:T(512)} %bitcast.22, s32[512]{0:T(512)} %bitcast.24, s32[1]{0:T(128)} %bitcast.14.count_ref, bf16[512,128,128]{2,1,0:T(8,128)(2,1)} %bitcast.20, bf16[32,128,256]{2,1,0:T(8,128)(2,1)} %bitcast.19), custom_call_target="tpu_custom_call" | custom-call | flops 4294967296 | bytes 23068672 | tf_op jit(solution)/shard_map/pallas_call | solution.py:74
  47.9 0.0 copy-start.2
  47.9 2.2 copy-done.2
  50.1 0.0 copy-start.6
  50.1 41.2 %shard_map.96 = bf16[512,256]{1,0:T(8,128)(2,1)S(1)} custom-call(bf16[4,4,512,256]{3,2,1,0:T(8,128)(2,1)S(1)} %bitcast.17), custom_call_target="tpu_custom_call" | custom-call | flops 2097152 | bytes 12582912 | tf_op jit(solution)/shard_map/pallas_call | solution.py:337
  91.3 0.0 copy-done
  91.3 0.0 copy-done.6
  91.4 1.1 multiply_convert_fusion
  92.5 1.0 fusion
  93.4 0.0 all-reduce.3.cloned.1.call-update
  93.5 0.0 all-reduce.5.cloned.1.call-start
  93.5 0.3 convolution_convert_fusion.x_ref
  93.8 35.4 %shard_map.97 = bf16[4,4,512,256]{3,2,1,0:T(8,128)(2,1)S(1)} custom-call(bf16[512,256]{1,0:T(8,128)(2,1)S(1)} %convolution_convert_fusion.x_ref), custom_call_target="tpu_custom_call" | custom-call | bytes 12582912 | tf_op jit(solution)/shard_map/pallas_call | solution.py:625
  129.1 0.0 copy-start.1
  129.2 1.9 copy-done.1
  131.1 20.5 %all-reduce.3.cloned.1.call-done = f32[256,256]{1,0:T(8,128)} async-done(((f32[256,256]{1,0:T(8,128)}), f32[256,256]{1,0:T(8,128)}) %all-reduce.3.cloned.1.call-update) | async-done | bytes 262160 | tf_op jit(solution)/shard_map/psum | solution.py:707
  151.6 0.0 all-reduce.5.cloned.1.call-update
  151.6 18.3 %shard_map.98 = bf16[32,128,256]{2,1,0:T(8,128)(2,1)} custom-call(s32[512]{0:T(512)} %bitcast.25, s32[512]{0:T(512)} %bitcast.23, s32[1]{0:T(128)} %bitcast.15.count_ref, bf16[512,128,128]{2,1,0:T(8,128)(2,1)} %bitcast.21, bf16[64,128,256]{2,1,0:T(8,128)(2,1)} %bitcast.16), custom_call_target="tpu_custom_call" | custom-call | flops 4294967296 | bytes 23068672 | tf_op jit(solution)/shard_map/pallas_call | solution.py:74
  169.9 0.0 copy-start.3
  169.9 1.6 copy-done.3
  171.5 17.0 %shard_map.99 = f32[512,256]{1,0:T(8,128)S(1)} custom-call(bf16[4,2,512,256]{3,2,1,0:T(8,128)(2,1)S(1)} %bitcast.18), custom_call_target="tpu_custom_call" | custom-call | flops 1048576 | bytes 6291456 | tf_op jit(solution)/shard_map/pallas_call | solution.py:426
  188.5 49.5 %all-reduce.5.cloned.1.call-done = f32[256,256]{1,0:T(8,128)} async-done(((f32[256,256]{1,0:T(8,128)}), f32[256,256]{1,0:T(8,128)}) %all-reduce.5.cloned.1.call-update) | async-done | bytes 262160 | tf_op jit(solution)/shard_map/psum | solution.py:707
  238.1 1.7 broadcast_multiply_fusion
  239.7 0.8 copy.14
Async XLA Ops:
  7.2 84.2 %copy-start = (bf16[256,256]{1,0:T(8,128)(2,1)S(1)}, bf16[256,256]{1,0:T(8,128)(2,1)}, u32[]{:S(2)}) copy-start(bf16[256,256]{1,0:T(8,128)(2,1)} %param.12) | copy-start | bytes 393220
  7.2 144.4 %all-reduce.3.cloned.1.call-start = ((), (), s32[]{:S(2)}) async-start(), calls=%async_computation | async-start | bytes 524288 | tf_op jit(solution)/shard_map/psum | solution.py:707
  7.9 1.0 copy-start.5
  28.6 1.3 copy-start.4
  47.9 2.2 copy-start.2
  50.1 41.2 %copy-start.6 = (bf16[512,256]{1,0:T(8,128)(2,1)S(1)}, bf16[512,256]{1,0:T(8,128)(2,1)}, u32[]{:S(2)}) copy-start(bf16[512,256]{1,0:T(8,128)(2,1)} %param.13) | copy-start | bytes 786436
  93.5 144.6 %all-reduce.5.cloned.1.call-start = ((), (), s32[]{:S(2)}) async-start(), calls=%async_computation.1 | async-start | bytes 524288 | tf_op jit(solution)/shard_map/psum | solution.py:707
  129.1 1.9 copy-start.1
  169.9 1.6 copy-start.3
Sparse Core Ops, SparseCore 0:
  93.6 57.9 all-reduce.2
  155.1 82.9 all-reduce.4

commit v9 on v8

--- a/solution.py
+++ b/solution.py
@@ -646,6 +646,93 @@
     return out.reshape(n, rows, lanes)
 
 
+def fused_sum_kernel(nr, nc, x_ref, out_ref, recv1, recv2, recv3, sems):
+    send1, got1, send2, got2, send3, got3 = sems
+    mesh_kind = pl.DeviceIdType.MESH
+    my_r = lax.axis_index("row")
+    my_c = lax.axis_index("col")
+    barrier = pltpu.get_barrier_semaphore()
+    for offset in range(1, nc):
+        pl.semaphore_signal(barrier, 1, device_id=(my_r, lax.rem(my_c + offset, nc)),
+                            device_id_type=mesh_kind)
+    for offset in range(1, nr):
+        pl.semaphore_signal(barrier, 1, device_id=(lax.rem(my_r + offset, nr), my_c),
+                            device_id_type=mesh_kind)
+    pl.semaphore_wait(barrier, nc + nr - 2)
+
+    def exchange(peers, axis_count, src_of, dst, send, got, me_index):
+        started = []
+        for offset in range(1, axis_count):
+            peer = lax.rem(me_index + offset, axis_count)
+            copy = pltpu.make_async_remote_copy(
+                src_ref=src_of(peer), dst_ref=dst.at[me_index],
+                send_sem=send.at[offset], recv_sem=got.at[me_index],
+                device_id=peers(peer), device_id_type=mesh_kind,
+            )
+            copy.start()
+            started.append(copy)
+        for offset in range(1, axis_count):
+            source = lax.rem(me_index + axis_count - offset, axis_count)
+            pltpu.make_async_remote_copy(
+                src_ref=src_of(source), dst_ref=dst.at[source],
+                send_sem=send.at[offset], recv_sem=got.at[source],
+                device_id=peers(source), device_id_type=mesh_kind,
+            ).wait_recv()
+        return started
+
+    along_col = lambda peer: (my_r, peer)
+    along_row = lambda peer: (peer, my_c)
+    recv1[my_c] = x_ref[my_c]
+    sends = exchange(along_col, nc, lambda peer: x_ref.at[peer], recv1, send1, got1, my_c)
+    part = recv1[0]
+    for j in range(1, nc):
+        part = part + recv1[j]
+    recv2[my_r] = part
+    sends += exchange(along_row, nr, lambda peer: recv2.at[my_r], recv2, send2, got2, my_r)
+    total = recv2[0]
+    for j in range(1, nr):
+        total = total + recv2[j]
+    recv3[my_c] = total
+    sends += exchange(along_col, nc, lambda peer: recv3.at[my_c], recv3, send3, got3, my_c)
+    out_ref[...] = recv3[...]
+    for copy in sends:
+        copy.wait_send()
+
+
+def fused_sum(local, collective_id):
+    nr = lax.axis_size("row")
+    nc = lax.axis_size("col")
+    height, width = local.shape
+    part = height // nc
+    out = pl.pallas_call(
+        functools.partial(fused_sum_kernel, nr, nc),
+        out_shape=jax.ShapeDtypeStruct((nc, part, width), local.dtype),
+        in_specs=[pl.BlockSpec(memory_space=pltpu.VMEM)],
+        out_specs=pl.BlockSpec(memory_space=pltpu.VMEM),
+        scratch_shapes=[
+            pltpu.VMEM((nc, part, width), local.dtype),
+            pltpu.VMEM((nr, part, width), local.dtype),
+            pltpu.VMEM((nc, part, width), local.dtype),
+            (
+                pltpu.SemaphoreType.DMA((nc,)),
+                pltpu.SemaphoreType.DMA((nc,)),
+                pltpu.SemaphoreType.DMA((nr,)),
+                pltpu.SemaphoreType.DMA((nr,)),
+                pltpu.SemaphoreType.DMA((nc,)),
+                pltpu.SemaphoreType.DMA((nc,)),
+            ),
+        ],
+        compiler_params=pltpu.CompilerParams(
+            collective_id=collective_id, has_side_effects=True,
+            vmem_limit_bytes=48 * 1024 * 1024,
+        ),
+        cost_estimate=pl.CostEstimate(
+            flops=local.size, transcendentals=0, bytes_accessed=3 * local.size * 4
+        ),
+    )(local.reshape(nc, part, width))
+    return out.reshape(height, width)
+
+
 def all_sum(local, collective_base):
     row_count = lax.axis_size("row")
     col_count = lax.axis_size("col")
@@ -704,7 +791,7 @@
     local_grad = lax.dot_general(
         aggregated, hidden_grad, (((0,), (0,)), ((), ())), preferred_element_type=jnp.float32
     )
-    weight_grad = lax.psum(lax.psum(local_grad, "row"), "col") * (1.0 / math.sqrt(node_total))
+    weight_grad = fused_sum(local_grad, 1) * (1.0 / math.sqrt(node_total))
     source_back = row_block.reshape(row_tiles, tile_edge, feat_width)
     partial_cols = sparse_product(
         tile_block, col_index, row_index, live_count, source_back, col_tiles, True

time: 248 us -> 184 us (0.74)
  waiting for transfers between devices: 70.1 us -> 0 us
  Pallas kernels: 150 us -> 171 us
  between operations: 14.8 us -> 1.42 us
    psum x2 -> x0, waiting for transfers between devices: 70 us -> none  [the longest x1 49.5 us: per_device(): lax.psum(lax.psum(local_grad, 'row'), 'col') * (1.0 / math.sqrt(node_total))]
    pallas_call x0 -> x1, Pallas kernels: none -> 20.2 us  [fused_sum(): pl.pallas_call(functools.partial(fused_sum_kernel, nr, nc), out_shape=jax...]
  transfers between devices with their start and end apart: 2 -> 0, of which waited for: 2 -> 0; matrix products, arithmetic and copies ran while one was open for 0% -> 0% of each run, Pallas kernels for 29% -> 0%
where the time goes in v9:
time: 184 us; the launch traced here: 183 us
  Pallas kernels  171 us (93%)
  local copies, waits for them, and re-layouts  8.78 us (5%)
    pallas_call x1, Pallas kernels, scatter_sum_2d(): pl.pallas_call(functools.partial(scatter_sum_2d_kernel, nx, ny), out_shap...  40.2 us
    pallas_call x2, Pallas kernels, sparse_product(): pl.pallas_call(functools.partial(spmm_kernel, transpose), out_shape=jax.S...  37.1 us
    pallas_call x1, Pallas kernels, gather_all_2d(): pl.pallas_call(functools.partial(gather_all_2d_kernel, nx, ny), out_shape...  33.9 us
    pallas_call x1, Pallas kernels, fused_sum(): pl.pallas_call(functools.partial(fused_sum_kernel, nr, nc), out_shape=jax...  20.2 us
    pallas_call x1, Pallas kernels, gather_row(): pl.pallas_call(functools.partial(gather_row_kernel, nz), out_shape=jax.Sh...  19.8 us
    pallas_call x1, Pallas kernels, scatter_sum_row(): pl.pallas_call(functools.partial(scatter_sum_row_kernel, nz), out_shape=j...  19.4 us
    unnamed x15, local copies, waits for them, and re-layouts  8.78 us

profile of v9, /device:TPU:0, one launch (start us, length us, event | category | flops | bytes accessed | tf_op | source)
XLA Modules:
  0.0 183.1 jit_solution(11005639708411398595)
XLA Ops:
  0.6 0.0 copy-start
  1.3 0.0 copy-start.5
  1.3 0.9 copy-done.5
  2.3 19.8 %shard_map.94 = bf16[4,2,512,256]{3,2,1,0:T(8,128)(2,1)S(1)} custom-call(bf16[512,256]{1,0:T(8,128)(2,1)S(1)} %copy-done.5), custom_call_target="tpu_custom_call" | custom-call | bytes 6291456 | tf_op jit(solution)/shard_map/pallas_call | solution.py:502
  22.0 0.0 copy-start.4
  22.1 1.3 copy-done.4
  23.4 18.4 %shard_map.95 = bf16[64,128,256]{2,1,0:T(8,128)(2,1)} custom-call(s32[512]{0:T(512)} %bitcast.26, s32[512]{0:T(512)} %bitcast.28, s32[1]{0:T(128)} %bitcast.16.count_ref, bf16[512,128,128]{2,1,0:T(8,128)(2,1)} %bitcast.23, bf16[32,128,256]{2,1,0:T(8,128)(2,1)} %bitcast.21), custom_call_target="tpu_custom_call" | custom-call | flops 4294967296 | bytes 23068672 | tf_op jit(solution)/shard_map/pallas_call | solution.py:74
  41.8 0.0 copy-start.2
  41.8 2.2 %copy-done.2 = bf16[64,128,256]{2,1,0:T(8,128)(2,1)S(1)} copy-done((bf16[64,128,256]{2,1,0:T(8,128)(2,1)S(1)}, bf16[64,128,256]{2,1,0:T(8,128)(2,1)}, u32[]{:S(2)}) %copy-start.2) | copy-done | bytes 4194328
  44.0 0.0 copy-start.6
  44.0 40.2 %shard_map.96 = bf16[512,256]{1,0:T(8,128)(2,1)S(1)} custom-call(bf16[4,4,512,256]{3,2,1,0:T(8,128)(2,1)S(1)} %bitcast.19), custom_call_target="tpu_custom_call" | custom-call | flops 2097152 | bytes 12582912 | tf_op jit(solution)/shard_map/pallas_call | solution.py:337
  84.2 0.0 copy-done
  84.2 0.0 copy-done.6
  84.2 1.1 multiply_convert_fusion
  85.3 0.3 fusion
  85.6 0.3 convolution_convert_fusion.x_ref
  85.8 20.2 %shard_map.97 = f32[16,16,256]{2,1,0:T(8,128)S(1)} custom-call(f32[16,16,256]{2,1,0:T(8,128)S(1)} %bitcast.22), custom_call_target="tpu_custom_call" | custom-call | flops 65536 | bytes 786432 | tf_op jit(solution)/shard_map/pallas_call | solution.py:707
  106.1 0.7 broadcast_multiply_fusion
  106.8 33.9 %shard_map.98 = bf16[4,4,512,256]{3,2,1,0:T(8,128)(2,1)S(1)} custom-call(bf16[512,256]{1,0:T(8,128)(2,1)S(1)} %convolution_convert_fusion.x_ref), custom_call_target="tpu_custom_call" | custom-call | bytes 12582912 | tf_op jit(solution)/shard_map/pallas_call | solution.py:625
  140.7 0.0 copy-start.1
  140.7 1.9 %copy-done.1 = bf16[4,4,512,256]{3,2,1,0:T(8,128)(2,1)} copy-done((bf16[4,4,512,256]{3,2,1,0:T(8,128)(2,1)}, bf16[4,4,512,256]{3,2,1,0:T(8,128)(2,1)S(1)}, u32[]{:S(2)}) %copy-start.1) | copy-done | bytes 4194328
  142.7 18.7 %shard_map.99 = bf16[32,128,256]{2,1,0:T(8,128)(2,1)} custom-call(s32[512]{0:T(512)} %bitcast.29, s32[512]{0:T(512)} %bitcast.27, s32[1]{0:T(128)} %bitcast.17.count_ref, bf16[512,128,128]{2,1,0:T(8,128)(2,1)} %bitcast.24, bf16[64,128,256]{2,1,0:T(8,128)(2,1)} %bitcast.18), custom_call_target="tpu_custom_call" | custom-call | flops 4294967296 | bytes 23068672 | tf_op jit(solution)/shard_map/pallas_call | solution.py:74
  161.4 0.0 copy-start.3
  161.4 1.6 copy-done.3
  162.9 19.4 %shard_map.100 = f32[512,256]{1,0:T(8,128)S(1)} custom-call(bf16[4,2,512,256]{3,2,1,0:T(8,128)(2,1)S(1)} %bitcast.20), custom_call_target="tpu_custom_call" | custom-call | flops 1048576 | bytes 6291456 | tf_op jit(solution)/shard_map/pallas_call | solution.py:426
  182.3 0.8 copy.12
Async XLA Ops:
  0.6 83.5 %copy-start = (bf16[256,256]{1,0:T(8,128)(2,1)S(1)}, bf16[256,256]{1,0:T(8,128)(2,1)}, u32[]{:S(2)}) copy-start(bf16[256,256]{1,0:T(8,128)(2,1)} %param.12) | copy-start | bytes 393220
  1.3 1.0 copy-start.5
  22.0 1.3 copy-start.4
  41.8 2.2 %copy-start.2 = (bf16[64,128,256]{2,1,0:T(8,128)(2,1)S(1)}, bf16[64,128,256]{2,1,0:T(8,128)(2,1)}, u32[]{:S(2)}) copy-start(bf16[64,128,256]{2,1,0:T(8,128)(2,1)} %shard_map.95) | copy-start | bytes 12582916
  44.0 40.2 %copy-start.6 = (bf16[512,256]{1,0:T(8,128)(2,1)S(1)}, bf16[512,256]{1,0:T(8,128)(2,1)}, u32[]{:S(2)}) copy-start(bf16[512,256]{1,0:T(8,128)(2,1)} %param.13) | copy-start | bytes 786436
  140.7 1.9 %copy-start.1 = (bf16[4,4,512,256]{3,2,1,0:T(8,128)(2,1)}, bf16[4,4,512,256]{3,2,1,0:T(8,128)(2,1)S(1)}, u32[]{:S(2)}) copy-start(bf16[4,4,512,256]{3,2,1,0:T(8,128)(2,1)S(1)} %shard_map.98) | copy-start | bytes 12582916
  161.4 1.6 copy-start.3

commit v10 on v9

--- a/solution.py
+++ b/solution.py
@@ -733,6 +733,190 @@
     return out.reshape(height, width)
 
 
+def gather_and_sum_kernel(nx, ny, nr, x_ref, w_ref, out_ref, wout_ref, full, recv1, recv2, recv3, sems):
+    send, got, own_sem, wsend1, wgot1, wsend2, wgot2, wsend3, wgot3 = sems
+    mesh_kind = pl.DeviceIdType.MESH
+    nc = nx * ny
+    me = lax.axis_index("col")
+    my_r = lax.axis_index("row")
+    my_y = me // nx
+    my_x = lax.rem(me, nx)
+    half = x_ref.shape[0] // 2
+    lower = pl.ds(0, half)
+    upper = pl.ds(half, half)
+    along_col = lambda peer: (my_r, peer)
+    along_row = lambda peer: (peer, me)
+
+    barrier = pltpu.get_barrier_semaphore()
+    for offset in range(1, nc):
+        pl.semaphore_signal(barrier, 1, device_id=along_col(lax.rem(me + offset, nc)),
+                            device_id_type=mesh_kind)
+    for offset in range(1, nr):
+        pl.semaphore_signal(barrier, 1, device_id=along_row(lax.rem(my_r + offset, nr)),
+                            device_id_type=mesh_kind)
+    pl.semaphore_wait(barrier, nc + nr - 2)
+
+    def start_all(peers, count, me_index, src_of, dst, sem_send, sem_got):
+        started = []
+        for offset in range(1, count):
+            peer = lax.rem(me_index + offset, count)
+            copy = pltpu.make_async_remote_copy(
+                src_ref=src_of(peer), dst_ref=dst.at[me_index],
+                send_sem=sem_send.at[offset], recv_sem=sem_got.at[me_index],
+                device_id=peers(peer), device_id_type=mesh_kind,
+            )
+            copy.start()
+            started.append(copy)
+        return started
+
+    def wait_all(peers, count, me_index, src_of, dst, sem_send, sem_got):
+        for offset in range(1, count):
+            source = lax.rem(me_index + count - offset, count)
+            pltpu.make_async_remote_copy(
+                src_ref=src_of(source), dst_ref=dst.at[source],
+                send_sem=sem_send.at[offset], recv_sem=sem_got.at[source],
+                device_id=peers(source), device_id_type=mesh_kind,
+            ).wait_recv()
+
+    own = pltpu.make_async_copy(x_ref, full.at[my_y, my_x], own_sem.at[0])
+    own.start()
+    sends = []
+    for offset in range(1, nx):
+        peer_x = lax.rem(my_x + offset, nx)
+        copy = pltpu.make_async_remote_copy(
+            src_ref=x_ref.at[lower], dst_ref=full.at[my_y, my_x, lower],
+            send_sem=send.at[0, offset], recv_sem=got.at[0, my_x],
+            device_id=torus_peer(my_y, peer_x, nx), device_id_type=mesh_kind,
+        )
+        copy.start()
+        sends.append(copy)
+    for offset in range(1, ny):
+        peer_y = lax.rem(my_y + offset, ny)
+        copy = pltpu.make_async_remote_copy(
+            src_ref=x_ref.at[upper], dst_ref=full.at[my_y, my_x, upper],
+            send_sem=send.at[1, offset], recv_sem=got.at[1, my_y],
+            device_id=torus_peer(peer_y, my_x, nx), device_id_type=mesh_kind,
+        )
+        copy.start()
+        sends.append(copy)
+    recv1[me] = w_ref[me]
+    weight_src = lambda peer: w_ref.at[peer]
+    sends += start_all(along_col, nc, me, weight_src, recv1, wsend1, wgot1)
+    own.wait()
+    for offset in range(1, nx):
+        source_x = lax.rem(my_x + nx - offset, nx)
+        pltpu.make_async_remote_copy(
+            src_ref=x_ref.at[lower], dst_ref=full.at[my_y, source_x, lower],
+            send_sem=send.at[0, offset], recv_sem=got.at[0, source_x],
+            device_id=torus_peer(my_y, source_x, nx), device_id_type=mesh_kind,
+        ).wait_recv()
+    for offset in range(1, ny):
+        peer_y = lax.rem(my_y + offset, ny)
+        copy = pltpu.make_async_remote_copy(
+            src_ref=full.at[my_y, :, lower], dst_ref=full.at[my_y, :, lower],
+            send_sem=send.at[2, offset], recv_sem=got.at[2, my_y],
+            device_id=torus_peer(peer_y, my_x, nx), device_id_type=mesh_kind,
+        )
+        copy.start()
+        sends.append(copy)
+    for offset in range(1, ny):
+        source_y = lax.rem(my_y + ny - offset, ny)
+        pltpu.make_async_remote_copy(
+            src_ref=x_ref.at[upper], dst_ref=full.at[source_y, my_x, upper],
+            send_sem=send.at[1, offset], recv_sem=got.at[1, source_y],
+            device_id=torus_peer(source_y, my_x, nx), device_id_type=mesh_kind,
+        ).wait_recv()
+    for offset in range(1, nx):
+        peer_x = lax.rem(my_x + offset, nx)
+        copy = pltpu.make_async_remote_copy(
+            src_ref=full.at[:, my_x, upper], dst_ref=full.at[:, my_x, upper],
+            send_sem=send.at[3, offset], recv_sem=got.at[3, my_x],
+            device_id=torus_peer(my_y, peer_x, nx), device_id_type=mesh_kind,
+        )
+        copy.start()
+        sends.append(copy)
+
+    wait_all(along_col, nc, me, weight_src, recv1, wsend1, wgot1)
+    part = recv1[0]
+    for j in range(1, nc):
+        part = part + recv1[j]
+    recv2[my_r] = part
+    row_src = lambda peer: recv2.at[my_r]
+    sends += start_all(along_row, nr, my_r, row_src, recv2, wsend2, wgot2)
+    wait_all(along_row, nr, my_r, row_src, recv2, wsend2, wgot2)
+    total = recv2[0]
+    for j in range(1, nr):
+        total = total + recv2[j]
+    recv3[me] = total
+    back_src = lambda peer: recv3.at[me]
+    sends += start_all(along_col, nc, me, back_src, recv3, wsend3, wgot3)
+
+    for offset in range(1, ny):
+        source_y = lax.rem(my_y + ny - offset, ny)
+        pltpu.make_async_remote_copy(
+            src_ref=full.at[source_y, :, lower], dst_ref=full.at[source_y, :, lower],
+            send_sem=send.at[2, offset], recv_sem=got.at[2, source_y],
+            device_id=torus_peer(source_y, my_x, nx), device_id_type=mesh_kind,
+        ).wait_recv()
+    for offset in range(1, nx):
+        source_x = lax.rem(my_x + nx - offset, nx)
+        pltpu.make_async_remote_copy(
+            src_ref=full.at[:, source_x, upper], dst_ref=full.at[:, source_x, upper],
+            send_sem=send.at[3, offset], recv_sem=got.at[3, source_x],
+            device_id=torus_peer(my_y, source_x, nx), device_id_type=mesh_kind,
+        ).wait_recv()
+    out_ref[...] = full[...]
+    wait_all(along_col, nc, me, back_src, recv3, wsend3, wgot3)
+    wout_ref[...] = recv3[...]
+    for copy in sends:
+        copy.wait_send()
+
+
+def gather_and_sum(x, local, nx, collective_id):
+    rows, lanes = x.shape
+    nc = lax.axis_size("col")
+    nr = lax.axis_size("row")
+    ny = nc // nx
+    side = max(nx, ny)
+    height, width = local.shape
+    part = height // nc
+    out, summed = pl.pallas_call(
+        functools.partial(gather_and_sum_kernel, nx, ny, nr),
+        out_shape=(
+            jax.ShapeDtypeStruct((ny, nx, rows, lanes), x.dtype),
+            jax.ShapeDtypeStruct((nc, part, width), local.dtype),
+        ),
+        in_specs=[pl.BlockSpec(memory_space=pltpu.VMEM)] * 2,
+        out_specs=(pl.BlockSpec(memory_space=pltpu.VMEM),) * 2,
+        scratch_shapes=[
+            pltpu.VMEM((ny, nx, rows, lanes), x.dtype),
+            pltpu.VMEM((nc, part, width), local.dtype),
+            pltpu.VMEM((nr, part, width), local.dtype),
+            pltpu.VMEM((nc, part, width), local.dtype),
+            (
+                pltpu.SemaphoreType.DMA((4, side)),
+                pltpu.SemaphoreType.DMA((4, side)),
+                pltpu.SemaphoreType.DMA((1,)),
+                pltpu.SemaphoreType.DMA((nc,)),
+                pltpu.SemaphoreType.DMA((nc,)),
+                pltpu.SemaphoreType.DMA((nr,)),
+                pltpu.SemaphoreType.DMA((nr,)),
+                pltpu.SemaphoreType.DMA((nc,)),
+                pltpu.SemaphoreType.DMA((nc,)),
+            ),
+        ],
+        compiler_params=pltpu.CompilerParams(
+            collective_id=collective_id, has_side_effects=True,
+            vmem_limit_bytes=48 * 1024 * 1024,
+        ),
+        cost_estimate=pl.CostEstimate(
+            flops=local.size, transcendentals=0,
+            bytes_accessed=3 * nc * x.size * x.dtype.itemsize + 3 * local.size * 4,
+        ),
+    )(x, local.reshape(nc, part, width))
+    return out.reshape(nc, rows, lanes), summed.reshape(height, width)
+
+
 def all_sum(local, collective_base):
     row_count = lax.axis_size("row")
     col_count = lax.axis_size("col")
@@ -787,11 +971,11 @@
     own_grad = lax.dot_general(
         hidden_grad, weight, (((1,), (1,)), ((), ())), preferred_element_type=jnp.float32
     ).astype(jnp.bfloat16)
-    row_block = gather_all_2d(own_grad, TORUS_X, 7)
     local_grad = lax.dot_general(
         aggregated, hidden_grad, (((0,), (0,)), ((), ())), preferred_element_type=jnp.float32
     )
-    weight_grad = fused_sum(local_grad, 1) * (1.0 / math.sqrt(node_total))
+    row_block, summed_grad = gather_and_sum(own_grad, local_grad, TORUS_X, 7)
+    weight_grad = summed_grad * (1.0 / math.sqrt(node_total))
     source_back = row_block.reshape(row_tiles, tile_edge, feat_width)
     partial_cols = sparse_product(
         tile_block, col_index, row_index, live_count, source_back, col_tiles, True

time: 184 us -> 171 us (0.929)
  Pallas kernels: 171 us -> 157 us
    pallas_call x2 -> x1, Pallas kernels: 54.2 us -> 40.8 us  [gather_and_sum(): pl.pallas_call(functools.partial(gather_and_sum_kernel, nx, ny, nr), out_...]
where the time goes in v10:
time: 171 us; the launch traced here: 170 us
  Pallas kernels  157 us (92%)
  local copies, waits for them, and re-layouts  8.77 us (5%)
    pallas_call x1, Pallas kernels, scatter_sum_2d(): pl.pallas_call(functools.partial(scatter_sum_2d_kernel, nx, ny), out_shap...  41.1 us
    pallas_call x1, Pallas kernels, gather_and_sum(): pl.pallas_call(functools.partial(gather_and_sum_kernel, nx, ny, nr), out_...  40.8 us
    pallas_call x2, Pallas kernels, sparse_product(): pl.pallas_call(functools.partial(spmm_kernel, transpose), out_shape=jax.S...  36.3 us
    pallas_call x1, Pallas kernels, gather_row(): pl.pallas_call(functools.partial(gather_row_kernel, nz), out_shape=jax.Sh...  19.8 us
    pallas_call x1, Pallas kernels, scatter_sum_row(): pl.pallas_call(functools.partial(scatter_sum_row_kernel, nz), out_shape=j...  19.3 us
    unnamed x15, local copies, waits for them, and re-layouts  8.77 us

profile of v10, /device:TPU:0, one launch (start us, length us, event | category | flops | bytes accessed | tf_op | source)
XLA Modules:
  0.0 169.8 jit_solution(16616211824704525862)
XLA Ops:
  0.6 0.0 copy-start
  1.3 0.0 copy-start.5
  1.3 0.9 copy-done.5
  2.3 19.8 %shard_map.94 = bf16[4,2,512,256]{3,2,1,0:T(8,128)(2,1)S(1)} custom-call(bf16[512,256]{1,0:T(8,128)(2,1)S(1)} %copy-done.5), custom_call_target="tpu_custom_call" | custom-call | bytes 6291456 | tf_op jit(solution)/shard_map/pallas_call | solution.py:502
  22.0 0.0 copy-start.3
  22.1 1.3 copy-done.3
  23.4 18.0 %shard_map.95 = bf16[64,128,256]{2,1,0:T(8,128)(2,1)} custom-call(s32[512]{0:T(512)} %bitcast.26, s32[512]{0:T(512)} %bitcast.28, s32[1]{0:T(128)} %bitcast.16.count_ref, bf16[512,128,128]{2,1,0:T(8,128)(2,1)} %bitcast.23, bf16[32,128,256]{2,1,0:T(8,128)(2,1)} %bitcast.20), custom_call_target="tpu_custom_call" | custom-call | flops 4294967296 | bytes 23068672 | tf_op jit(solution)/shard_map/pallas_call | solution.py:74
  41.4 0.0 copy-start.1
  41.4 2.2 %copy-done.1 = bf16[64,128,256]{2,1,0:T(8,128)(2,1)S(1)} copy-done((bf16[64,128,256]{2,1,0:T(8,128)(2,1)S(1)}, bf16[64,128,256]{2,1,0:T(8,128)(2,1)}, u32[]{:S(2)}) %copy-start.1) | copy-done | bytes 4194328
  43.6 0.0 copy-start.6
  43.6 41.1 %shard_map.96 = bf16[512,256]{1,0:T(8,128)(2,1)S(1)} custom-call(bf16[4,4,512,256]{3,2,1,0:T(8,128)(2,1)S(1)} %bitcast.18), custom_call_target="tpu_custom_call" | custom-call | flops 2097152 | bytes 12582912 | tf_op jit(solution)/shard_map/pallas_call | solution.py:337
  84.7 0.0 copy-done
  84.7 0.0 copy-done.6
  84.7 1.1 multiply_convert_fusion
  85.8 0.3 fusion
  86.1 0.3 convolution_convert_fusion.x_ref
  86.4 40.8 %shard_map.97 = (bf16[4,4,512,256]{3,2,1,0:T(8,128)(2,1)S(1)}, f32[16,16,256]{2,1,0:T(8,128)S(1)}) custom-call(bf16[512,256]{1,0:T(8,128)(2,1)S(1)} %convolution_convert_fusion.x_ref, f32[16,16,256]{2,1,0:T(8,128)S(1)} %bitcast.22), custom_call_target="tpu_custom_call" | custom-call | flops 65536 | bytes 13369344 | tf_op jit(solution)/shard_map/pallas_call | solution.py:883
  127.1 0.0 copy-start.4
  127.1 1.9 %copy-done.4 = bf16[4,4,512,256]{3,2,1,0:T(8,128)(2,1)} copy-done((bf16[4,4,512,256]{3,2,1,0:T(8,128)(2,1)}, bf16[4,4,512,256]{3,2,1,0:T(8,128)(2,1)S(1)}, u32[]{:S(2)}) %copy-start.4) | copy-done | bytes 4194328
  129.1 0.7 broadcast_multiply_fusion
  129.8 18.3 %shard_map.98 = bf16[32,128,256]{2,1,0:T(8,128)(2,1)} custom-call(s32[512]{0:T(512)} %bitcast.29, s32[512]{0:T(512)} %bitcast.27, s32[1]{0:T(128)} %bitcast.17.count_ref, bf16[512,128,128]{2,1,0:T(8,128)(2,1)} %bitcast.24, bf16[64,128,256]{2,1,0:T(8,128)(2,1)} %bitcast.21), custom_call_target="tpu_custom_call" | custom-call | flops 4294967296 | bytes 23068672 | tf_op jit(solution)/shard_map/pallas_call | solution.py:74
  148.1 0.0 copy-start.2
  148.1 1.6 copy-done.2
  149.7 19.3 %shard_map.99 = f32[512,256]{1,0:T(8,128)S(1)} custom-call(bf16[4,2,512,256]{3,2,1,0:T(8,128)(2,1)S(1)} %bitcast.19), custom_call_target="tpu_custom_call" | custom-call | flops 1048576 | bytes 6291456 | tf_op jit(solution)/shard_map/pallas_call | solution.py:426
  169.0 0.8 copy.12
Async XLA Ops:
  0.6 84.1 %copy-start = (bf16[256,256]{1,0:T(8,128)(2,1)S(1)}, bf16[256,256]{1,0:T(8,128)(2,1)}, u32[]{:S(2)}) copy-start(bf16[256,256]{1,0:T(8,128)(2,1)} %param.12) | copy-start | bytes 393220
  1.3 1.0 copy-start.5
  22.0 1.3 copy-start.3
  41.4 2.2 %copy-start.1 = (bf16[64,128,256]{2,1,0:T(8,128)(2,1)S(1)}, bf16[64,128,256]{2,1,0:T(8,128)(2,1)}, u32[]{:S(2)}) copy-start(bf16[64,128,256]{2,1,0:T(8,128)(2,1)} %shard_map.95) | copy-start | bytes 12582916
  43.6 41.1 %copy-start.6 = (bf16[512,256]{1,0:T(8,128)(2,1)S(1)}, bf16[512,256]{1,0:T(8,128)(2,1)}, u32[]{:S(2)}) copy-start(bf16[512,256]{1,0:T(8,128)(2,1)} %param.13) | copy-start | bytes 786436
  127.1 1.9 %copy-start.4 = (bf16[4,4,512,256]{3,2,1,0:T(8,128)(2,1)}, bf16[4,4,512,256]{3,2,1,0:T(8,128)(2,1)S(1)}, u32[]{:S(2)}) copy-start(bf16[4,4,512,256]{3,2,1,0:T(8,128)(2,1)S(1)} %get-tuple-element.6) | copy-start | bytes 12582916
  148.1 1.6 copy-start.2

commit v11 on v10

--- a/solution.py
+++ b/solution.py
@@ -270,13 +270,6 @@
             send_sem=send1.at[0, offset], recv_sem=got1.at[0, source_x],
             device_id=torus_peer(my_y, source_x, nx), device_id_type=mesh_kind,
         ).wait_recv()
-    for offset in range(1, ny):
-        source_y = lax.rem(my_y + ny - offset, ny)
-        pltpu.make_async_remote_copy(
-            src_ref=x_hbm.at[source_y, :, upper], dst_ref=recv1.at[1, source_y],
-            send_sem=send1.at[1, offset], recv_sem=got1.at[1, source_y],
-            device_id=torus_peer(source_y, my_x, nx), device_id_type=mesh_kind,
-        ).wait_recv()
 
     def add_up(stack):
         total = stack[0].astype(jnp.float32)
@@ -286,10 +279,7 @@
 
     for target in range(ny):
         mid[0, target] = add_up(recv1[0, :, target]).astype(mid.dtype)
-    for target in range(nx):
-        mid[1, target] = add_up(recv1[1, :, target]).astype(mid.dtype)
     recv2[0, my_y] = mid[0, my_y]
-    recv2[1, my_x] = mid[1, my_x]
 
     for offset in range(1, ny):
         peer_y = lax.rem(my_y + offset, ny)
@@ -300,6 +290,16 @@
         )
         copy.start()
         sends.append(copy)
+    for offset in range(1, ny):
+        source_y = lax.rem(my_y + ny - offset, ny)
+        pltpu.make_async_remote_copy(
+            src_ref=x_hbm.at[source_y, :, upper], dst_ref=recv1.at[1, source_y],
+            send_sem=send1.at[1, offset], recv_sem=got1.at[1, source_y],
+            device_id=torus_peer(source_y, my_x, nx), device_id_type=mesh_kind,
+        ).wait_recv()
+    for target in range(nx):
+        mid[1, target] = add_up(recv1[1, :, target]).astype(mid.dtype)
+    recv2[1, my_x] = mid[1, my_x]
     for offset in range(1, nx):
         peer_x = lax.rem(my_x + offset, nx)
         copy = pltpu.make_async_remote_copy(
@@ -316,6 +316,7 @@
             send_sem=send2.at[0, offset], recv_sem=got2.at[0, source_y],
             device_id=torus_peer(source_y, my_x, nx), device_id_type=mesh_kind,
         ).wait_recv()
+    out_ref[lower] = add_up(recv2[0]).astype(out_ref.dtype)
     for offset in range(1, nx):
         source_x = lax.rem(my_x + nx - offset, nx)
         pltpu.make_async_remote_copy(
@@ -323,7 +324,6 @@
             send_sem=send2.at[1, offset], recv_sem=got2.at[1, source_x],
             device_id=torus_peer(my_y, source_x, nx), device_id_type=mesh_kind,
         ).wait_recv()
-    out_ref[lower] = add_up(recv2[0]).astype(out_ref.dtype)
     out_ref[upper] = add_up(recv2[1]).astype(out_ref.dtype)
     for copy in sends:
         copy.wait_send()

time: 171 us -> 172 us (level)
  no operation moved by 1% of the time
where the time goes in v11:
time: 172 us; the launch traced here: 170 us
  Pallas kernels  158 us (92%)
  local copies, waits for them, and re-layouts  8.77 us (5%)
    pallas_call x1, Pallas kernels, gather_and_sum(): pl.pallas_call(functools.partial(gather_and_sum_kernel, nx, ny, nr), out_...  40.4 us
    pallas_call x1, Pallas kernels, scatter_sum_2d(): pl.pallas_call(functools.partial(scatter_sum_2d_kernel, nx, ny), out_shap...  39.9 us
    pallas_call x2, Pallas kernels, sparse_product(): pl.pallas_call(functools.partial(spmm_kernel, transpose), out_shape=jax.S...  38 us
    pallas_call x1, Pallas kernels, gather_row(): pl.pallas_call(functools.partial(gather_row_kernel, nz), out_shape=jax.Sh...  19.8 us
    pallas_call x1, Pallas kernels, scatter_sum_row(): pl.pallas_call(functools.partial(scatter_sum_row_kernel, nz), out_shape=j...  19.5 us
    unnamed x15, local copies, waits for them, and re-layouts  8.77 us

profile of v11, /device:TPU:0, one launch (start us, length us, event | category | flops | bytes accessed | tf_op | source)
XLA Modules:
  0.0 170.1 jit_solution(8614930400738618458)
XLA Ops:
  0.6 0.0 copy-start
  1.3 0.0 copy-start.5
  1.3 0.9 copy-done.5
  2.3 19.8 %shard_map.94 = bf16[4,2,512,256]{3,2,1,0:T(8,128)(2,1)S(1)} custom-call(bf16[512,256]{1,0:T(8,128)(2,1)S(1)} %copy-done.5), custom_call_target="tpu_custom_call" | custom-call | bytes 6291456 | tf_op jit(solution)/shard_map/pallas_call | solution.py:502
  22.0 0.0 copy-start.3
  22.1 1.3 copy-done.3
  23.4 18.9 %shard_map.95 = bf16[64,128,256]{2,1,0:T(8,128)(2,1)} custom-call(s32[512]{0:T(512)} %bitcast.26, s32[512]{0:T(512)} %bitcast.28, s32[1]{0:T(128)} %bitcast.16.count_ref, bf16[512,128,128]{2,1,0:T(8,128)(2,1)} %bitcast.23, bf16[32,128,256]{2,1,0:T(8,128)(2,1)} %bitcast.20), custom_call_target="tpu_custom_call" | custom-call | flops 4294967296 | bytes 23068672 | tf_op jit(solution)/shard_map/pallas_call | solution.py:74
  42.3 0.0 copy-start.1
  42.3 2.2 %copy-done.1 = bf16[64,128,256]{2,1,0:T(8,128)(2,1)S(1)} copy-done((bf16[64,128,256]{2,1,0:T(8,128)(2,1)S(1)}, bf16[64,128,256]{2,1,0:T(8,128)(2,1)}, u32[]{:S(2)}) %copy-start.1) | copy-done | bytes 4194328
  44.5 0.0 copy-start.6
  44.5 39.9 %shard_map.96 = bf16[512,256]{1,0:T(8,128)(2,1)S(1)} custom-call(bf16[4,4,512,256]{3,2,1,0:T(8,128)(2,1)S(1)} %bitcast.18), custom_call_target="tpu_custom_call" | custom-call | flops 2097152 | bytes 12582912 | tf_op jit(solution)/shard_map/pallas_call | solution.py:337
  84.3 0.0 copy-done
  84.3 0.0 copy-done.6
  84.4 1.1 multiply_convert_fusion
  85.5 0.3 fusion
  85.7 0.3 convolution_convert_fusion.x_ref
  86.0 40.4 %shard_map.97 = (bf16[4,4,512,256]{3,2,1,0:T(8,128)(2,1)S(1)}, f32[16,16,256]{2,1,0:T(8,128)S(1)}) custom-call(bf16[512,256]{1,0:T(8,128)(2,1)S(1)} %convolution_convert_fusion.x_ref, f32[16,16,256]{2,1,0:T(8,128)S(1)} %bitcast.22), custom_call_target="tpu_custom_call" | custom-call | flops 65536 | bytes 13369344 | tf_op jit(solution)/shard_map/pallas_call | solution.py:883
  126.4 0.0 copy-start.4
  126.4 1.9 %copy-done.4 = bf16[4,4,512,256]{3,2,1,0:T(8,128)(2,1)} copy-done((bf16[4,4,512,256]{3,2,1,0:T(8,128)(2,1)}, bf16[4,4,512,256]{3,2,1,0:T(8,128)(2,1)S(1)}, u32[]{:S(2)}) %copy-start.4) | copy-done | bytes 4194328
  128.4 0.7 broadcast_multiply_fusion
  129.1 19.1 %shard_map.98 = bf16[32,128,256]{2,1,0:T(8,128)(2,1)} custom-call(s32[512]{0:T(512)} %bitcast.29, s32[512]{0:T(512)} %bitcast.27, s32[1]{0:T(128)} %bitcast.17.count_ref, bf16[512,128,128]{2,1,0:T(8,128)(2,1)} %bitcast.24, bf16[64,128,256]{2,1,0:T(8,128)(2,1)} %bitcast.21), custom_call_target="tpu_custom_call" | custom-call | flops 4294967296 | bytes 23068672 | tf_op jit(solution)/shard_map/pallas_call | solution.py:74
  148.2 0.0 copy-start.2
  148.2 1.6 copy-done.2
  149.8 19.5 %shard_map.99 = f32[512,256]{1,0:T(8,128)S(1)} custom-call(bf16[4,2,512,256]{3,2,1,0:T(8,128)(2,1)S(1)} %bitcast.19), custom_call_target="tpu_custom_call" | custom-call | flops 1048576 | bytes 6291456 | tf_op jit(solution)/shard_map/pallas_call | solution.py:426
  169.3 0.8 copy.12
Async XLA Ops:
  0.6 83.7 %copy-start = (bf16[256,256]{1,0:T(8,128)(2,1)S(1)}, bf16[256,256]{1,0:T(8,128)(2,1)}, u32[]{:S(2)}) copy-start(bf16[256,256]{1,0:T(8,128)(2,1)} %param.12) | copy-start | bytes 393220
  1.3 1.0 copy-start.5
  22.0 1.3 copy-start.3
  42.3 2.2 %copy-start.1 = (bf16[64,128,256]{2,1,0:T(8,128)(2,1)S(1)}, bf16[64,128,256]{2,1,0:T(8,128)(2,1)}, u32[]{:S(2)}) copy-start(bf16[64,128,256]{2,1,0:T(8,128)(2,1)} %shard_map.95) | copy-start | bytes 12582916
  44.5 39.9 %copy-start.6 = (bf16[512,256]{1,0:T(8,128)(2,1)S(1)}, bf16[512,256]{1,0:T(8,128)(2,1)}, u32[]{:S(2)}) copy-start(bf16[512,256]{1,0:T(8,128)(2,1)} %param.13) | copy-start | bytes 786436
  126.4 1.9 %copy-start.4 = (bf16[4,4,512,256]{3,2,1,0:T(8,128)(2,1)}, bf16[4,4,512,256]{3,2,1,0:T(8,128)(2,1)S(1)}, u32[]{:S(2)}) copy-start(bf16[4,4,512,256]{3,2,1,0:T(8,128)(2,1)S(1)} %get-tuple-element.6) | copy-start | bytes 12582916
  148.2 1.6 copy-start.2

commit v12 on v11

--- a/solution.py
+++ b/solution.py
@@ -382,30 +382,42 @@
     my_z = me // 2
     my_core = lax.rem(me, 2)
     other_core = 1 - my_core
+    partner = row_peer(my_z * 2 + other_core)
     greet_row(my_z, my_core, nz)
     own = pltpu.make_async_copy(x_hbm.at[:, my_core], own1, own_sem.at[0])
     own.start()
-    first = pltpu.make_async_remote_copy(
-        src_ref=x_hbm.at[:, other_core], dst_ref=recv1,
-        send_sem=send1.at[0], recv_sem=got1.at[0],
-        device_id=row_peer(my_z * 2 + other_core), device_id_type=mesh_kind,
-    )
-    first.start()
+    sends = []
+    for offset in range(nz):
+        target_z = lax.rem(my_z + offset + 1, nz)
+        copy = pltpu.make_async_remote_copy(
+            src_ref=x_hbm.at[target_z, other_core], dst_ref=recv1.at[target_z],
+            send_sem=send1.at[offset], recv_sem=got1.at[target_z],
+            device_id=partner, device_id_type=mesh_kind,
+        )
+        copy.start()
+        sends.append(copy)
     own.wait()
-    first.wait_recv()
-    for target in range(nz):
-        mid[target] = (own1[target].astype(jnp.float32) + recv1[target].astype(jnp.float32)).astype(mid.dtype)
-    sends = []
-    for offset in range(1, nz):
-        peer_z = lax.rem(my_z + offset, nz)
-        copy = pltpu.make_async_remote_copy(
-            src_ref=mid.at[peer_z], dst_ref=recv2.at[my_z],
-            send_sem=send2.at[offset], recv_sem=got2.at[my_z],
-            device_id=row_peer(peer_z * 2 + my_core), device_id_type=mesh_kind,
-        )
-        copy.start()
-        sends.append(copy)
-    total = mid[my_z].astype(jnp.float32)
+    for offset in range(nz - 1):
+        target_z = lax.rem(my_z + offset + 1, nz)
+        pltpu.make_async_remote_copy(
+            src_ref=x_hbm.at[target_z, other_core], dst_ref=recv1.at[target_z],
+            send_sem=send1.at[offset], recv_sem=got1.at[target_z],
+            device_id=partner, device_id_type=mesh_kind,
+        ).wait_recv()
+        mid[target_z] = (own1[target_z].astype(jnp.float32) + recv1[target_z].astype(jnp.float32)).astype(mid.dtype)
+        copy = pltpu.make_async_remote_copy(
+            src_ref=mid.at[target_z], dst_ref=recv2.at[my_z],
+            send_sem=send2.at[offset + 1], recv_sem=got2.at[my_z],
+            device_id=row_peer(target_z * 2 + my_core), device_id_type=mesh_kind,
+        )
+        copy.start()
+        sends.append(copy)
+    pltpu.make_async_remote_copy(
+        src_ref=x_hbm.at[my_z, other_core], dst_ref=recv1.at[my_z],
+        send_sem=send1.at[nz - 1], recv_sem=got1.at[my_z],
+        device_id=partner, device_id_type=mesh_kind,
+    ).wait_recv()
+    total = own1[my_z].astype(jnp.float32) + recv1[my_z].astype(jnp.float32)
     for offset in range(1, nz):
         source_z = lax.rem(my_z + nz - offset, nz)
         pltpu.make_async_remote_copy(
@@ -415,7 +427,6 @@
         ).wait_recv()
         total = total + recv2[source_z].astype(jnp.float32)
     out_ref[...] = total.astype(out_ref.dtype)
-    first.wait_send()
     for copy in sends:
         copy.wait_send()
 
@@ -434,8 +445,8 @@
             pltpu.VMEM((nz, rows, lanes), x.dtype),
             pltpu.VMEM((nz, rows, lanes), x.dtype),
             (
-                pltpu.SemaphoreType.DMA((1,)),
-                pltpu.SemaphoreType.DMA((1,)),
+                pltpu.SemaphoreType.DMA((nz,)),
+                pltpu.SemaphoreType.DMA((nz,)),
                 pltpu.SemaphoreType.DMA((nz,)),
                 pltpu.SemaphoreType.DMA((nz,)),
                 pltpu.SemaphoreType.DMA((1,)),

time: 172 us -> 169 us (0.983)
  Pallas kernels: 158 us -> 155 us
    pallas_call x1, Pallas kernels: 19.5 us -> 17.3 us  [scatter_sum_row(): pl.pallas_call(functools.partial(scatter_sum_row_kernel, nz), out_shape=j...]
where the time goes in v12:
time: 169 us; the launch traced here: 168 us
  Pallas kernels  155 us (92%)
  local copies, waits for them, and re-layouts  8.77 us (5%)
    pallas_call x1, Pallas kernels, gather_and_sum(): pl.pallas_call(functools.partial(gather_and_sum_kernel, nx, ny, nr), out_...  41.4 us
    pallas_call x1, Pallas kernels, scatter_sum_2d(): pl.pallas_call(functools.partial(scatter_sum_2d_kernel, nx, ny), out_shap...  38.5 us
    pallas_call x2, Pallas kernels, sparse_product(): pl.pallas_call(functools.partial(spmm_kernel, transpose), out_shape=jax.S...  38.4 us
    pallas_call x1, Pallas kernels, gather_row(): pl.pallas_call(functools.partial(gather_row_kernel, nz), out_shape=jax.Sh...  19.8 us
    pallas_call x1, Pallas kernels, scatter_sum_row(): pl.pallas_call(functools.partial(scatter_sum_row_kernel, nz), out_shape=j...  17.3 us
    unnamed x15, local copies, waits for them, and re-layouts  8.77 us

profile of v12, /device:TPU:0, one launch (start us, length us, event | category | flops | bytes accessed | tf_op | source)
XLA Modules:
  0.0 167.9 jit_solution(16993689892322189724)
XLA Ops:
  0.6 0.0 copy-start
  1.3 0.0 copy-start.5
  1.3 0.9 copy-done.5
  2.3 19.8 %shard_map.94 = bf16[4,2,512,256]{3,2,1,0:T(8,128)(2,1)S(1)} custom-call(bf16[512,256]{1,0:T(8,128)(2,1)S(1)} %copy-done.5), custom_call_target="tpu_custom_call" | custom-call | bytes 6291456 | tf_op jit(solution)/shard_map/pallas_call | solution.py:513
  22.0 0.0 copy-start.3
  22.1 1.3 copy-done.3
  23.4 19.1 %shard_map.95 = bf16[64,128,256]{2,1,0:T(8,128)(2,1)} custom-call(s32[512]{0:T(512)} %bitcast.26, s32[512]{0:T(512)} %bitcast.28, s32[1]{0:T(128)} %bitcast.16.count_ref, bf16[512,128,128]{2,1,0:T(8,128)(2,1)} %bitcast.23, bf16[32,128,256]{2,1,0:T(8,128)(2,1)} %bitcast.20), custom_call_target="tpu_custom_call" | custom-call | flops 4294967296 | bytes 23068672 | tf_op jit(solution)/shard_map/pallas_call | solution.py:74
  42.5 0.0 copy-start.1
  42.5 2.2 %copy-done.1 = bf16[64,128,256]{2,1,0:T(8,128)(2,1)S(1)} copy-done((bf16[64,128,256]{2,1,0:T(8,128)(2,1)S(1)}, bf16[64,128,256]{2,1,0:T(8,128)(2,1)}, u32[]{:S(2)}) %copy-start.1) | copy-done | bytes 4194328
  44.7 0.0 copy-start.6
  44.7 38.5 %shard_map.96 = bf16[512,256]{1,0:T(8,128)(2,1)S(1)} custom-call(bf16[4,4,512,256]{3,2,1,0:T(8,128)(2,1)S(1)} %bitcast.18), custom_call_target="tpu_custom_call" | custom-call | flops 2097152 | bytes 12582912 | tf_op jit(solution)/shard_map/pallas_call | solution.py:337
  83.1 0.0 copy-done
  83.2 0.0 copy-done.6
  83.2 1.1 multiply_convert_fusion
  84.3 0.3 fusion
  84.5 0.3 convolution_convert_fusion.x_ref
  84.8 41.4 %shard_map.97 = (bf16[4,4,512,256]{3,2,1,0:T(8,128)(2,1)S(1)}, f32[16,16,256]{2,1,0:T(8,128)S(1)}) custom-call(bf16[512,256]{1,0:T(8,128)(2,1)S(1)} %convolution_convert_fusion.x_ref, f32[16,16,256]{2,1,0:T(8,128)S(1)} %bitcast.22), custom_call_target="tpu_custom_call" | custom-call | flops 65536 | bytes 13369344 | tf_op jit(solution)/shard_map/pallas_call | solution.py:894
  126.2 0.0 copy-start.4
  126.3 1.9 %copy-done.4 = bf16[4,4,512,256]{3,2,1,0:T(8,128)(2,1)} copy-done((bf16[4,4,512,256]{3,2,1,0:T(8,128)(2,1)}, bf16[4,4,512,256]{3,2,1,0:T(8,128)(2,1)S(1)}, u32[]{:S(2)}) %copy-start.4) | copy-done | bytes 4194328
  128.2 0.7 broadcast_multiply_fusion
  128.9 19.3 %shard_map.98 = bf16[32,128,256]{2,1,0:T(8,128)(2,1)} custom-call(s32[512]{0:T(512)} %bitcast.29, s32[512]{0:T(512)} %bitcast.27, s32[1]{0:T(128)} %bitcast.17.count_ref, bf16[512,128,128]{2,1,0:T(8,128)(2,1)} %bitcast.24, bf16[64,128,256]{2,1,0:T(8,128)(2,1)} %bitcast.21), custom_call_target="tpu_custom_call" | custom-call | flops 4294967296 | bytes 23068672 | tf_op jit(solution)/shard_map/pallas_call | solution.py:74
  148.2 0.0 copy-start.2
  148.2 1.6 copy-done.2
  149.8 17.3 %shard_map.99 = f32[512,256]{1,0:T(8,128)S(1)} custom-call(bf16[4,2,512,256]{3,2,1,0:T(8,128)(2,1)S(1)} %bitcast.19), custom_call_target="tpu_custom_call" | custom-call | flops 1048576 | bytes 6291456 | tf_op jit(solution)/shard_map/pallas_call | solution.py:437
  167.1 0.8 copy.12
Async XLA Ops:
  0.6 82.5 %copy-start = (bf16[256,256]{1,0:T(8,128)(2,1)S(1)}, bf16[256,256]{1,0:T(8,128)(2,1)}, u32[]{:S(2)}) copy-start(bf16[256,256]{1,0:T(8,128)(2,1)} %param.12) | copy-start | bytes 393220
  1.3 1.0 copy-start.5
  22.0 1.3 copy-start.3
  42.5 2.2 %copy-start.1 = (bf16[64,128,256]{2,1,0:T(8,128)(2,1)S(1)}, bf16[64,128,256]{2,1,0:T(8,128)(2,1)}, u32[]{:S(2)}) copy-start(bf16[64,128,256]{2,1,0:T(8,128)(2,1)} %shard_map.95) | copy-start | bytes 12582916
  44.7 38.5 %copy-start.6 = (bf16[512,256]{1,0:T(8,128)(2,1)S(1)}, bf16[512,256]{1,0:T(8,128)(2,1)}, u32[]{:S(2)}) copy-start(bf16[512,256]{1,0:T(8,128)(2,1)} %param.13) | copy-start | bytes 786436
  126.2 1.9 %copy-start.4 = (bf16[4,4,512,256]{3,2,1,0:T(8,128)(2,1)}, bf16[4,4,512,256]{3,2,1,0:T(8,128)(2,1)S(1)}, u32[]{:S(2)}) copy-start(bf16[4,4,512,256]{3,2,1,0:T(8,128)(2,1)S(1)} %get-tuple-element.6) | copy-start | bytes 12582916
  148.2 1.6 copy-start.2

commit v13 on v12

--- a/solution.py
+++ b/solution.py
@@ -469,6 +469,7 @@
     my_z = me // 2
     my_core = lax.rem(me, 2)
     other_core = 1 - my_core
+    partner = row_peer(my_z * 2 + other_core)
     greet_row(my_z, my_core, nz)
     own = pltpu.make_async_copy(x_ref, full.at[my_z, my_core], own_sem.at[0])
     own.start()
@@ -482,7 +483,18 @@
         )
         copy.start()
         sends.append(copy)
+
+    def forward(block_z, slot):
+        copy = pltpu.make_async_remote_copy(
+            src_ref=full.at[block_z, my_core], dst_ref=full.at[block_z, my_core],
+            send_sem=send2.at[slot], recv_sem=got2.at[block_z],
+            device_id=partner, device_id_type=mesh_kind,
+        )
+        copy.start()
+        sends.append(copy)
+
     own.wait()
+    forward(my_z, 0)
     for offset in range(1, nz):
         source_z = lax.rem(my_z + nz - offset, nz)
         pltpu.make_async_remote_copy(
@@ -490,20 +502,16 @@
             send_sem=send1.at[offset], recv_sem=got1.at[source_z],
             device_id=row_peer(source_z * 2 + my_core), device_id_type=mesh_kind,
         ).wait_recv()
-    second = pltpu.make_async_remote_copy(
-        src_ref=full.at[:, my_core], dst_ref=full.at[:, my_core],
-        send_sem=send2.at[0], recv_sem=got2.at[0],
-        device_id=row_peer(my_z * 2 + other_core), device_id_type=mesh_kind,
-    )
-    second.start()
-    pltpu.make_async_remote_copy(
-        src_ref=full.at[:, other_core], dst_ref=full.at[:, other_core],
-        send_sem=send2.at[0], recv_sem=got2.at[0],
-        device_id=row_peer(my_z * 2 + other_core), device_id_type=mesh_kind,
-    ).wait_recv()
+        forward(source_z, offset)
+    for offset in range(nz):
+        block_z = lax.rem(my_z + nz - offset, nz)
+        pltpu.make_async_remote_copy(
+            src_ref=full.at[block_z, other_core], dst_ref=full.at[block_z, other_core],
+            send_sem=send2.at[offset], recv_sem=got2.at[block_z],
+            device_id=partner, device_id_type=mesh_kind,
+        ).wait_recv()
     for copy in sends:
         copy.wait_send()
-    second.wait_send()
     out_ref[...] = full[...]
 
 
@@ -520,8 +528,8 @@
             (
                 pltpu.SemaphoreType.DMA((nz,)),
                 pltpu.SemaphoreType.DMA((nz,)),
-                pltpu.SemaphoreType.DMA((1,)),
-                pltpu.SemaphoreType.DMA((1,)),
+                pltpu.SemaphoreType.DMA((nz,)),
+                pltpu.SemaphoreType.DMA((nz,)),
                 pltpu.SemaphoreType.DMA((1,)),
             ),
         ],

time: 169 us -> 170 us (level)
  no operation moved by 1% of the time
where the time goes in v13:
time: 170 us; the launch traced here: 168 us
  Pallas kernels  155 us (91%)
  local copies, waits for them, and re-layouts  8.77 us (5%)
    pallas_call x1, Pallas kernels, gather_and_sum(): pl.pallas_call(functools.partial(gather_and_sum_kernel, nx, ny, nr), out_...  40.6 us
    pallas_call x1, Pallas kernels, scatter_sum_2d(): pl.pallas_call(functools.partial(scatter_sum_2d_kernel, nx, ny), out_shap...  40.1 us
    pallas_call x2, Pallas kernels, sparse_product(): pl.pallas_call(functools.partial(spmm_kernel, transpose), out_shape=jax.S...  38 us
    pallas_call x1, Pallas kernels, gather_row(): pl.pallas_call(functools.partial(gather_row_kernel, nz), out_shape=jax.Sh...  19.1 us
    pallas_call x1, Pallas kernels, scatter_sum_row(): pl.pallas_call(functools.partial(scatter_sum_row_kernel, nz), out_shape=j...  17.6 us
    unnamed x15, local copies, waits for them, and re-layouts  8.77 us

profile of v13, /device:TPU:0, one launch (start us, length us, event | category | flops | bytes accessed | tf_op | source)
XLA Modules:
  0.0 167.9 jit_solution(17306079188274340252)
XLA Ops:
  0.6 0.0 copy-start
  1.3 0.0 copy-start.5
  1.3 0.9 copy-done.5
  2.3 19.1 %shard_map.94 = bf16[4,2,512,256]{3,2,1,0:T(8,128)(2,1)S(1)} custom-call(bf16[512,256]{1,0:T(8,128)(2,1)S(1)} %copy-done.5), custom_call_target="tpu_custom_call" | custom-call | bytes 6291456 | tf_op jit(solution)/shard_map/pallas_call | solution.py:521
  21.4 0.0 copy-start.3
  21.4 1.3 copy-done.3
  22.7 18.9 %shard_map.95 = bf16[64,128,256]{2,1,0:T(8,128)(2,1)} custom-call(s32[512]{0:T(512)} %bitcast.26, s32[512]{0:T(512)} %bitcast.28, s32[1]{0:T(128)} %bitcast.16.count_ref, bf16[512,128,128]{2,1,0:T(8,128)(2,1)} %bitcast.23, bf16[32,128,256]{2,1,0:T(8,128)(2,1)} %bitcast.20), custom_call_target="tpu_custom_call" | custom-call | flops 4294967296 | bytes 23068672 | tf_op jit(solution)/shard_map/pallas_call | solution.py:74
  41.6 0.0 copy-start.1
  41.6 2.2 %copy-done.1 = bf16[64,128,256]{2,1,0:T(8,128)(2,1)S(1)} copy-done((bf16[64,128,256]{2,1,0:T(8,128)(2,1)S(1)}, bf16[64,128,256]{2,1,0:T(8,128)(2,1)}, u32[]{:S(2)}) %copy-start.1) | copy-done | bytes 4194328
  43.8 0.0 copy-start.6
  43.8 40.1 %shard_map.96 = bf16[512,256]{1,0:T(8,128)(2,1)S(1)} custom-call(bf16[4,4,512,256]{3,2,1,0:T(8,128)(2,1)S(1)} %bitcast.18), custom_call_target="tpu_custom_call" | custom-call | flops 2097152 | bytes 12582912 | tf_op jit(solution)/shard_map/pallas_call | solution.py:337
  83.9 0.0 copy-done
  83.9 0.0 copy-done.6
  83.9 1.1 multiply_convert_fusion
  85.0 0.3 fusion
  85.3 0.3 convolution_convert_fusion.x_ref
  85.5 40.6 %shard_map.97 = (bf16[4,4,512,256]{3,2,1,0:T(8,128)(2,1)S(1)}, f32[16,16,256]{2,1,0:T(8,128)S(1)}) custom-call(bf16[512,256]{1,0:T(8,128)(2,1)S(1)} %convolution_convert_fusion.x_ref, f32[16,16,256]{2,1,0:T(8,128)S(1)} %bitcast.22), custom_call_target="tpu_custom_call" | custom-call | flops 65536 | bytes 13369344 | tf_op jit(solution)/shard_map/pallas_call | solution.py:902
  126.2 0.0 copy-start.4
  126.2 1.9 %copy-done.4 = bf16[4,4,512,256]{3,2,1,0:T(8,128)(2,1)} copy-done((bf16[4,4,512,256]{3,2,1,0:T(8,128)(2,1)}, bf16[4,4,512,256]{3,2,1,0:T(8,128)(2,1)S(1)}, u32[]{:S(2)}) %copy-start.4) | copy-done | bytes 4194328
  128.1 0.7 broadcast_multiply_fusion
  128.8 19.1 %shard_map.98 = bf16[32,128,256]{2,1,0:T(8,128)(2,1)} custom-call(s32[512]{0:T(512)} %bitcast.29, s32[512]{0:T(512)} %bitcast.27, s32[1]{0:T(128)} %bitcast.17.count_ref, bf16[512,128,128]{2,1,0:T(8,128)(2,1)} %bitcast.24, bf16[64,128,256]{2,1,0:T(8,128)(2,1)} %bitcast.21), custom_call_target="tpu_custom_call" | custom-call | flops 4294967296 | bytes 23068672 | tf_op jit(solution)/shard_map/pallas_call | solution.py:74
  148.0 0.0 copy-start.2
  148.0 1.6 copy-done.2
  149.5 17.6 %shard_map.99 = f32[512,256]{1,0:T(8,128)S(1)} custom-call(bf16[4,2,512,256]{3,2,1,0:T(8,128)(2,1)S(1)} %bitcast.19), custom_call_target="tpu_custom_call" | custom-call | flops 1048576 | bytes 6291456 | tf_op jit(solution)/shard_map/pallas_call | solution.py:437
  167.1 0.8 copy.12
Async XLA Ops:
  0.6 83.2 %copy-start = (bf16[256,256]{1,0:T(8,128)(2,1)S(1)}, bf16[256,256]{1,0:T(8,128)(2,1)}, u32[]{:S(2)}) copy-start(bf16[256,256]{1,0:T(8,128)(2,1)} %param.12) | copy-start | bytes 393220
  1.3 1.0 copy-start.5
  21.4 1.3 copy-start.3
  41.6 2.2 %copy-start.1 = (bf16[64,128,256]{2,1,0:T(8,128)(2,1)S(1)}, bf16[64,128,256]{2,1,0:T(8,128)(2,1)}, u32[]{:S(2)}) copy-start(bf16[64,128,256]{2,1,0:T(8,128)(2,1)} %shard_map.95) | copy-start | bytes 12582916
  43.8 40.1 %copy-start.6 = (bf16[512,256]{1,0:T(8,128)(2,1)S(1)}, bf16[512,256]{1,0:T(8,128)(2,1)}, u32[]{:S(2)}) copy-start(bf16[512,256]{1,0:T(8,128)(2,1)} %param.13) | copy-start | bytes 786436
  126.2 1.9 %copy-start.4 = (bf16[4,4,512,256]{3,2,1,0:T(8,128)(2,1)}, bf16[4,4,512,256]{3,2,1,0:T(8,128)(2,1)S(1)}, u32[]{:S(2)}) copy-start(bf16[4,4,512,256]{3,2,1,0:T(8,128)(2,1)S(1)} %get-tuple-element.6) | copy-start | bytes 12582916
  148.0 1.6 copy-start.2

commit v14 on v13

--- a/solution.py
+++ b/solution.py
@@ -8,8 +8,8 @@
 from jax.experimental.pallas import tpu as pltpu
 from jax.sharding import PartitionSpec as P
 
-SLOTS_PER_STEP = 32
-UNROLL = 32
+SLOTS_PER_STEP = 64
+UNROLL = 64
 TORUS_X = 4
 
 

time: 170 us -> 163 us (0.959)
  Pallas kernels: 155 us -> 148 us
    pallas_call x2, Pallas kernels: 38 us -> 32.6 us  [sparse_product(): pl.pallas_call(functools.partial(spmm_kernel, transpose), out_shape=jax.S...]
where the time goes in v14:
time: 163 us; the launch traced here: 161 us
  Pallas kernels  148 us (91%)
  local copies, waits for them, and re-layouts  8.77 us (5%)
    pallas_call x1, Pallas kernels, gather_and_sum(): pl.pallas_call(functools.partial(gather_and_sum_kernel, nx, ny, nr), out_...  40.8 us
    pallas_call x1, Pallas kernels, scatter_sum_2d(): pl.pallas_call(functools.partial(scatter_sum_2d_kernel, nx, ny), out_shap...  39.4 us
    pallas_call x2, Pallas kernels, sparse_product(): pl.pallas_call(functools.partial(spmm_kernel, transpose), out_shape=jax.S...  32.6 us
    pallas_call x1, Pallas kernels, gather_row(): pl.pallas_call(functools.partial(gather_row_kernel, nz), out_shape=jax.Sh...  19.1 us
    pallas_call x1, Pallas kernels, scatter_sum_row(): pl.pallas_call(functools.partial(scatter_sum_row_kernel, nz), out_shape=j...  16.6 us
    unnamed x15, local copies, waits for them, and re-layouts  8.77 us

profile of v14, /device:TPU:0, one launch (start us, length us, event | category | flops | bytes accessed | tf_op | source)
XLA Modules:
  0.0 161.0 jit_solution(2294070486072330522)
XLA Ops:
  0.6 0.0 copy-start
  1.3 0.0 copy-start.5
  1.3 0.9 copy-done.5
  2.3 19.1 %shard_map.94 = bf16[4,2,512,256]{3,2,1,0:T(8,128)(2,1)S(1)} custom-call(bf16[512,256]{1,0:T(8,128)(2,1)S(1)} %copy-done.5), custom_call_target="tpu_custom_call" | custom-call | bytes 6291456 | tf_op jit(solution)/shard_map/pallas_call | solution.py:521
  21.4 0.0 copy-start.3
  21.4 1.3 copy-done.3
  22.7 16.2 %shard_map.95 = bf16[64,128,256]{2,1,0:T(8,128)(2,1)} custom-call(s32[512]{0:T(512)} %bitcast.26, s32[512]{0:T(512)} %bitcast.28, s32[1]{0:T(128)} %bitcast.16.count_ref, bf16[512,128,128]{2,1,0:T(8,128)(2,1)} %bitcast.23, bf16[32,128,256]{2,1,0:T(8,128)(2,1)} %bitcast.20), custom_call_target="tpu_custom_call" | custom-call | flops 4294967296 | bytes 23068672 | tf_op jit(solution)/shard_map/pallas_call | solution.py:74
  38.9 0.0 copy-start.1
  38.9 2.2 %copy-done.1 = bf16[64,128,256]{2,1,0:T(8,128)(2,1)S(1)} copy-done((bf16[64,128,256]{2,1,0:T(8,128)(2,1)S(1)}, bf16[64,128,256]{2,1,0:T(8,128)(2,1)}, u32[]{:S(2)}) %copy-start.1) | copy-done | bytes 4194328
  41.1 0.0 copy-start.6
  41.1 39.4 %shard_map.96 = bf16[512,256]{1,0:T(8,128)(2,1)S(1)} custom-call(bf16[4,4,512,256]{3,2,1,0:T(8,128)(2,1)S(1)} %bitcast.18), custom_call_target="tpu_custom_call" | custom-call | flops 2097152 | bytes 12582912 | tf_op jit(solution)/shard_map/pallas_call | solution.py:337
  80.5 0.0 copy-done
  80.5 0.0 copy-done.6
  80.5 1.1 multiply_convert_fusion
  81.6 0.3 fusion
  81.9 0.3 convolution_convert_fusion.x_ref
  82.2 40.8 %shard_map.97 = (bf16[4,4,512,256]{3,2,1,0:T(8,128)(2,1)S(1)}, f32[16,16,256]{2,1,0:T(8,128)S(1)}) custom-call(bf16[512,256]{1,0:T(8,128)(2,1)S(1)} %convolution_convert_fusion.x_ref, f32[16,16,256]{2,1,0:T(8,128)S(1)} %bitcast.22), custom_call_target="tpu_custom_call" | custom-call | flops 65536 | bytes 13369344 | tf_op jit(solution)/shard_map/pallas_call | solution.py:902
  123.0 0.0 copy-start.4
  123.0 1.9 %copy-done.4 = bf16[4,4,512,256]{3,2,1,0:T(8,128)(2,1)} copy-done((bf16[4,4,512,256]{3,2,1,0:T(8,128)(2,1)}, bf16[4,4,512,256]{3,2,1,0:T(8,128)(2,1)S(1)}, u32[]{:S(2)}) %copy-start.4) | copy-done | bytes 4194328
  124.9 0.7 broadcast_multiply_fusion
  125.6 16.4 %shard_map.98 = bf16[32,128,256]{2,1,0:T(8,128)(2,1)} custom-call(s32[512]{0:T(512)} %bitcast.29, s32[512]{0:T(512)} %bitcast.27, s32[1]{0:T(128)} %bitcast.17.count_ref, bf16[512,128,128]{2,1,0:T(8,128)(2,1)} %bitcast.24, bf16[64,128,256]{2,1,0:T(8,128)(2,1)} %bitcast.21), custom_call_target="tpu_custom_call" | custom-call | flops 4294967296 | bytes 23068672 | tf_op jit(solution)/shard_map/pallas_call | solution.py:74
  142.0 0.0 copy-start.2
  142.1 1.6 copy-done.2
  143.6 16.6 %shard_map.99 = f32[512,256]{1,0:T(8,128)S(1)} custom-call(bf16[4,2,512,256]{3,2,1,0:T(8,128)(2,1)S(1)} %bitcast.19), custom_call_target="tpu_custom_call" | custom-call | flops 1048576 | bytes 6291456 | tf_op jit(solution)/shard_map/pallas_call | solution.py:437
  160.2 0.8 copy.12
Async XLA Ops:
  0.6 79.9 %copy-start = (bf16[256,256]{1,0:T(8,128)(2,1)S(1)}, bf16[256,256]{1,0:T(8,128)(2,1)}, u32[]{:S(2)}) copy-start(bf16[256,256]{1,0:T(8,128)(2,1)} %param.12) | copy-start | bytes 393220
  1.3 1.0 copy-start.5
  21.4 1.3 copy-start.3
  38.9 2.2 %copy-start.1 = (bf16[64,128,256]{2,1,0:T(8,128)(2,1)S(1)}, bf16[64,128,256]{2,1,0:T(8,128)(2,1)}, u32[]{:S(2)}) copy-start(bf16[64,128,256]{2,1,0:T(8,128)(2,1)} %shard_map.95) | copy-start | bytes 12582916
  41.1 39.5 %copy-start.6 = (bf16[512,256]{1,0:T(8,128)(2,1)S(1)}, bf16[512,256]{1,0:T(8,128)(2,1)}, u32[]{:S(2)}) copy-start(bf16[512,256]{1,0:T(8,128)(2,1)} %param.13) | copy-start | bytes 786436
  123.0 1.9 %copy-start.4 = (bf16[4,4,512,256]{3,2,1,0:T(8,128)(2,1)}, bf16[4,4,512,256]{3,2,1,0:T(8,128)(2,1)S(1)}, u32[]{:S(2)}) copy-start(bf16[4,4,512,256]{3,2,1,0:T(8,128)(2,1)S(1)} %get-tuple-element.6) | copy-start | bytes 12582916
  142.0 1.6 copy-start.2

commit v15 on v14

--- a/solution.py
+++ b/solution.py
@@ -8,8 +8,8 @@
 from jax.experimental.pallas import tpu as pltpu
 from jax.sharding import PartitionSpec as P
 
-SLOTS_PER_STEP = 64
-UNROLL = 64
+SLOTS_PER_STEP = 128
+UNROLL = 128
 TORUS_X = 4
 
 

time: 163 us -> 161 us (0.988)
  no operation moved by 1% of the time
where the time goes in v15:
time: 161 us; the launch traced here: 159 us
  Pallas kernels  147 us (91%)
  local copies, waits for them, and re-layouts  8.77 us (5%)
  matrix products  1.63 us (1%)
    pallas_call x1, Pallas kernels, gather_and_sum(): pl.pallas_call(functools.partial(gather_and_sum_kernel, nx, ny, nr), out_...  41.2 us
    pallas_call x1, Pallas kernels, scatter_sum_2d(): pl.pallas_call(functools.partial(scatter_sum_2d_kernel, nx, ny), out_shap...  38.2 us
    pallas_call x2, Pallas kernels, sparse_product(): pl.pallas_call(functools.partial(spmm_kernel, transpose), out_shape=jax.S...  32.2 us
    pallas_call x1, Pallas kernels, gather_row(): pl.pallas_call(functools.partial(gather_row_kernel, nz), out_shape=jax.Sh...  19.1 us
    pallas_call x1, Pallas kernels, scatter_sum_row(): pl.pallas_call(functools.partial(scatter_sum_row_kernel, nz), out_shape=j...  15.9 us
    unnamed x15, local copies, waits for them, and re-layouts  8.77 us

profile of v15, /device:TPU:0, one launch (start us, length us, event | category | flops | bytes accessed | tf_op | source)
XLA Modules:
  0.0 159.1 jit_solution(15114876174889623855)
XLA Ops:
  0.6 0.0 copy-start
  1.3 0.0 copy-start.5
  1.3 0.9 copy-done.5
  2.3 19.1 %shard_map.94 = bf16[4,2,512,256]{3,2,1,0:T(8,128)(2,1)S(1)} custom-call(bf16[512,256]{1,0:T(8,128)(2,1)S(1)} %copy-done.5), custom_call_target="tpu_custom_call" | custom-call | bytes 6291456 | tf_op jit(solution)/shard_map/pallas_call | solution.py:521
  21.4 0.0 copy-start.3
  21.4 1.3 copy-done.3
  22.7 16.1 %shard_map.95 = bf16[64,128,256]{2,1,0:T(8,128)(2,1)} custom-call(s32[512]{0:T(512)} %bitcast.26, s32[512]{0:T(512)} %bitcast.28, s32[1]{0:T(128)} %bitcast.16.count_ref, bf16[512,128,128]{2,1,0:T(8,128)(2,1)} %bitcast.23, bf16[32,128,256]{2,1,0:T(8,128)(2,1)} %bitcast.20), custom_call_target="tpu_custom_call" | custom-call | flops 4294967296 | bytes 23068672 | tf_op jit(solution)/shard_map/pallas_call | solution.py:74
  38.7 0.0 copy-start.1
  38.7 2.2 %copy-done.1 = bf16[64,128,256]{2,1,0:T(8,128)(2,1)S(1)} copy-done((bf16[64,128,256]{2,1,0:T(8,128)(2,1)S(1)}, bf16[64,128,256]{2,1,0:T(8,128)(2,1)}, u32[]{:S(2)}) %copy-start.1) | copy-done | bytes 4194328
  40.9 0.0 copy-start.6
  40.9 38.2 %shard_map.96 = bf16[512,256]{1,0:T(8,128)(2,1)S(1)} custom-call(bf16[4,4,512,256]{3,2,1,0:T(8,128)(2,1)S(1)} %bitcast.18), custom_call_target="tpu_custom_call" | custom-call | flops 2097152 | bytes 12582912 | tf_op jit(solution)/shard_map/pallas_call | solution.py:337
  79.1 0.0 copy-done
  79.1 0.0 copy-done.6
  79.1 1.1 multiply_convert_fusion
  80.2 0.3 fusion
  80.5 0.3 convolution_convert_fusion.x_ref
  80.8 41.2 %shard_map.97 = (bf16[4,4,512,256]{3,2,1,0:T(8,128)(2,1)S(1)}, f32[16,16,256]{2,1,0:T(8,128)S(1)}) custom-call(bf16[512,256]{1,0:T(8,128)(2,1)S(1)} %convolution_convert_fusion.x_ref, f32[16,16,256]{2,1,0:T(8,128)S(1)} %bitcast.22), custom_call_target="tpu_custom_call" | custom-call | flops 65536 | bytes 13369344 | tf_op jit(solution)/shard_map/pallas_call | solution.py:902
  122.0 0.0 copy-start.4
  122.0 1.9 %copy-done.4 = bf16[4,4,512,256]{3,2,1,0:T(8,128)(2,1)} copy-done((bf16[4,4,512,256]{3,2,1,0:T(8,128)(2,1)}, bf16[4,4,512,256]{3,2,1,0:T(8,128)(2,1)S(1)}, u32[]{:S(2)}) %copy-start.4) | copy-done | bytes 4194328
  123.9 0.7 broadcast_multiply_fusion
  124.6 16.2 %shard_map.98 = bf16[32,128,256]{2,1,0:T(8,128)(2,1)} custom-call(s32[512]{0:T(512)} %bitcast.29, s32[512]{0:T(512)} %bitcast.27, s32[1]{0:T(128)} %bitcast.17.count_ref, bf16[512,128,128]{2,1,0:T(8,128)(2,1)} %bitcast.24, bf16[64,128,256]{2,1,0:T(8,128)(2,1)} %bitcast.21), custom_call_target="tpu_custom_call" | custom-call | flops 4294967296 | bytes 23068672 | tf_op jit(solution)/shard_map/pallas_call | solution.py:74
  140.8 0.0 copy-start.2
  140.8 1.6 copy-done.2
  142.4 15.9 %shard_map.99 = f32[512,256]{1,0:T(8,128)S(1)} custom-call(bf16[4,2,512,256]{3,2,1,0:T(8,128)(2,1)S(1)} %bitcast.19), custom_call_target="tpu_custom_call" | custom-call | flops 1048576 | bytes 6291456 | tf_op jit(solution)/shard_map/pallas_call | solution.py:437
  158.3 0.8 copy.12
Async XLA Ops:
  0.6 78.5 %copy-start = (bf16[256,256]{1,0:T(8,128)(2,1)S(1)}, bf16[256,256]{1,0:T(8,128)(2,1)}, u32[]{:S(2)}) copy-start(bf16[256,256]{1,0:T(8,128)(2,1)} %param.12) | copy-start | bytes 393220
  1.3 1.0 copy-start.5
  21.4 1.3 copy-start.3
  38.7 2.2 %copy-start.1 = (bf16[64,128,256]{2,1,0:T(8,128)(2,1)S(1)}, bf16[64,128,256]{2,1,0:T(8,128)(2,1)}, u32[]{:S(2)}) copy-start(bf16[64,128,256]{2,1,0:T(8,128)(2,1)} %shard_map.95) | copy-start | bytes 12582916
  40.9 38.2 %copy-start.6 = (bf16[512,256]{1,0:T(8,128)(2,1)S(1)}, bf16[512,256]{1,0:T(8,128)(2,1)}, u32[]{:S(2)}) copy-start(bf16[512,256]{1,0:T(8,128)(2,1)} %param.13) | copy-start | bytes 786436
  122.0 1.9 %copy-start.4 = (bf16[4,4,512,256]{3,2,1,0:T(8,128)(2,1)}, bf16[4,4,512,256]{3,2,1,0:T(8,128)(2,1)S(1)}, u32[]{:S(2)}) copy-start(bf16[4,4,512,256]{3,2,1,0:T(8,128)(2,1)S(1)} %get-tuple-element.6) | copy-start | bytes 12582916
  140.8 1.6 copy-start.2
